TPU v7x, 256 devices: a whole 4x4x8 slice. The times are simulated.
256 devices in a mesh: section: 16 (over x, z_lo), replica: 16 (over y, z_hi, core).
Axes of the slice: x: 4, y: 4, z: 8 (z_hi: 2, z_lo: 4; z = z_hi * 4 + z_lo), core: 2. Of those that a mesh axis runs over, the one named last changes fastest.
Arguments:
- wa_local: bfloat16 [16, 16, 576, 1536], P('section', 'replica'), may hold values from -0.25 to 0.25
- wb_local: bfloat16 [16, 16, 1536, 576], P('section', 'replica'), may hold values from -0.15625 to 0.15625
- wa_master: float32 [16, 576, 1536], P('section', 'replica'), may hold values from -0.25 to 0.25
- wb_master: float32 [16, 1536, 576], P('section', None, 'replica'), may hold values from -0.15625 to 0.15625
- wa_moment: float32 [16, 576, 1536], P('section', 'replica'), may hold values from -0.075 to 0.075
- wb_moment: float32 [16, 1536, 576], P('section', None, 'replica'), may hold values from -0.045927934 to 0.045927934
- counts: int32 [16], P('section'), may hold values from 1 to 6
- inputs: bfloat16 [4096, 576], P('replica'), may hold values from -6 to 6
Outputs:
- wa_next: float32 [16, 576, 1536], P('section', 'replica')
- wb_next: float32 [16, 1536, 576], P('section', None, 'replica')
- boundary: bfloat16 [16, 4096, 576], P('section', 'replica')
Inputs may be any that keep to these rules, and one draw needn't show every extreme that they name: `counts`: each section applies its layer at least once and at most 6 times.
All inputs are finite; a program needn't handle non-finite values.
Results may differ from a plain program's by a relative error of at most 0.03.
Values may be sent and summed in bfloat16 or wider, within the bound.
No kernel may reach another device: no remote copies, remote signals or barrier semaphores. Data moves between devices by JAX's collectives and lax.ppermute only.
A program may use at most 64 MiB of HBM per device.

v0:
```python
import functools

import jax
import jax.numpy as jnp
from jax import lax
from jax.experimental import pallas as pl
from jax.experimental.pallas import tpu as pltpu
from jax.sharding import PartitionSpec as P

AXES = ("section", "replica")
F32, BF16 = jnp.float32, jnp.bfloat16
BOTH = (0, 1)
ORDER = (0, -1, 1, 2)
PLACE = (0, 2, 3, 1)
QUARTERS = (2, 1, 3, 0)


def device(x, y, z, core):
    x, y, z = x % 4, y % 4, z % 8
    return (x * 4 + z % 4) * 16 + y * 4 + (z // 4) * 2 + core


def route(move, cores=BOTH, planes=range(4)):
    return [
        (device(x, y, z, core), device(*move(x, y, z, core)))
        for x in planes
        for y in range(4)
        for z in range(8)
        for core in cores
    ]


def y_step(by, cores=BOTH):
    return route(lambda x, y, z, core: (x, y + by, z, core), cores)


def z_step(by, cores=BOTH):
    return route(lambda x, y, z, core: (x, y, z + by, core), cores)


def core_swap(cores=BOTH):
    return route(lambda x, y, z, core: (x, y, z, 1 - core), cores)


def send(block, pairs):
    return lax.ppermute(block, AXES, pairs)


def pair_kernel(info, a_own, b_own, a_got, b_got, *refs):
    outs, own_v, got_v, own_sem, got_sem = refs[:4], *refs[4:]
    y, core = info[2], info[3]
    quarter = own_v.shape[1]

    def fetch(own, got):
        for at, by in enumerate(QUARTERS):
            rows = pl.ds(pl.multiple_of(lax.rem(y + by, 4) * quarter, 16), quarter)
            pltpu.make_async_copy(own.at[rows], own_v.at[at], own_sem.at[at]).start()
            pltpu.make_async_copy(got.at[rows], got_v.at[at], got_sem.at[at]).start()

    @pl.when(core == 0)
    def _():
        fetch(a_own, a_got)

    @pl.when(core == 1)
    def _():
        fetch(b_own, b_got)

    for at in range(4):
        pltpu.make_async_copy(own_v.at[at], own_v.at[at], own_sem.at[at]).wait()
        pltpu.make_async_copy(got_v.at[at], got_v.at[at], got_sem.at[at]).wait()
        outs[at][...] = (own_v[at].astype(F32) + got_v[at].astype(F32)).astype(BF16)


def pair_sum(info, *blocks):
    height, hidden = blocks[0].shape
    quarter = height // 4
    vmem, hbm = pl.BlockSpec(memory_space=pltpu.VMEM), pl.BlockSpec(memory_space=pltpu.HBM)
    return pl.pallas_call(
        pair_kernel,
        name="pair_sum",
        out_shape=(jax.ShapeDtypeStruct((quarter, hidden), BF16),) * 4,
        in_specs=[pl.BlockSpec(memory_space=pltpu.SMEM)] + [hbm] * 4,
        out_specs=(vmem,) * 4,
        scratch_shapes=[
            pltpu.VMEM((4, quarter, hidden), BF16),
            pltpu.VMEM((4, quarter, hidden), BF16),
            pltpu.SemaphoreType.DMA((4,)),
            pltpu.SemaphoreType.DMA((4,)),
        ],
        compiler_params=pltpu.CompilerParams(vmem_limit_bytes=48 << 20),
    )(info, *[pltpu.with_memory_space_constraint(block, pltpu.HBM) for block in blocks])


def relay_kernel(step, has_held, info, rows_ref, *refs):
    held, refs = (refs[:4], refs[4:]) if has_held else ((), refs)
    own, crossed, outs = refs[:8], refs[8:16], refs[16:20]
    last_ref, wa_v, wb_v, stream, done_v, sem_a, sem_b = refs[20:]
    x, z_low, y, core = info[0], info[1], info[2], info[3]
    hidden = wa_v.shape[2]
    half = hidden // 2
    quarter = own[0].shape[1]

    def load(section):
        place = info[8 + lax.rem(section - z_low + 4, 4)]

        def copy(src, dst_v, side, sem):
            row = lax.rem(y + ORDER[side] + 4, 4) * quarter
            pltpu.make_async_copy(
                src,
                dst_v.at[section, pl.ds(pl.multiple_of(row, 16), quarter)],
                sem.at[section],
            ).start()

        def fetch(a_bufs, b_bufs):
            for message in range(4):

                @pl.when(place == message)
                def _(message=message):
                    for side in range(4):
                        copy(a_bufs[2 * message + side // 2].at[side % 2], wa_v, side, sem_a)

            for part in range(2):

                @pl.when(place // 2 == part)
                def _(part=part):
                    for side in range(4):
                        copy(b_bufs[2 * side + part].at[lax.rem(place, 2)], wb_v, side, sem_b)

        @pl.when(core == 0)
        def _():
            fetch(own, crossed)

        @pl.when(core == 1)
        def _():
            fetch(crossed, own)

    @pl.when(x == step)
    def _():
        load(0)
        stream[...] = rows_ref[...].astype(F32)

        def run(section, carry):
            @pl.when(section < 3)
            def _():
                load(section + 1)

            pltpu.make_async_copy(wa_v.at[section], wa_v.at[section], sem_a.at[section]).wait()
            pltpu.make_async_copy(wb_v.at[section], wb_v.at[section], sem_b.at[section]).wait()

            def layer(step, carry):
                value = stream[...]
                scale = lax.rsqrt(jnp.mean(value * value, axis=-1, keepdims=True) + 1e-5)
                narrow = value.astype(BF16)
                total = None
                for at in range(2):
                    columns = pl.ds(at * half, half)
                    gate = jnp.dot(narrow, wa_v[section, :, columns], preferred_element_type=F32)
                    gate = gate * (0.5 * scale)
                    act = (gate + gate * jnp.tanh(gate)).astype(BF16)
                    part = lax.dot_general(
                        act,
                        wb_v[section, :, columns],
                        (((1,), (1,)), ((), ())),
                        preferred_element_type=F32,
                    )
                    total = part if total is None else total + part
                stream[...] = value + total
                return carry

            lax.fori_loop(0, info[4 + lax.rem(z_low - section + 4, 4)], layer, 0)
            done = stream[...].astype(BF16)
            done_v[section] = done
            stream[...] = done.astype(F32)
            return carry

        lax.fori_loop(0, 4, run, 0)
        last_ref[...] = done_v[3]
        for by in range(4):
            outs[by][...] = done_v[lax.rem(z_low + by, 4)]

    if has_held:

        @pl.when(x != step)
        def _():
            for by in range(4):
                outs[by][...] = held[by][...]


def relay(step, info, rows, held, own, crossed):
    vmem, hbm = pl.BlockSpec(memory_space=pltpu.VMEM), pl.BlockSpec(memory_space=pltpu.HBM)
    count, width = rows.shape
    height, hidden = 4 * own[0].shape[1], own[0].shape[2]
    return pl.pallas_call(
        functools.partial(relay_kernel, step, len(held) > 0),
        name="relay",
        out_shape=(jax.ShapeDtypeStruct((count, width), BF16),) * 5,
        in_specs=[pl.BlockSpec(memory_space=pltpu.SMEM), vmem]
        + [vmem] * len(held)
        + [hbm] * (len(own) + len(crossed)),
        out_specs=(vmem,) * 5,
        scratch_shapes=[
            pltpu.VMEM((4, height, hidden), BF16),
            pltpu.VMEM((4, height, hidden), BF16),
            pltpu.VMEM((count, width), F32),
            pltpu.VMEM((4, count, width), BF16),
            pltpu.SemaphoreType.DMA((4,)),
            pltpu.SemaphoreType.DMA((4,)),
        ],
        compiler_params=pltpu.CompilerParams(vmem_limit_bytes=48 << 20),
    )(info, rows, *held, *own, *crossed)


def line_kernel(info, *refs):
    pieces, out_ref, rows_v = refs[:4], *refs[4:]
    count = pieces[0].shape[0]
    for by, piece in enumerate(pieces):
        start = lax.rem(info[1] - by + 4, 4) * count
        rows_v[pl.ds(pl.multiple_of(start, 16), count), :] = piece[...].astype(F32)
    out_ref[...] = rows_v[...].T.astype(BF16)


def line_up(info, pieces):
    count, width = pieces[0].shape
    vmem = pl.BlockSpec(memory_space=pltpu.VMEM)
    return pl.pallas_call(
        line_kernel,
        name="line_up",
        out_shape=jax.ShapeDtypeStruct((width, 4 * count), BF16),
        in_specs=[pl.BlockSpec(memory_space=pltpu.SMEM)] + [vmem] * 4,
        out_specs=vmem,
        scratch_shapes=[pltpu.VMEM((4 * count, width), F32)],
        compiler_params=pltpu.CompilerParams(vmem_limit_bytes=16 << 20),
    )(info, *pieces)


def body(wa_local, wb_local, wa_master, wb_master, wa_moment, wb_moment, counts, inputs):
    section, replica = lax.axis_index("section"), lax.axis_index("replica")
    x, z_low = section // 4, section % 4
    y, z_high, core = replica // 4, (replica // 2) % 2, replica % 2
    first, low = core == 0, z_high == 0
    replicas = lax.axis_size("replica")
    owned, hidden = wa_master.shape[1], wa_master.shape[2]
    chunk = 2 * owned
    place = jnp.stack([x, z_low, y, core])

    a_own, b_own = wa_local[0, 0], wb_local[0, 0].T
    a_got = send(a_own, core_swap((1,)))
    b_got = send(b_own, core_swap((0,)))
    layers = [counts] + [
        send(counts, route(lambda x, y, z, core, by=by: (x, y, z // 4 * 4 + (z + by) % 4, core)))
        for by in (1, 2, 3)
    ]
    across, ahead, behind, mine = pair_sum(place, a_own, b_own, a_got, b_got)
    gots = send(across, y_step(2)), send(ahead, y_step(1)), send(behind, y_step(-1))
    info = jnp.concatenate([place, *layers, jnp.array(PLACE, jnp.int32)])
    gots, info, wa_master, wb_master, wa_moment, wb_moment = lax.optimization_barrier(
        (gots, info, wa_master, wb_master, wa_moment, wb_moment)
    )
    total = mine.astype(F32) + sum(got.astype(F32) for got in gots)
    top, bottom = total[:chunk], total[chunk:]
    z_got = send(jnp.where(low, bottom, top).astype(BF16), z_step(4))

    gain = 0.7 * 1.9
    a_state = (1.0 - gain) * wa_master[0] - (0.7 * 0.81) * wa_moment[0]
    b_state = ((1.0 - gain) * wb_master[0] - (0.7 * 0.81) * wb_moment[0]).T
    kept = jnp.where(first, a_state, b_state)
    state_got = send(jnp.where(first, b_state, a_state), core_swap())
    state = jnp.concatenate([jnp.where(first, kept, state_got), jnp.where(first, state_got, kept)])
    updated = state + (gain / replicas) * (jnp.where(low, top, bottom) + z_got.astype(F32))
    w = updated.astype(BF16)
    ours = jnp.where(first, updated[:owned], updated[owned:])
    theirs = send(jnp.where(first, updated[owned:], updated[:owned]), core_swap())

    def turn(by):
        return y_step(by, (0,)) + z_step(by, (1,))

    def cross(by):
        return z_step(by, (0,)) + y_step(by, (1,))

    w_far, theirs = lax.optimization_barrier((send(w, z_step(4)), theirs))
    wa_next = jnp.where(first, ours, theirs)[None]
    wb_next = jnp.where(first, theirs, ours).T[None]
    k_low, k_high = jnp.where(low, w, w_far), jnp.where(low, w_far, w)
    k0 = jnp.stack([k_low, k_high])
    k_behind, k_ahead = send(k0, turn(1)), send(k0, turn(-1))
    k_across = jnp.stack([send(k_low, turn(2)), send(k_high, turn(-2))])
    shape = (2, 2 * chunk, hidden)
    near = jnp.stack([k0, k_behind]).reshape(shape)
    far = jnp.stack([k_ahead, k_across]).reshape(shape)
    near_behind, near_ahead = send(near, cross(1)), send(near, cross(-1))
    far_behind, far_ahead = send(far, cross(1)), send(far, cross(-1))
    near_behind, wa_next, wb_next = lax.optimization_barrier((near_behind, wa_next, wb_next))
    near_across, far_across = send(near_behind, cross(1)), send(far_ahead, cross(-1))
    own = [near, far, near_behind, far_behind, near_ahead, far_ahead, near_across, far_across]
    crossed = [send(block, core_swap()) for block in own]

    rows_each = inputs.shape[0] // 4
    rows = lax.dynamic_slice_in_dim(inputs, z_low * rows_each, rows_each, 0)
    held = ()
    for step in range(4):
        *held, last = relay(step, info, rows, held, own, crossed)
        if step < 3:
            rows = send(last, route(lambda x, y, z, core: (x + 1, y, z, core), planes=(step,)))

    pieces = [held[0]] + [
        send(held[by], route(lambda x, y, z, core, by=by: (x, y, z // 4 * 4 + (z + by) % 4, core)))
        for by in (1, 2, 3)
    ]
    boundary = line_up(info, pieces).T
    return wa_next, wb_next, boundary[None]


def solution(mesh):
    return jax.shard_map(
        body,
        mesh=mesh,
        in_specs=(
            P("section", "replica", None, None),
            P("section", "replica", None, None),
            P("section", "replica", None),
            P("section", None, "replica"),
            P("section", "replica", None),
            P("section", None, "replica"),
            P("section"),
            P("replica", None),
        ),
        out_specs=(
            P("section", "replica", None),
            P("section", None, "replica"),
            P("section", "replica", None),
        ),
        check_vma=False,
    )
```

profile of v0, /device:TPU:6, one launch (start us, length us, event | category | flops | bytes accessed | tf_op | source)
XLA Modules:
  0.0 227.3 jit_solution(3352580821531626317)
XLA Ops:
  2.1 4.4 %collective-permute-start.1 = (bf16[576,1536]{1,0:T(8,128)(2,1)}, bf16[576,1536]{1,0:T(8,128)(2,1)}, u32[]{:S(2)}, u32[]{:S(2)}) collective-permute-start(bf16[576,1536]{1,0:T(8,128)(2,1)} %bitcast.43), channel_id=1, source_target_pairs={{0,1},{16,17},{32,33},{48,49},{2,3},{18,19},{34,35},{50,51},{4,5},... | collective-permute-start | bytes 5308424 | tf_op jit(solution)/shard_map/ppermute | solution.py:46
  8.9 2.7 %pair_sum.1 = (bf16[144,1536]{1,0:T(8,128)(2,1)S(1)}, bf16[144,1536]{1,0:T(8,128)(2,1)S(1)}, bf16[144,1536]{1,0:T(8,128)(2,1)S(1)}, bf16[144,1536]{1,0:T(8,128)(2,1)S(1)}) custom-call(s32[4]{0:T(128)S(1)} %pad_add_fusion.info, bf16[576,1536]{1,0:T(8,128)(2,1)} %bitcast.42, bf16[576,1536]{1,0:T(8,128)(2,1)} %bitcast.44, bf16[576,1536]{1,0:T(8,128)(2,1)} %copy-done.4, ...), custom_call_target="tpu_custom_call" | custom-call | tf_op jit(solution)/shard_map/pair_sum/pallas_call | solution.py:78
  11.5 3.3 %collective-permute-start.2 = (bf16[144,1536]{1,0:T(8,128)(2,1)S(1)}, bf16[144,1536]{1,0:T(8,128)(2,1)}, u32[]{:S(2)}, u32[]{:S(2)}) collective-permute-start(bf16[144,1536]{1,0:T(8,128)(2,1)S(1)} %get-tuple-element.39), channel_id=1, source_target_pairs={{0,8},{1,9},{16,24},{17,25},{32,40},{33,41},{48,56},{49,57},{2,10}... | collective-permute-start | bytes 1327112 | tf_op jit(solution)/shard_map/ppermute | solution.py:46
  15.5 2.6 %collective-permute-start.4 = (bf16[144,1536]{1,0:T(8,128)(2,1)S(1)}, bf16[144,1536]{1,0:T(8,128)(2,1)}, u32[]{:S(2)}, u32[]{:S(2)}) collective-permute-start(bf16[144,1536]{1,0:T(8,128)(2,1)S(1)} %get-tuple-element.41), channel_id=1, source_target_pairs={{0,12},{1,13},{16,28},{17,29},{32,44},{33,45},{48,60},{49,61},{2,1... | collective-permute-start | bytes 1327112 | tf_op jit(solution)/shard_map/ppermute | solution.py:46
  18.1 3.3 %collective-permute-start.6 = (s32[1]{0:T(128)}, s32[1]{0:T(128)}, u32[]{:S(2)}, u32[]{:S(2)}) collective-permute-start(s32[1]{0:T(128)} %param.15), channel_id=1, source_target_pairs={{0,32},{1,33},{16,48},{17,49},{32,0},{33,1},{48,16},{49,17},{2,34}... | collective-permute-start | bytes 20 | tf_op jit(solution)/shard_map/ppermute | solution.py:46
  24.0 3.3 %collective-permute-start.7 = (s32[1]{0:T(128)}, s32[1]{0:T(128)}, u32[]{:S(2)}, u32[]{:S(2)}) collective-permute-start(s32[1]{0:T(128)} %param.15), channel_id=1, source_target_pairs={{0,48},{1,49},{16,0},{17,1},{32,16},{33,17},{48,32},{49,33},{2,50}... | collective-permute-start | bytes 20 | tf_op jit(solution)/shard_map/ppermute | solution.py:46
  30.7 4.6 %collective-permute-done.3 = bf16[144,1536]{1,0:T(8,128)(2,1)} collective-permute-done((bf16[144,1536]{1,0:T(8,128)(2,1)S(1)}, bf16[144,1536]{1,0:T(8,128)(2,1)}, u32[]{:S(2)}, u32[]{:S(2)}) %collective-permute-start.3) | collective-permute-done | bytes 442400 | tf_op jit(solution)/shard_map/ppermute | solution.py:46
  37.4 7.3 %collective-permute-start.9 = (bf16[72,1536]{1,0:T(8,128)(2,1)S(1)}, bf16[72,1536]{1,0:T(8,128)(2,1)S(1)}, u32[]{:S(2)}, u32[]{:S(2)}) collective-permute-start(bf16[72,1536]{1,0:T(8,128)(2,1)S(1)} %select_convert_fusion), channel_id=1, source_target_pairs={{0,2},{1,3},{16,18},{17,19},{32,34},{33,35},{48,50},{49,51},{2,0},... | collective-permute-start | bytes 663560 | tf_op jit(solution)/shard_map/ppermute | solution.py:46
  44.8 7.1 %collective-permute-done.9 = bf16[72,1536]{1,0:T(8,128)(2,1)S(1)} collective-permute-done((bf16[72,1536]{1,0:T(8,128)(2,1)S(1)}, bf16[72,1536]{1,0:T(8,128)(2,1)S(1)}, u32[]{:S(2)}, u32[]{:S(2)}) %collective-permute-start.9) | collective-permute-done | bytes 221216 | tf_op jit(solution)/shard_map/ppermute | solution.py:46
  52.1 8.6 %collective-permute-start.10 = (bf16[72,1536]{1,0:T(8,128)(2,1)S(1)}, bf16[72,1536]{1,0:T(8,128)(2,1)S(1)}, u32[]{:S(2)}, u32[]{:S(2)}) collective-permute-start(bf16[72,1536]{1,0:T(8,128)(2,1)S(1)} %get-tuple-element.78), channel_id=1, source_target_pairs={{0,2},{1,3},{16,18},{17,19},{32,34},{33,35},{48,50},{49,51},{2,0},... | collective-permute-start | bytes 663560 | tf_op jit(solution)/shard_map/ppermute | solution.py:46
  60.8 7.8 %collective-permute-done.10 = bf16[72,1536]{1,0:T(8,128)(2,1)S(1)} collective-permute-done((bf16[72,1536]{1,0:T(8,128)(2,1)S(1)}, bf16[72,1536]{1,0:T(8,128)(2,1)S(1)}, u32[]{:S(2)}, u32[]{:S(2)}) %collective-permute-start.10) | collective-permute-done | bytes 221216 | tf_op jit(solution)/shard_map/ppermute | solution.py:46
  68.6 2.1 collective-permute-start.15
  76.1 2.5 %collective-permute-done.16 = bf16[72,1536]{1,0:T(8,128)(2,1)S(1)} collective-permute-done((bf16[72,1536]{1,0:T(8,128)(2,1)S(1)}, bf16[72,1536]{1,0:T(8,128)(2,1)S(1)}, u32[]{:S(2)}, u32[]{:S(2)}) %collective-permute-start.16) | collective-permute-done | bytes 221216 | tf_op jit(solution)/shard_map/ppermute | solution.py:46
  78.7 4.6 %collective-permute-done.12 = bf16[2,72,1536]{2,1,0:T(8,128)(2,1)S(1)} collective-permute-done((bf16[2,72,1536]{2,1,0:T(8,128)(2,1)S(1)}, bf16[2,72,1536]{2,1,0:T(8,128)(2,1)S(1)}, u32[]{:S(2)}, u32[]{:S(2)}) %collective-permute-start.12) | collective-permute-done | bytes 442400 | tf_op jit(solution)/shard_map/ppermute | solution.py:46
  83.4 6.0 %collective-permute-start.18 = (bf16[2,144,1536]{2,1,0:T(8,128)(2,1)S(1)}, bf16[2,144,1536]{2,1,0:T(8,128)(2,1)S(1)}, u32[]{:S(2)}, u32[]{:S(2)}) collective-permute-start(bf16[2,144,1536]{2,1,0:T(8,128)(2,1)S(1)} %pad_maximum_fusion.refs_0_.refs_4_), channel_id=1, source_target_pairs={{0,50},{16,0},{32,16},{48,32},{2,48},{18,2},{34,18},{50,34},{4,54}... | collective-permute-start | bytes 2654216 | tf_op jit(solution)/shard_map/ppermute | solution.py:46
  89.5 3.3 %collective-permute-start.19 = (bf16[2,144,1536]{2,1,0:T(8,128)(2,1)S(1)}, bf16[2,144,1536]{2,1,0:T(8,128)(2,1)}, u32[]{:S(2)}, u32[]{:S(2)}) collective-permute-start(bf16[2,144,1536]{2,1,0:T(8,128)(2,1)S(1)} %pad_maximum_fusion.1.refs_1_.refs_5_), channel_id=1, source_target_pairs={{0,50},{16,0},{32,16},{48,32},{2,48},{18,2},{34,18},{50,34},{4,54}... | collective-permute-start | bytes 2654216 | tf_op jit(solution)/shard_map/ppermute | solution.py:46
  92.9 10.8 %collective-permute-done.13.refs_2_.refs_6_ = bf16[2,144,1536]{2,1,0:T(8,128)(2,1)} collective-permute-done((bf16[2,144,1536]{2,1,0:T(8,128)(2,1)S(1)}, bf16[2,144,1536]{2,1,0:T(8,128)(2,1)}, u32[]{:S(2)}, u32[]{:S(2)}) %collective-permute-start.13) | collective-permute-done | bytes 884768 | tf_op jit(solution)/shard_map/ppermute | solution.py:46
  103.9 5.6 %collective-permute-done.19.refs_5_.refs_9_ = bf16[2,144,1536]{2,1,0:T(8,128)(2,1)} collective-permute-done((bf16[2,144,1536]{2,1,0:T(8,128)(2,1)S(1)}, bf16[2,144,1536]{2,1,0:T(8,128)(2,1)}, u32[]{:S(2)}, u32[]{:S(2)}) %collective-permute-start.19) | collective-permute-done | bytes 884768 | tf_op jit(solution)/shard_map/ppermute | solution.py:46
  109.4 3.8 %collective-permute-start.21 = (bf16[2,144,1536]{2,1,0:T(8,128)(2,1)}, bf16[2,144,1536]{2,1,0:T(8,128)(2,1)}, u32[]{:S(2)}, u32[]{:S(2)}) collective-permute-start(bf16[2,144,1536]{2,1,0:T(8,128)(2,1)} %collective-permute-done.19.refs_5_.refs_9_), channel_id=1, source_target_pairs={{0,50},{16,0},{32,16},{48,32},{2,48},{18,2},{34,18},{50,34},{4,54}... | collective-permute-start | bytes 2654216 | tf_op jit(solution)/shard_map/ppermute | solution.py:46
  113.2 4.9 %collective-permute-done.17.refs_3_.refs_7_ = bf16[2,144,1536]{2,1,0:T(8,128)(2,1)} collective-permute-done((bf16[2,144,1536]{2,1,0:T(8,128)(2,1)S(1)}, bf16[2,144,1536]{2,1,0:T(8,128)(2,1)}, u32[]{:S(2)}, u32[]{:S(2)}) %collective-permute-start.17) | collective-permute-done | bytes 884768 | tf_op jit(solution)/shard_map/ppermute | solution.py:46
  118.7 8.9 %collective-permute-done.20.refs_6_.refs_10_ = bf16[2,144,1536]{2,1,0:T(8,128)(2,1)} collective-permute-done((bf16[2,144,1536]{2,1,0:T(8,128)(2,1)}, bf16[2,144,1536]{2,1,0:T(8,128)(2,1)}, u32[]{:S(2)}, u32[]{:S(2)}) %collective-permute-start.20) | collective-permute-done | bytes 884768 | tf_op jit(solution)/shard_map/ppermute | solution.py:46
  136.5 65.4 %collective-permute-done.32.rows_ref = bf16[64,576]{1,0:T(8,128)(2,1)S(1)} collective-permute-done((bf16[64,576]{1,0:T(8,128)(2,1)S(1)}, bf16[64,576]{1,0:T(8,128)(2,1)S(1)}, u32[]{:S(2)}, u32[]{:S(2)}) %collective-permute-start.32) | collective-permute-done | bytes 73760 | tf_op jit(solution)/shard_map/ppermute | solution.py:46
  201.9 16.6 %relay.7 = (bf16[64,576]{1,0:T(8,128)(2,1)S(1)}, bf16[64,576]{1,0:T(8,128)(2,1)S(1)}, bf16[64,576]{1,0:T(8,128)(2,1)S(1)}, bf16[64,576]{1,0:T(8,128)(2,1)S(1)}, bf16[64,576]{1,0:T(8,128)(2,1)}) custom-call(s32[12]{0:T(128)S(1)} %concatenate.9.info, bf16[64,576]{1,0:T(8,128)(2,1)S(1)} %collective-permute-done.32.rows_ref, ...), custom_call_target="tpu_custom_call" | custom-call | tf_op jit(solution)/shard_map/relay/pallas_call | solution.py:193
  218.7 3.7 %collective-permute-start.35 = (bf16[64,576]{1,0:T(8,128)(2,1)S(1)}, bf16[64,576]{1,0:T(8,128)(2,1)S(1)}, u32[]{:S(2)}, u32[]{:S(2)}) collective-permute-start(bf16[64,576]{1,0:T(8,128)(2,1)S(1)} %get-tuple-element.74), channel_id=1, source_target_pairs={{0,48},{1,49},{16,0},{17,1},{32,16},{33,17},{48,32},{49,33},{2,50}... | collective-permute-start | bytes 221192 | tf_op jit(solution)/shard_map/ppermute | solution.py:46
  (92 shorter events, 32.7 us)
Async XLA Ops:
  11.5 19.1 %collective-permute-start.2 = (bf16[144,1536]{1,0:T(8,128)(2,1)S(1)}, bf16[144,1536]{1,0:T(8,128)(2,1)}, u32[]{:S(2)}, u32[]{:S(2)}) collective-permute-start(bf16[144,1536]{1,0:T(8,128)(2,1)S(1)} %get-tuple-element.39), channel_id=1, source_target_pairs={{0,8},{1,9},{16,24},{17,25},{32,40},{33,41},{48,56},{49,57},{2,10}... | collective-permute-start | bytes 1327112 | tf_op jit(solution)/shard_map/ppermute | solution.py:46
  14.8 20.4 %collective-permute-start.3 = (bf16[144,1536]{1,0:T(8,128)(2,1)S(1)}, bf16[144,1536]{1,0:T(8,128)(2,1)}, u32[]{:S(2)}, u32[]{:S(2)}) collective-permute-start(bf16[144,1536]{1,0:T(8,128)(2,1)S(1)} %get-tuple-element.40), channel_id=1, source_target_pairs={{0,4},{1,5},{16,20},{17,21},{32,36},{33,37},{48,52},{49,53},{2,6},... | collective-permute-start | bytes 1327112 | tf_op jit(solution)/shard_map/ppermute | solution.py:46
  15.5 20.1 %collective-permute-start.4 = (bf16[144,1536]{1,0:T(8,128)(2,1)S(1)}, bf16[144,1536]{1,0:T(8,128)(2,1)}, u32[]{:S(2)}, u32[]{:S(2)}) collective-permute-start(bf16[144,1536]{1,0:T(8,128)(2,1)S(1)} %get-tuple-element.41), channel_id=1, source_target_pairs={{0,12},{1,13},{16,28},{17,29},{32,44},{33,45},{48,60},{49,61},{2,1... | collective-permute-start | bytes 1327112 | tf_op jit(solution)/shard_map/ppermute | solution.py:46
  35.8 8.9 %collective-permute-start.8 = (f32[36,1536]{1,0:T(8,128)S(1)}, f32[36,1536]{1,0:T(8,128)S(1)}, u32[]{:S(2)}, u32[]{:S(2)}) collective-permute-start(f32[36,1536]{1,0:T(8,128)S(1)} %bitcast_select_fusion), channel_id=1, source_target_pairs={{0,1},{1,0},{16,17},{17,16},{32,33},{33,32},{48,49},{49,48},{2,3},... | collective-permute-start | bytes 663560 | tf_op jit(solution)/shard_map/ppermute | solution.py:46
  37.4 14.5 %collective-permute-start.9 = (bf16[72,1536]{1,0:T(8,128)(2,1)S(1)}, bf16[72,1536]{1,0:T(8,128)(2,1)S(1)}, u32[]{:S(2)}, u32[]{:S(2)}) collective-permute-start(bf16[72,1536]{1,0:T(8,128)(2,1)S(1)} %select_convert_fusion), channel_id=1, source_target_pairs={{0,2},{1,3},{16,18},{17,19},{32,34},{33,35},{48,50},{49,51},{2,0},... | collective-permute-start | bytes 663560 | tf_op jit(solution)/shard_map/ppermute | solution.py:46
  52.1 16.5 %collective-permute-start.10 = (bf16[72,1536]{1,0:T(8,128)(2,1)S(1)}, bf16[72,1536]{1,0:T(8,128)(2,1)S(1)}, u32[]{:S(2)}, u32[]{:S(2)}) collective-permute-start(bf16[72,1536]{1,0:T(8,128)(2,1)S(1)} %get-tuple-element.78), channel_id=1, source_target_pairs={{0,2},{1,3},{16,18},{17,19},{32,34},{33,35},{48,50},{49,51},{2,0},... | collective-permute-start | bytes 663560 | tf_op jit(solution)/shard_map/ppermute | solution.py:46
  60.7 7.9 %collective-permute-start.11 = (f32[36,1536]{1,0:T(8,128)S(1)}, f32[36,1536]{1,0:T(8,128)S(1)}, u32[]{:S(2)}, u32[]{:S(2)}) collective-permute-start(f32[36,1536]{1,0:T(8,128)S(1)} %slice_select_fusion.1), channel_id=1, source_target_pairs={{0,1},{1,0},{16,17},{17,16},{32,33},{33,32},{48,49},{49,48},{2,3},... | collective-permute-start | bytes 663560 | tf_op jit(solution)/shard_map/ppermute | solution.py:46
  68.6 7.5 %collective-permute-start.15 = (bf16[72,1536]{1,0:T(8,128)(2,1)S(1)}, bf16[72,1536]{1,0:T(8,128)(2,1)S(1)}, u32[]{:S(2)}, u32[]{:S(2)}) collective-permute-start(bf16[72,1536]{1,0:T(8,128)(2,1)S(1)} %get-tuple-element.84), channel_id=1, source_target_pairs={{0,8},{16,24},{32,40},{48,56},{2,10},{18,26},{34,42},{50,58},{4,12... | collective-permute-start | bytes 663560 | tf_op jit(solution)/shard_map/ppermute | solution.py:46
  70.7 7.9 %collective-permute-start.16 = (bf16[72,1536]{1,0:T(8,128)(2,1)S(1)}, bf16[72,1536]{1,0:T(8,128)(2,1)S(1)}, u32[]{:S(2)}, u32[]{:S(2)}) collective-permute-start(bf16[72,1536]{1,0:T(8,128)(2,1)S(1)} %get-tuple-element.85), channel_id=1, source_target_pairs={{0,8},{16,24},{32,40},{48,56},{2,10},{18,26},{34,42},{50,58},{4,12... | collective-permute-start | bytes 663560 | tf_op jit(solution)/shard_map/ppermute | solution.py:46
  72.3 11.0 %collective-permute-start.12 = (bf16[2,72,1536]{2,1,0:T(8,128)(2,1)S(1)}, bf16[2,72,1536]{2,1,0:T(8,128)(2,1)S(1)}, u32[]{:S(2)}, u32[]{:S(2)}) collective-permute-start(bf16[2,72,1536]{2,1,0:T(8,128)(2,1)S(1)} %pad_maximum_fusion.2), channel_id=1, source_target_pairs={{0,4},{16,20},{32,36},{48,52},{2,6},{18,22},{34,38},{50,54},{4,8},... | collective-permute-start | bytes 1327112 | tf_op jit(solution)/shard_map/ppermute | solution.py:46
  73.7 15.7 %collective-permute-start.14 = (bf16[2,72,1536]{2,1,0:T(8,128)(2,1)S(1)}, bf16[2,72,1536]{2,1,0:T(8,128)(2,1)S(1)}, u32[]{:S(2)}, u32[]{:S(2)}) collective-permute-start(bf16[2,72,1536]{2,1,0:T(8,128)(2,1)S(1)} %pad_maximum_fusion.2), channel_id=1, source_target_pairs={{0,12},{16,28},{32,44},{48,60},{2,14},{18,30},{34,46},{50,62},{4,0... | collective-permute-start | bytes 1327112 | tf_op jit(solution)/shard_map/ppermute | solution.py:46
  83.3 20.4 %collective-permute-start.22 = (bf16[2,144,1536]{2,1,0:T(8,128)(2,1)S(1)}, bf16[2,144,1536]{2,1,0:T(8,128)(2,1)S(1)}, u32[]{:S(2)}, u32[]{:S(2)}) collective-permute-start(bf16[2,144,1536]{2,1,0:T(8,128)(2,1)S(1)} %pad_maximum_fusion.refs_0_.refs_4_), channel_id=1, source_target_pairs={{0,1},{1,0},{16,17},{17,16},{32,33},{33,32},{48,49},{49,48},{2,3},... | collective-permute-start | bytes 2654216 | tf_op jit(solution)/shard_map/ppermute | solution.py:46
  83.4 20.3 %collective-permute-start.18 = (bf16[2,144,1536]{2,1,0:T(8,128)(2,1)S(1)}, bf16[2,144,1536]{2,1,0:T(8,128)(2,1)S(1)}, u32[]{:S(2)}, u32[]{:S(2)}) collective-permute-start(bf16[2,144,1536]{2,1,0:T(8,128)(2,1)S(1)} %pad_maximum_fusion.refs_0_.refs_4_), channel_id=1, source_target_pairs={{0,50},{16,0},{32,16},{48,32},{2,48},{18,2},{34,18},{50,34},{4,54}... | collective-permute-start | bytes 2654216 | tf_op jit(solution)/shard_map/ppermute | solution.py:46
  89.4 14.4 %collective-permute-start.13 = (bf16[2,144,1536]{2,1,0:T(8,128)(2,1)S(1)}, bf16[2,144,1536]{2,1,0:T(8,128)(2,1)}, u32[]{:S(2)}, u32[]{:S(2)}) collective-permute-start(bf16[2,144,1536]{2,1,0:T(8,128)(2,1)S(1)} %pad_maximum_fusion.refs_0_.refs_4_), channel_id=1, source_target_pairs={{0,16},{16,32},{32,48},{48,2},{2,18},{18,34},{34,50},{50,0},{4,20}... | collective-permute-start | bytes 2654216 | tf_op jit(solution)/shard_map/ppermute | solution.py:46
  89.5 19.9 %collective-permute-start.19 = (bf16[2,144,1536]{2,1,0:T(8,128)(2,1)S(1)}, bf16[2,144,1536]{2,1,0:T(8,128)(2,1)}, u32[]{:S(2)}, u32[]{:S(2)}) collective-permute-start(bf16[2,144,1536]{2,1,0:T(8,128)(2,1)S(1)} %pad_maximum_fusion.1.refs_1_.refs_5_), channel_id=1, source_target_pairs={{0,50},{16,0},{32,16},{48,32},{2,48},{18,2},{34,18},{50,34},{4,54}... | collective-permute-start | bytes 2654216 | tf_op jit(solution)/shard_map/ppermute | solution.py:46
  92.8 20.4 %collective-permute-start.23 = (bf16[2,144,1536]{2,1,0:T(8,128)(2,1)S(1)}, bf16[2,144,1536]{2,1,0:T(8,128)(2,1)S(1)}, u32[]{:S(2)}, u32[]{:S(2)}) collective-permute-start(bf16[2,144,1536]{2,1,0:T(8,128)(2,1)S(1)} %pad_maximum_fusion.1.refs_1_.refs_5_), channel_id=1, source_target_pairs={{0,1},{1,0},{16,17},{17,16},{32,33},{33,32},{48,49},{49,48},{2,3},... | collective-permute-start | bytes 2654216 | tf_op jit(solution)/shard_map/ppermute | solution.py:46
  103.8 14.4 %collective-permute-start.17 = (bf16[2,144,1536]{2,1,0:T(8,128)(2,1)S(1)}, bf16[2,144,1536]{2,1,0:T(8,128)(2,1)}, u32[]{:S(2)}, u32[]{:S(2)}) collective-permute-start(bf16[2,144,1536]{2,1,0:T(8,128)(2,1)S(1)} %pad_maximum_fusion.1.refs_1_.refs_5_), channel_id=1, source_target_pairs={{0,16},{16,32},{32,48},{48,2},{2,18},{18,34},{34,50},{50,0},{4,20}... | collective-permute-start | bytes 2654216 | tf_op jit(solution)/shard_map/ppermute | solution.py:46
  103.8 14.4 %collective-permute-start.26 = (bf16[2,144,1536]{2,1,0:T(8,128)(2,1)S(1)}, bf16[2,144,1536]{2,1,0:T(8,128)(2,1)S(1)}, u32[]{:S(2)}, u32[]{:S(2)}) collective-permute-start(bf16[2,144,1536]{2,1,0:T(8,128)(2,1)S(1)} %collective-permute-done.18.refs_4_.refs_8_), channel_id=1, source_target_pairs={{0,1},{1,0},{16,17},{17,16},{32,33},{33,32},{48,49},{49,48},{2,3},... | collective-permute-start | bytes 2654216 | tf_op jit(solution)/shard_map/ppermute | solution.py:46
  103.8 23.8 %collective-permute-start.20 = (bf16[2,144,1536]{2,1,0:T(8,128)(2,1)}, bf16[2,144,1536]{2,1,0:T(8,128)(2,1)}, u32[]{:S(2)}, u32[]{:S(2)}) collective-permute-start(bf16[2,144,1536]{2,1,0:T(8,128)(2,1)} %collective-permute-done.13.refs_2_.refs_6_), channel_id=1, source_target_pairs={{0,16},{16,32},{32,48},{48,2},{2,18},{18,34},{34,50},{50,0},{4,20}... | collective-permute-start | bytes 2654216 | tf_op jit(solution)/shard_map/ppermute | solution.py:46
  109.4 18.2 %collective-permute-start.21 = (bf16[2,144,1536]{2,1,0:T(8,128)(2,1)}, bf16[2,144,1536]{2,1,0:T(8,128)(2,1)}, u32[]{:S(2)}, u32[]{:S(2)}) collective-permute-start(bf16[2,144,1536]{2,1,0:T(8,128)(2,1)} %collective-permute-done.19.refs_5_.refs_9_), channel_id=1, source_target_pairs={{0,50},{16,0},{32,16},{48,32},{2,48},{18,2},{34,18},{50,34},{4,54}... | collective-permute-start | bytes 2654216 | tf_op jit(solution)/shard_map/ppermute | solution.py:46
  113.2 16.7 %collective-permute-start.24 = (bf16[2,144,1536]{2,1,0:T(8,128)(2,1)}, bf16[2,144,1536]{2,1,0:T(8,128)(2,1)}, u32[]{:S(2)}, u32[]{:S(2)}) collective-permute-start(bf16[2,144,1536]{2,1,0:T(8,128)(2,1)} %collective-permute-done.13.refs_2_.refs_6_), channel_id=1, source_target_pairs={{0,1},{1,0},{16,17},{17,16},{32,33},{33,32},{48,49},{49,48},{2,3},... | collective-permute-start | bytes 2654216 | tf_op jit(solution)/shard_map/ppermute | solution.py:46
  118.1 11.8 %collective-permute-start.27 = (bf16[2,144,1536]{2,1,0:T(8,128)(2,1)}, bf16[2,144,1536]{2,1,0:T(8,128)(2,1)}, u32[]{:S(2)}, u32[]{:S(2)}) collective-permute-start(bf16[2,144,1536]{2,1,0:T(8,128)(2,1)} %collective-permute-done.19.refs_5_.refs_9_), channel_id=1, source_target_pairs={{0,1},{1,0},{16,17},{17,16},{32,33},{33,32},{48,49},{49,48},{2,3},... | collective-permute-start | bytes 2654216 | tf_op jit(solution)/shard_map/ppermute | solution.py:46
  118.1 11.8 %collective-permute-start.25 = (bf16[2,144,1536]{2,1,0:T(8,128)(2,1)}, bf16[2,144,1536]{2,1,0:T(8,128)(2,1)}, u32[]{:S(2)}, u32[]{:S(2)}) collective-permute-start(bf16[2,144,1536]{2,1,0:T(8,128)(2,1)} %collective-permute-done.17.refs_3_.refs_7_), channel_id=1, source_target_pairs={{0,1},{1,0},{16,17},{17,16},{32,33},{33,32},{48,49},{49,48},{2,3},... | collective-permute-start | bytes 2654216 | tf_op jit(solution)/shard_map/ppermute | solution.py:46
  135.2 66.7 %collective-permute-start.32 = (bf16[64,576]{1,0:T(8,128)(2,1)S(1)}, bf16[64,576]{1,0:T(8,128)(2,1)S(1)}, u32[]{:S(2)}, u32[]{:S(2)}) collective-permute-start(bf16[64,576]{1,0:T(8,128)(2,1)S(1)} %get-tuple-element.66), channel_id=1, source_target_pairs={{128,192},{129,193},{144,208},{145,209},{160,224},{161,225},{176,2... | collective-permute-start | bytes 221192 | tf_op jit(solution)/shard_map/ppermute | solution.py:46
  (22 other events, 353.6 us)
where the time goes:
time: 226 us; the launch traced here: 227 us
  waiting for transfers between devices  129 us (57%)
  starting transfers between devices  64.8 us (29%)
  Pallas kernels  22.9 us (10%)
  local copies, waits for them, and re-layouts  6.91 us (3%)
  other arithmetic  2.32 us (1%)
    ppermute x36, waiting for transfers between devices, send(): return lax.ppermute(block, AXES, pairs)  129 us
    ppermute x36, starting transfers between devices, send(): return lax.ppermute(block, AXES, pairs)  64.8 us
    pallas_call x4, Pallas kernels, relay(): pl.pallas_call(functools.partial(relay_kernel, step, len(held) > 0), name...  18.8 us
  transfers between devices with their start and end apart: 36, of which 18 were waited for; matrix products, arithmetic and copies ran while one was open for 3% of the time, Pallas kernels for 0%

commit v1 on v0

--- a/solution.py
+++ b/solution.py
@@ -4,6 +4,7 @@
 import jax.numpy as jnp
 from jax import lax
 from jax.experimental import pallas as pl
+from jax.experimental.layout import Layout, with_layout_constraint
 from jax.experimental.pallas import tpu as pltpu
 from jax.sharding import PartitionSpec as P
 
@@ -46,14 +47,16 @@
     return lax.ppermute(block, AXES, pairs)
 
 
-def pair_kernel(info, a_own, b_own, a_got, b_got, *refs):
-    outs, own_v, got_v, own_sem, got_sem = refs[:4], *refs[4:]
-    y, core = info[2], info[3]
-    quarter = own_v.shape[1]
+def pair_kernel(place, a_own, b_own, a_got, b_got, *refs):
+    outs, own_v, got_v, own_sem, got_sem = refs[:8], *refs[8:]
+    y, core, z_high = place[0], place[1], place[2]
+    chunk = own_v.shape[1]
 
     def fetch(own, got):
-        for at, by in enumerate(QUARTERS):
-            rows = pl.ds(pl.multiple_of(lax.rem(y + by, 4) * quarter, 16), quarter)
+        for at in range(8):
+            half = 1 - z_high if at < 4 else z_high
+            row = (2 * lax.rem(y + QUARTERS[at % 4], 4) + half) * chunk
+            rows = pl.ds(pl.multiple_of(row, 8), chunk)
             pltpu.make_async_copy(own.at[rows], own_v.at[at], own_sem.at[at]).start()
             pltpu.make_async_copy(got.at[rows], got_v.at[at], got_sem.at[at]).start()
 
@@ -65,30 +68,30 @@
     def _():
         fetch(b_own, b_got)
 
-    for at in range(4):
+    for at in range(8):
         pltpu.make_async_copy(own_v.at[at], own_v.at[at], own_sem.at[at]).wait()
         pltpu.make_async_copy(got_v.at[at], got_v.at[at], got_sem.at[at]).wait()
         outs[at][...] = (own_v[at].astype(F32) + got_v[at].astype(F32)).astype(BF16)
 
 
-def pair_sum(info, *blocks):
+def pair_sum(place, *blocks):
     height, hidden = blocks[0].shape
-    quarter = height // 4
+    chunk = height // 8
     vmem, hbm = pl.BlockSpec(memory_space=pltpu.VMEM), pl.BlockSpec(memory_space=pltpu.HBM)
     return pl.pallas_call(
         pair_kernel,
         name="pair_sum",
-        out_shape=(jax.ShapeDtypeStruct((quarter, hidden), BF16),) * 4,
+        out_shape=(jax.ShapeDtypeStruct((chunk, hidden), BF16),) * 8,
         in_specs=[pl.BlockSpec(memory_space=pltpu.SMEM)] + [hbm] * 4,
-        out_specs=(vmem,) * 4,
+        out_specs=(vmem,) * 8,
         scratch_shapes=[
-            pltpu.VMEM((4, quarter, hidden), BF16),
-            pltpu.VMEM((4, quarter, hidden), BF16),
-            pltpu.SemaphoreType.DMA((4,)),
-            pltpu.SemaphoreType.DMA((4,)),
+            pltpu.VMEM((8, chunk, hidden), BF16),
+            pltpu.VMEM((8, chunk, hidden), BF16),
+            pltpu.SemaphoreType.DMA((8,)),
+            pltpu.SemaphoreType.DMA((8,)),
         ],
         compiler_params=pltpu.CompilerParams(vmem_limit_bytes=48 << 20),
-    )(info, *[pltpu.with_memory_space_constraint(block, pltpu.HBM) for block in blocks])
+    )(place, *[pltpu.with_memory_space_constraint(block, pltpu.HBM) for block in blocks])
 
 
 def relay_kernel(step, has_held, info, rows_ref, *refs):
@@ -206,7 +209,7 @@
             pltpu.SemaphoreType.DMA((4,)),
             pltpu.SemaphoreType.DMA((4,)),
         ],
-        compiler_params=pltpu.CompilerParams(vmem_limit_bytes=48 << 20),
+        compiler_params=pltpu.CompilerParams(vmem_limit_bytes=20 << 20),
     )(info, rows, *held, *own, *crossed)
 
 
@@ -241,7 +244,6 @@
     replicas = lax.axis_size("replica")
     owned, hidden = wa_master.shape[1], wa_master.shape[2]
     chunk = 2 * owned
-    place = jnp.stack([x, z_low, y, core])
 
     a_own, b_own = wa_local[0, 0], wb_local[0, 0].T
     a_got = send(a_own, core_swap((1,)))
@@ -250,15 +252,24 @@
         send(counts, route(lambda x, y, z, core, by=by: (x, y, z // 4 * 4 + (z + by) % 4, core)))
         for by in (1, 2, 3)
     ]
-    across, ahead, behind, mine = pair_sum(place, a_own, b_own, a_got, b_got)
-    gots = send(across, y_step(2)), send(ahead, y_step(1)), send(behind, y_step(-1))
-    info = jnp.concatenate([place, *layers, jnp.array(PLACE, jnp.int32)])
-    gots, info, wa_master, wb_master, wa_moment, wb_moment = lax.optimization_barrier(
-        (gots, info, wa_master, wb_master, wa_moment, wb_moment)
-    )
-    total = mine.astype(F32) + sum(got.astype(F32) for got in gots)
-    top, bottom = total[:chunk], total[chunk:]
-    z_got = send(jnp.where(low, bottom, top).astype(BF16), z_step(4))
+    def y_sends(across, ahead, behind):
+        return send(across, y_step(2)), send(ahead, y_step(1)), send(behind, y_step(-1))
+
+    *away, away_mine, across, ahead, behind, mine = pair_sum(
+        jnp.stack([y, core, z_high]), a_own, b_own, a_got, b_got
+    )
+    away_gots = y_sends(*away)
+    info = jnp.concatenate(
+        [jnp.stack([x, z_low, y, core]), *layers, jnp.array(PLACE, jnp.int32)]
+    )
+    away_gots, kept_parts, info, wa_master, wb_master, wa_moment, wb_moment = (
+        lax.optimization_barrier(
+            (away_gots, (across, ahead, behind), info, wa_master, wb_master, wa_moment, wb_moment)
+        )
+    )
+    away_total = away_mine.astype(F32) + sum(got.astype(F32) for got in away_gots)
+    z_got = send(away_total.astype(BF16), z_step(4))
+    total = mine.astype(F32) + sum(got.astype(F32) for got in y_sends(*kept_parts))
 
     gain = 0.7 * 1.9
     a_state = (1.0 - gain) * wa_master[0] - (0.7 * 0.81) * wa_moment[0]
@@ -266,7 +277,7 @@
     kept = jnp.where(first, a_state, b_state)
     state_got = send(jnp.where(first, b_state, a_state), core_swap())
     state = jnp.concatenate([jnp.where(first, kept, state_got), jnp.where(first, state_got, kept)])
-    updated = state + (gain / replicas) * (jnp.where(low, top, bottom) + z_got.astype(F32))
+    updated = state + (gain / replicas) * (total + z_got.astype(F32))
     w = updated.astype(BF16)
     ours = jnp.where(first, updated[:owned], updated[owned:])
     theirs = send(jnp.where(first, updated[owned:], updated[:owned]), core_swap())
@@ -278,8 +289,12 @@
         return z_step(by, (0,)) + y_step(by, (1,))
 
     w_far, theirs = lax.optimization_barrier((send(w, z_step(4)), theirs))
-    wa_next = jnp.where(first, ours, theirs)[None]
-    wb_next = jnp.where(first, theirs, ours).T[None]
+    wa_next = with_layout_constraint(
+        jnp.where(first, ours, theirs)[None], Layout((1, 0, 2))
+    )
+    wb_next = with_layout_constraint(
+        jnp.where(first, theirs, ours).T[None], Layout((2, 0, 1))
+    )
     k_low, k_high = jnp.where(low, w, w_far), jnp.where(low, w_far, w)
     k0 = jnp.stack([k_low, k_high])
     k_behind, k_ahead = send(k0, turn(1)), send(k0, turn(-1))
@@ -287,15 +302,17 @@
     shape = (2, 2 * chunk, hidden)
     near = jnp.stack([k0, k_behind]).reshape(shape)
     far = jnp.stack([k_ahead, k_across]).reshape(shape)
-    near_behind, near_ahead = send(near, cross(1)), send(near, cross(-1))
-    far_behind, far_ahead = send(far, cross(1)), send(far, cross(-1))
-    near_behind, wa_next, wb_next = lax.optimization_barrier((near_behind, wa_next, wb_next))
-    near_across, far_across = send(near_behind, cross(1)), send(far_ahead, cross(-1))
+    rows_each = inputs.shape[0] // 4
+    rows = lax.dynamic_slice_in_dim(inputs, z_low * rows_each, rows_each, 0)
+    near_behind, far_later, wa_next, wb_next, rows = lax.optimization_barrier(
+        (send(near, cross(1)), far, wa_next, wb_next, rows)
+    )
+    far_ahead, near_later = lax.optimization_barrier((send(far, cross(-1)), near))
+    near_across, far_behind = send(near_behind, cross(1)), send(far_later, cross(1))
+    far_across, near_ahead = send(far_ahead, cross(-1)), send(near_later, cross(-1))
     own = [near, far, near_behind, far_behind, near_ahead, far_ahead, near_across, far_across]
     crossed = [send(block, core_swap()) for block in own]
 
-    rows_each = inputs.shape[0] // 4
-    rows = lax.dynamic_slice_in_dim(inputs, z_low * rows_each, rows_each, 0)
     held = ()
     for step in range(4):
         *held, last = relay(step, info, rows, held, own, crossed)

time: 226 us -> 250 us (1.11)
  waiting for transfers between devices: 129 us -> 144 us
  Pallas kernels: 22.9 us -> 30.8 us
    ppermute x36 -> x39, waiting for transfers between devices: 129 us -> 144 us  [send(): return lax.ppermute(block, AXES, pairs)]
    pallas_call x4, Pallas kernels: 18.8 us -> 26.5 us  [relay(): pl.pallas_call(functools.partial(relay_kernel, step, len(held) > 0), name...]
    unnamed x23 -> x14, local copies, waits for them, and re-layouts: 4.12 us -> 1.28 us
    ppermute x36 -> x39, starting transfers between devices: 64.8 us -> 63.6 us  [send(): return lax.ppermute(block, AXES, pairs)]
  transfers between devices with their start and end apart: 36 -> 39, of which waited for: 18 -> 20; matrix products, arithmetic and copies ran while one was open for 3% -> 3% of each run, Pallas kernels for 0% -> 0%
where the time goes in v1:
time: 250 us; the launch traced here: 249 us
  waiting for transfers between devices  144 us (58%)
  starting transfers between devices  63.6 us (25%)
  Pallas kernels  30.8 us (12%)
  local copies, waits for them, and re-layouts  6.84 us (3%)
  other arithmetic  2.88 us (1%)
    ppermute x39, waiting for transfers between devices, send(): return lax.ppermute(block, AXES, pairs)  144 us
    ppermute x39, starting transfers between devices, send(): return lax.ppermute(block, AXES, pairs)  63.6 us
    pallas_call x4, Pallas kernels, relay(): pl.pallas_call(functools.partial(relay_kernel, step, len(held) > 0), name...  26.5 us
  transfers between devices with their start and end apart: 39, of which 20 were waited for; matrix products, arithmetic and copies ran while one was open for 3% of the time, Pallas kernels for 0%

profile of v1, /device:TPU:6, one launch (start us, length us, event | category | flops | bytes accessed | tf_op | source)
XLA Modules:
  0.0 249.4 jit_solution(6790732705481920722)
XLA Ops:
  2.1 4.4 %collective-permute-start.1 = (bf16[576,1536]{1,0:T(8,128)(2,1)}, bf16[576,1536]{1,0:T(8,128)(2,1)}, u32[]{:S(2)}, u32[]{:S(2)}) collective-permute-start(bf16[576,1536]{1,0:T(8,128)(2,1)} %bitcast.44), channel_id=1, source_target_pairs={{0,1},{16,17},{32,33},{48,49},{2,3},{18,19},{34,35},{50,51},{4,5},... | collective-permute-start | bytes 5308424 | tf_op jit(solution)/shard_map/ppermute | solution.py:47
  8.9 2.8 %pair_sum.1 = (bf16[72,1536]{1,0:T(8,128)(2,1)S(1)}, bf16[72,1536]{1,0:T(8,128)(2,1)S(1)}, bf16[72,1536]{1,0:T(8,128)(2,1)S(1)}, bf16[72,1536]{1,0:T(8,128)(2,1)...) custom-call(s32[3]{0:T(128)S(1)} %pad_add_fusion.place, ...), custom_call_target="tpu_custom_call" | custom-call | tf_op jit(solution)/shard_map/pair_sum/pallas_call | solution.py:81
  11.7 3.3 %collective-permute-start.2 = (bf16[72,1536]{1,0:T(8,128)(2,1)S(1)}, bf16[72,1536]{1,0:T(8,128)(2,1)S(1)}, u32[]{:S(2)}, u32[]{:S(2)}) collective-permute-start(bf16[72,1536]{1,0:T(8,128)(2,1)S(1)} %get-tuple-element.50), channel_id=1, source_target_pairs={{0,8},{1,9},{16,24},{17,25},{32,40},{33,41},{48,56},{49,57},{2,10}... | collective-permute-start | bytes 663560 | tf_op jit(solution)/shard_map/ppermute | solution.py:47
  15.7 2.6 %collective-permute-start.4 = (bf16[72,1536]{1,0:T(8,128)(2,1)S(1)}, bf16[72,1536]{1,0:T(8,128)(2,1)}, u32[]{:S(2)}, u32[]{:S(2)}) collective-permute-start(bf16[72,1536]{1,0:T(8,128)(2,1)S(1)} %get-tuple-element.52), channel_id=1, source_target_pairs={{0,12},{1,13},{16,28},{17,29},{32,44},{33,45},{48,60},{49,61},{2,1... | collective-permute-start | bytes 663560 | tf_op jit(solution)/shard_map/ppermute | solution.py:47
  18.2 3.3 %collective-permute-start.6 = (s32[1]{0:T(128)}, s32[1]{0:T(128)}, u32[]{:S(2)}, u32[]{:S(2)}) collective-permute-start(s32[1]{0:T(128)} %param.15), channel_id=1, source_target_pairs={{0,32},{1,33},{16,48},{17,49},{32,0},{33,1},{48,16},{49,17},{2,34}... | collective-permute-start | bytes 20 | tf_op jit(solution)/shard_map/ppermute | solution.py:47
  24.1 3.3 %collective-permute-start.7 = (s32[1]{0:T(128)}, s32[1]{0:T(128)}, u32[]{:S(2)}, u32[]{:S(2)}) collective-permute-start(s32[1]{0:T(128)} %param.15), channel_id=1, source_target_pairs={{0,48},{1,49},{16,0},{17,1},{32,16},{33,17},{48,32},{49,33},{2,50}... | collective-permute-start | bytes 20 | tf_op jit(solution)/shard_map/ppermute | solution.py:47
  31.8 2.5 collective-permute-start.11
  35.5 4.9 %collective-permute-start.12 = (bf16[72,1536]{1,0:T(8,128)(2,1)S(1)}, bf16[72,1536]{1,0:T(8,128)(2,1)S(1)}, u32[]{:S(2)}, u32[]{:S(2)}) collective-permute-start(bf16[72,1536]{1,0:T(8,128)(2,1)S(1)} %add_convert_fusion), channel_id=1, source_target_pairs={{0,2},{1,3},{16,18},{17,19},{32,34},{33,35},{48,50},{49,51},{2,0},... | collective-permute-start | bytes 663560 | tf_op jit(solution)/shard_map/ppermute | solution.py:47
  42.2 7.0 %collective-permute-done.12 = bf16[72,1536]{1,0:T(8,128)(2,1)S(1)} collective-permute-done((bf16[72,1536]{1,0:T(8,128)(2,1)S(1)}, bf16[72,1536]{1,0:T(8,128)(2,1)S(1)}, u32[]{:S(2)}, u32[]{:S(2)}) %collective-permute-start.12) | collective-permute-done | bytes 221216 | tf_op jit(solution)/shard_map/ppermute | solution.py:47
  49.4 5.6 %collective-permute-start.13 = (bf16[72,1536]{1,0:T(8,128)(2,1)S(1)}, bf16[72,1536]{1,0:T(8,128)(2,1)S(1)}, u32[]{:S(2)}, u32[]{:S(2)}) collective-permute-start(bf16[72,1536]{1,0:T(8,128)(2,1)S(1)} %get-tuple-element.97), channel_id=1, source_target_pairs={{0,2},{1,3},{16,18},{17,19},{32,34},{33,35},{48,50},{49,51},{2,0},... | collective-permute-start | bytes 663560 | tf_op jit(solution)/shard_map/ppermute | solution.py:47
  55.2 5.5 %collective-permute-done.13 = bf16[72,1536]{1,0:T(8,128)(2,1)S(1)} collective-permute-done((bf16[72,1536]{1,0:T(8,128)(2,1)S(1)}, bf16[72,1536]{1,0:T(8,128)(2,1)S(1)}, u32[]{:S(2)}, u32[]{:S(2)}) %collective-permute-start.13) | collective-permute-done | bytes 221216 | tf_op jit(solution)/shard_map/ppermute | solution.py:47
  60.7 2.3 collective-permute-start.18
  64.9 3.1 %collective-permute-start.17 = (bf16[2,72,1536]{2,1,0:T(8,128)(2,1)S(1)}, bf16[2,72,1536]{2,1,0:T(8,128)(2,1)S(1)}, u32[]{:S(2)}, u32[]{:S(2)}) collective-permute-start(bf16[2,72,1536]{2,1,0:T(8,128)(2,1)S(1)} %pad_maximum_fusion.2), channel_id=1, source_target_pairs={{0,12},{16,28},{32,44},{48,60},{2,14},{18,30},{34,46},{50,62},{4,0... | collective-permute-start | bytes 1327112 | tf_op jit(solution)/shard_map/ppermute | solution.py:47
  68.2 2.5 collective-permute-done.19
  70.7 4.6 %collective-permute-done.15 = bf16[2,72,1536]{2,1,0:T(8,128)(2,1)S(1)} collective-permute-done((bf16[2,72,1536]{2,1,0:T(8,128)(2,1)S(1)}, bf16[2,72,1536]{2,1,0:T(8,128)(2,1)S(1)}, u32[]{:S(2)}, u32[]{:S(2)}) %collective-permute-start.15) | collective-permute-done | bytes 442400 | tf_op jit(solution)/shard_map/ppermute | solution.py:47
  75.4 5.2 %collective-permute-start.16 = (bf16[2,144,1536]{2,1,0:T(8,128)(2,1)S(1)}, bf16[2,144,1536]{2,1,0:T(8,128)(2,1)S(1)}, u32[]{:S(2)}, u32[]{:S(2)}) collective-permute-start(bf16[2,144,1536]{2,1,0:T(8,128)(2,1)S(1)} %pad_maximum_fusion.refs_0_.refs_4_), channel_id=1, source_target_pairs={{0,16},{16,32},{32,48},{48,2},{2,18},{18,34},{34,50},{50,0},{4,20}... | collective-permute-start | bytes 2654216 | tf_op jit(solution)/shard_map/ppermute | solution.py:47
  80.6 2.8 %collective-permute-start.21 = (bf16[2,144,1536]{2,1,0:T(8,128)(2,1)S(1)}, bf16[2,144,1536]{2,1,0:T(8,128)(2,1)}, u32[]{:S(2)}, u32[]{:S(2)}) collective-permute-start(bf16[2,144,1536]{2,1,0:T(8,128)(2,1)S(1)} %pad_maximum_fusion.1.refs_1_.refs_5_), channel_id=1, source_target_pairs={{0,50},{16,0},{32,16},{48,32},{2,48},{18,2},{34,18},{50,34},{4,54}... | collective-permute-start | bytes 2654216 | tf_op jit(solution)/shard_map/ppermute | solution.py:47
  88.6 5.8 %collective-permute-done.16.refs_2_.refs_6_ = bf16[2,144,1536]{2,1,0:T(8,128)(2,1)S(1)} collective-permute-done((bf16[2,144,1536]{2,1,0:T(8,128)(2,1)S(1)}, bf16[2,144,1536]{2,1,0:T(8,128)(2,1)S(1)}, u32[]{:S(2)}, u32[]{:S(2)}) %collective-permute-start.16) | collective-permute-done | bytes 884768 | tf_op jit(solution)/shard_map/ppermute | solution.py:47
  94.4 3.0 %collective-permute-start.20 = (bf16[2,144,1536]{2,1,0:T(8,128)(2,1)S(1)}, bf16[2,144,1536]{2,1,0:T(8,128)(2,1)S(1)}, u32[]{:S(2)}, u32[]{:S(2)}) collective-permute-start(bf16[2,144,1536]{2,1,0:T(8,128)(2,1)S(1)} %pad_maximum_fusion.1.refs_1_.refs_5_), channel_id=1, source_target_pairs={{0,16},{16,32},{32,48},{48,2},{2,18},{18,34},{34,50},{50,0},{4,20}... | collective-permute-start | bytes 2654216 | tf_op jit(solution)/shard_map/ppermute | solution.py:47
  99.9 18.2 %collective-permute-done.20.refs_3_.refs_7_ = bf16[2,144,1536]{2,1,0:T(8,128)(2,1)S(1)} collective-permute-done((bf16[2,144,1536]{2,1,0:T(8,128)(2,1)S(1)}, bf16[2,144,1536]{2,1,0:T(8,128)(2,1)S(1)}, u32[]{:S(2)}, u32[]{:S(2)}) %collective-permute-start.20) | collective-permute-done | bytes 884768 | tf_op jit(solution)/shard_map/ppermute | solution.py:47
  130.4 84.2 %collective-permute-done.35.rows_ref = bf16[64,576]{1,0:T(8,128)(2,1)S(1)} collective-permute-done((bf16[64,576]{1,0:T(8,128)(2,1)S(1)}, bf16[64,576]{1,0:T(8,128)(2,1)S(1)}, u32[]{:S(2)}, u32[]{:S(2)}) %collective-permute-start.35) | collective-permute-done | bytes 73760 | tf_op jit(solution)/shard_map/ppermute | solution.py:47
  214.6 24.4 %relay.7 = (bf16[64,576]{1,0:T(8,128)(2,1)S(1)}, bf16[64,576]{1,0:T(8,128)(2,1)S(1)}, bf16[64,576]{1,0:T(8,128)(2,1)S(1)}, bf16[64,576]{1,0:T(8,128)(2,1)S(1)}, bf16[64,576]{1,0:T(8,128)(2,1)}) custom-call(s32[12]{0:T(128)S(1)} %concatenate.8.info, bf16[64,576]{1,0:T(8,128)(2,1)S(1)} %collective-permute-done.35.rows_ref, ...), custom_call_target="tpu_custom_call" | custom-call | tf_op jit(solution)/shard_map/relay/pallas_call | solution.py:196
  239.1 3.6 %collective-permute-start.37 = (bf16[64,576]{1,0:T(8,128)(2,1)S(1)}, bf16[64,576]{1,0:T(8,128)(2,1)S(1)}, u32[]{:S(2)}, u32[]{:S(2)}) collective-permute-start(bf16[64,576]{1,0:T(8,128)(2,1)S(1)} %get-tuple-element.95), channel_id=1, source_target_pairs={{0,32},{1,33},{16,48},{17,49},{32,0},{33,1},{48,16},{49,17},{2,34}... | collective-permute-start | bytes 221192 | tf_op jit(solution)/shard_map/ppermute | solution.py:47
  242.9 2.5 %collective-permute-done.36.refs_1_ = bf16[64,576]{1,0:T(8,128)(2,1)S(1)} collective-permute-done((bf16[64,576]{1,0:T(8,128)(2,1)S(1)}, bf16[64,576]{1,0:T(8,128)(2,1)S(1)}, u32[]{:S(2)}, u32[]{:S(2)}) %collective-permute-start.36) | collective-permute-done | bytes 73760 | tf_op jit(solution)/shard_map/ppermute | solution.py:47
  (91 shorter events, 40.5 us)
Async XLA Ops:
  2.1 6.8 %collective-permute-start.1 = (bf16[576,1536]{1,0:T(8,128)(2,1)}, bf16[576,1536]{1,0:T(8,128)(2,1)}, u32[]{:S(2)}, u32[]{:S(2)}) collective-permute-start(bf16[576,1536]{1,0:T(8,128)(2,1)} %bitcast.44), channel_id=1, source_target_pairs={{0,1},{16,17},{32,33},{48,49},{2,3},{18,19},{34,35},{50,51},{4,5},... | collective-permute-start | bytes 5308424 | tf_op jit(solution)/shard_map/ppermute | solution.py:47
  11.7 19.1 %collective-permute-start.2 = (bf16[72,1536]{1,0:T(8,128)(2,1)S(1)}, bf16[72,1536]{1,0:T(8,128)(2,1)S(1)}, u32[]{:S(2)}, u32[]{:S(2)}) collective-permute-start(bf16[72,1536]{1,0:T(8,128)(2,1)S(1)} %get-tuple-element.50), channel_id=1, source_target_pairs={{0,8},{1,9},{16,24},{17,25},{32,40},{33,41},{48,56},{49,57},{2,10}... | collective-permute-start | bytes 663560 | tf_op jit(solution)/shard_map/ppermute | solution.py:47
  15.0 15.8 %collective-permute-start.3 = (bf16[72,1536]{1,0:T(8,128)(2,1)S(1)}, bf16[72,1536]{1,0:T(8,128)(2,1)S(1)}, u32[]{:S(2)}, u32[]{:S(2)}) collective-permute-start(bf16[72,1536]{1,0:T(8,128)(2,1)S(1)} %get-tuple-element.51), channel_id=1, source_target_pairs={{0,4},{1,5},{16,20},{17,21},{32,36},{33,37},{48,52},{49,53},{2,6},... | collective-permute-start | bytes 663560 | tf_op jit(solution)/shard_map/ppermute | solution.py:47
  15.7 15.2 %collective-permute-start.4 = (bf16[72,1536]{1,0:T(8,128)(2,1)S(1)}, bf16[72,1536]{1,0:T(8,128)(2,1)}, u32[]{:S(2)}, u32[]{:S(2)}) collective-permute-start(bf16[72,1536]{1,0:T(8,128)(2,1)S(1)} %get-tuple-element.52), channel_id=1, source_target_pairs={{0,12},{1,13},{16,28},{17,29},{32,44},{33,45},{48,60},{49,61},{2,1... | collective-permute-start | bytes 663560 | tf_op jit(solution)/shard_map/ppermute | solution.py:47
  30.8 9.7 %collective-permute-start.9 = (bf16[72,1536]{1,0:T(8,128)(2,1)S(1)}, bf16[72,1536]{1,0:T(8,128)(2,1)S(1)}, u32[]{:S(2)}, u32[]{:S(2)}) collective-permute-start(bf16[72,1536]{1,0:T(8,128)(2,1)S(1)} %get-tuple-element.61), channel_id=1, source_target_pairs={{0,8},{1,9},{16,24},{17,25},{32,40},{33,41},{48,56},{49,57},{2,10}... | collective-permute-start | bytes 663560 | tf_op jit(solution)/shard_map/ppermute | solution.py:47
  30.9 11.2 %collective-permute-start.10 = (bf16[72,1536]{1,0:T(8,128)(2,1)S(1)}, bf16[72,1536]{1,0:T(8,128)(2,1)S(1)}, u32[]{:S(2)}, u32[]{:S(2)}) collective-permute-start(bf16[72,1536]{1,0:T(8,128)(2,1)S(1)} %get-tuple-element.62), channel_id=1, source_target_pairs={{0,4},{1,5},{16,20},{17,21},{32,36},{33,37},{48,52},{49,53},{2,6},... | collective-permute-start | bytes 663560 | tf_op jit(solution)/shard_map/ppermute | solution.py:47
  31.8 10.4 %collective-permute-start.11 = (bf16[72,1536]{1,0:T(8,128)(2,1)S(1)}, bf16[72,1536]{1,0:T(8,128)(2,1)S(1)}, u32[]{:S(2)}, u32[]{:S(2)}) collective-permute-start(bf16[72,1536]{1,0:T(8,128)(2,1)S(1)} %get-tuple-element.63), channel_id=1, source_target_pairs={{0,12},{1,13},{16,28},{17,29},{32,44},{33,45},{48,60},{49,61},{2,1... | collective-permute-start | bytes 663560 | tf_op jit(solution)/shard_map/ppermute | solution.py:47
  35.5 13.7 %collective-permute-start.12 = (bf16[72,1536]{1,0:T(8,128)(2,1)S(1)}, bf16[72,1536]{1,0:T(8,128)(2,1)S(1)}, u32[]{:S(2)}, u32[]{:S(2)}) collective-permute-start(bf16[72,1536]{1,0:T(8,128)(2,1)S(1)} %add_convert_fusion), channel_id=1, source_target_pairs={{0,2},{1,3},{16,18},{17,19},{32,34},{33,35},{48,50},{49,51},{2,0},... | collective-permute-start | bytes 663560 | tf_op jit(solution)/shard_map/ppermute | solution.py:47
  49.4 11.2 %collective-permute-start.13 = (bf16[72,1536]{1,0:T(8,128)(2,1)S(1)}, bf16[72,1536]{1,0:T(8,128)(2,1)S(1)}, u32[]{:S(2)}, u32[]{:S(2)}) collective-permute-start(bf16[72,1536]{1,0:T(8,128)(2,1)S(1)} %get-tuple-element.97), channel_id=1, source_target_pairs={{0,2},{1,3},{16,18},{17,19},{32,34},{33,35},{48,50},{49,51},{2,0},... | collective-permute-start | bytes 663560 | tf_op jit(solution)/shard_map/ppermute | solution.py:47
  60.7 7.5 %collective-permute-start.18 = (bf16[72,1536]{1,0:T(8,128)(2,1)S(1)}, bf16[72,1536]{1,0:T(8,128)(2,1)S(1)}, u32[]{:S(2)}, u32[]{:S(2)}) collective-permute-start(bf16[72,1536]{1,0:T(8,128)(2,1)S(1)} %get-tuple-element.103), channel_id=1, source_target_pairs={{0,8},{16,24},{32,40},{48,56},{2,10},{18,26},{34,42},{50,58},{4,12... | collective-permute-start | bytes 663560 | tf_op jit(solution)/shard_map/ppermute | solution.py:47
  63.0 7.7 %collective-permute-start.19 = (bf16[72,1536]{1,0:T(8,128)(2,1)S(1)}, bf16[72,1536]{1,0:T(8,128)(2,1)S(1)}, u32[]{:S(2)}, u32[]{:S(2)}) collective-permute-start(bf16[72,1536]{1,0:T(8,128)(2,1)S(1)} %get-tuple-element.104), channel_id=1, source_target_pairs={{0,8},{16,24},{32,40},{48,56},{2,10},{18,26},{34,42},{50,58},{4,12... | collective-permute-start | bytes 663560 | tf_op jit(solution)/shard_map/ppermute | solution.py:47
  64.3 11.0 %collective-permute-start.15 = (bf16[2,72,1536]{2,1,0:T(8,128)(2,1)S(1)}, bf16[2,72,1536]{2,1,0:T(8,128)(2,1)S(1)}, u32[]{:S(2)}, u32[]{:S(2)}) collective-permute-start(bf16[2,72,1536]{2,1,0:T(8,128)(2,1)S(1)} %pad_maximum_fusion.2), channel_id=1, source_target_pairs={{0,4},{16,20},{32,36},{48,52},{2,6},{18,22},{34,38},{50,54},{4,8},... | collective-permute-start | bytes 1327112 | tf_op jit(solution)/shard_map/ppermute | solution.py:47
  64.9 15.6 %collective-permute-start.17 = (bf16[2,72,1536]{2,1,0:T(8,128)(2,1)S(1)}, bf16[2,72,1536]{2,1,0:T(8,128)(2,1)S(1)}, u32[]{:S(2)}, u32[]{:S(2)}) collective-permute-start(bf16[2,72,1536]{2,1,0:T(8,128)(2,1)S(1)} %pad_maximum_fusion.2), channel_id=1, source_target_pairs={{0,12},{16,28},{32,44},{48,60},{2,14},{18,30},{34,46},{50,62},{4,0... | collective-permute-start | bytes 1327112 | tf_op jit(solution)/shard_map/ppermute | solution.py:47
  75.4 18.9 %collective-permute-start.16 = (bf16[2,144,1536]{2,1,0:T(8,128)(2,1)S(1)}, bf16[2,144,1536]{2,1,0:T(8,128)(2,1)S(1)}, u32[]{:S(2)}, u32[]{:S(2)}) collective-permute-start(bf16[2,144,1536]{2,1,0:T(8,128)(2,1)S(1)} %pad_maximum_fusion.refs_0_.refs_4_), channel_id=1, source_target_pairs={{0,16},{16,32},{32,48},{48,2},{2,18},{18,34},{34,50},{50,0},{4,20}... | collective-permute-start | bytes 2654216 | tf_op jit(solution)/shard_map/ppermute | solution.py:47
  80.6 13.8 %collective-permute-start.21 = (bf16[2,144,1536]{2,1,0:T(8,128)(2,1)S(1)}, bf16[2,144,1536]{2,1,0:T(8,128)(2,1)}, u32[]{:S(2)}, u32[]{:S(2)}) collective-permute-start(bf16[2,144,1536]{2,1,0:T(8,128)(2,1)S(1)} %pad_maximum_fusion.1.refs_1_.refs_5_), channel_id=1, source_target_pairs={{0,50},{16,0},{32,16},{48,32},{2,48},{18,2},{34,18},{50,34},{4,54}... | collective-permute-start | bytes 2654216 | tf_op jit(solution)/shard_map/ppermute | solution.py:47
  83.5 14.0 %collective-permute-start.25 = (bf16[2,144,1536]{2,1,0:T(8,128)(2,1)S(1)}, bf16[2,144,1536]{2,1,0:T(8,128)(2,1)}, u32[]{:S(2)}, u32[]{:S(2)}) collective-permute-start(bf16[2,144,1536]{2,1,0:T(8,128)(2,1)S(1)} %pad_maximum_fusion.refs_0_.refs_4_), channel_id=1, source_target_pairs={{0,1},{1,0},{16,17},{17,16},{32,33},{33,32},{48,49},{49,48},{2,3},... | collective-permute-start | bytes 2654216 | tf_op jit(solution)/shard_map/ppermute | solution.py:47
  83.5 14.4 %collective-permute-start.26 = (bf16[2,144,1536]{2,1,0:T(8,128)(2,1)S(1)}, bf16[2,144,1536]{2,1,0:T(8,128)(2,1)}, u32[]{:S(2)}, u32[]{:S(2)}) collective-permute-start(bf16[2,144,1536]{2,1,0:T(8,128)(2,1)S(1)} %pad_maximum_fusion.1.refs_1_.refs_5_), channel_id=1, source_target_pairs={{0,1},{1,0},{16,17},{17,16},{32,33},{33,32},{48,49},{49,48},{2,3},... | collective-permute-start | bytes 2654216 | tf_op jit(solution)/shard_map/ppermute | solution.py:47
  94.3 23.7 %collective-permute-start.27 = (bf16[2,144,1536]{2,1,0:T(8,128)(2,1)S(1)}, bf16[2,144,1536]{2,1,0:T(8,128)(2,1)S(1)}, u32[]{:S(2)}, u32[]{:S(2)}) collective-permute-start(bf16[2,144,1536]{2,1,0:T(8,128)(2,1)S(1)} %collective-permute-done.16.refs_2_.refs_6_), channel_id=1, source_target_pairs={{0,1},{1,0},{16,17},{17,16},{32,33},{33,32},{48,49},{49,48},{2,3},... | collective-permute-start | bytes 2654216 | tf_op jit(solution)/shard_map/ppermute | solution.py:47
  94.3 24.3 %collective-permute-start.23 = (bf16[2,144,1536]{2,1,0:T(8,128)(2,1)S(1)}, bf16[2,144,1536]{2,1,0:T(8,128)(2,1)S(1)}, u32[]{:S(2)}, u32[]{:S(2)}) collective-permute-start(bf16[2,144,1536]{2,1,0:T(8,128)(2,1)S(1)} %collective-permute-done.16.refs_2_.refs_6_), channel_id=1, source_target_pairs={{0,16},{16,32},{32,48},{48,2},{2,18},{18,34},{34,50},{50,0},{4,20}... | collective-permute-start | bytes 2654216 | tf_op jit(solution)/shard_map/ppermute | solution.py:47
  94.4 23.6 %collective-permute-start.20 = (bf16[2,144,1536]{2,1,0:T(8,128)(2,1)S(1)}, bf16[2,144,1536]{2,1,0:T(8,128)(2,1)S(1)}, u32[]{:S(2)}, u32[]{:S(2)}) collective-permute-start(bf16[2,144,1536]{2,1,0:T(8,128)(2,1)S(1)} %pad_maximum_fusion.1.refs_1_.refs_5_), channel_id=1, source_target_pairs={{0,16},{16,32},{32,48},{48,2},{2,18},{18,34},{34,50},{50,0},{4,20}... | collective-permute-start | bytes 2654216 | tf_op jit(solution)/shard_map/ppermute | solution.py:47
  97.4 21.2 %collective-permute-start.22 = (bf16[2,144,1536]{2,1,0:T(8,128)(2,1)S(1)}, bf16[2,144,1536]{2,1,0:T(8,128)(2,1)S(1)}, u32[]{:S(2)}, u32[]{:S(2)}) collective-permute-start(bf16[2,144,1536]{2,1,0:T(8,128)(2,1)S(1)} %pad_maximum_fusion.refs_0_.refs_4_), channel_id=1, source_target_pairs={{0,50},{16,0},{32,16},{48,32},{2,48},{18,2},{34,18},{50,34},{4,54}... | collective-permute-start | bytes 2654216 | tf_op jit(solution)/shard_map/ppermute | solution.py:47
  97.9 22.1 %collective-permute-start.24 = (bf16[2,144,1536]{2,1,0:T(8,128)(2,1)}, bf16[2,144,1536]{2,1,0:T(8,128)(2,1)S(1)}, u32[]{:S(2)}, u32[]{:S(2)}) collective-permute-start(bf16[2,144,1536]{2,1,0:T(8,128)(2,1)} %collective-permute-done.21.refs_5_.refs_9_), channel_id=1, source_target_pairs={{0,50},{16,0},{32,16},{48,32},{2,48},{18,2},{34,18},{50,34},{4,54}... | collective-permute-start | bytes 2654216 | tf_op jit(solution)/shard_map/ppermute | solution.py:47
  129.1 85.5 %collective-permute-start.35 = (bf16[64,576]{1,0:T(8,128)(2,1)S(1)}, bf16[64,576]{1,0:T(8,128)(2,1)S(1)}, u32[]{:S(2)}, u32[]{:S(2)}) collective-permute-start(bf16[64,576]{1,0:T(8,128)(2,1)S(1)} %get-tuple-element.88), channel_id=1, source_target_pairs={{128,192},{129,193},{144,208},{145,209},{160,224},{161,225},{176,2... | collective-permute-start | bytes 221192 | tf_op jit(solution)/shard_map/ppermute | solution.py:47
  239.1 7.9 %collective-permute-start.37 = (bf16[64,576]{1,0:T(8,128)(2,1)S(1)}, bf16[64,576]{1,0:T(8,128)(2,1)S(1)}, u32[]{:S(2)}, u32[]{:S(2)}) collective-permute-start(bf16[64,576]{1,0:T(8,128)(2,1)S(1)} %get-tuple-element.95), channel_id=1, source_target_pairs={{0,32},{1,33},{16,48},{17,49},{32,0},{33,1},{48,16},{49,17},{2,34}... | collective-permute-start | bytes 221192 | tf_op jit(solution)/shard_map/ppermute | solution.py:47
  (22 other events, 287.9 us)

commit v2 on v1

--- a/solution.py
+++ b/solution.py
@@ -78,11 +78,13 @@
     height, hidden = blocks[0].shape
     chunk = height // 8
     vmem, hbm = pl.BlockSpec(memory_space=pltpu.VMEM), pl.BlockSpec(memory_space=pltpu.HBM)
+    anywhere = pl.BlockSpec(memory_space=pl.ANY)
+    own = [pltpu.with_memory_space_constraint(block, pltpu.HBM) for block in blocks[:2]]
     return pl.pallas_call(
         pair_kernel,
         name="pair_sum",
         out_shape=(jax.ShapeDtypeStruct((chunk, hidden), BF16),) * 8,
-        in_specs=[pl.BlockSpec(memory_space=pltpu.SMEM)] + [hbm] * 4,
+        in_specs=[pl.BlockSpec(memory_space=pltpu.SMEM)] + [hbm] * 2 + [anywhere] * 2,
         out_specs=(vmem,) * 8,
         scratch_shapes=[
             pltpu.VMEM((8, chunk, hidden), BF16),
@@ -90,8 +92,15 @@
             pltpu.SemaphoreType.DMA((8,)),
             pltpu.SemaphoreType.DMA((8,)),
         ],
-        compiler_params=pltpu.CompilerParams(vmem_limit_bytes=48 << 20),
-    )(place, *[pltpu.with_memory_space_constraint(block, pltpu.HBM) for block in blocks])
+        compiler_params=pltpu.CompilerParams(vmem_limit_bytes=24 << 20),
+    )(place, *own, *blocks[2:])
+
+
+def pick(index, values):
+    value = values[0]
+    for at in range(1, len(values)):
+        value = jnp.where(index == at, values[at], value)
+    return value
 
 
 def relay_kernel(step, has_held, info, rows_ref, *refs):
@@ -104,7 +113,7 @@
     quarter = own[0].shape[1]
 
     def load(section):
-        place = info[8 + lax.rem(section - z_low + 4, 4)]
+        place = pick(lax.rem(section - z_low + 4, 4), PLACE)
 
         def copy(src, dst_v, side, sem):
             row = lax.rem(y + ORDER[side] + 4, 4) * quarter
@@ -190,6 +199,7 @@
 
 
 def relay(step, info, rows, held, own, crossed):
+    blocks = [pltpu.with_memory_space_constraint(block, pltpu.HBM) for block in own + crossed]
     vmem, hbm = pl.BlockSpec(memory_space=pltpu.VMEM), pl.BlockSpec(memory_space=pltpu.HBM)
     count, width = rows.shape
     height, hidden = 4 * own[0].shape[1], own[0].shape[2]
@@ -197,8 +207,8 @@
         functools.partial(relay_kernel, step, len(held) > 0),
         name="relay",
         out_shape=(jax.ShapeDtypeStruct((count, width), BF16),) * 5,
-        in_specs=[pl.BlockSpec(memory_space=pltpu.SMEM), vmem]
-        + [vmem] * len(held)
+        in_specs=[pl.BlockSpec(memory_space=pltpu.SMEM)]
+        + [vmem] * (1 + len(held))
         + [hbm] * (len(own) + len(crossed)),
         out_specs=(vmem,) * 5,
         scratch_shapes=[
@@ -209,8 +219,8 @@
             pltpu.SemaphoreType.DMA((4,)),
             pltpu.SemaphoreType.DMA((4,)),
         ],
-        compiler_params=pltpu.CompilerParams(vmem_limit_bytes=20 << 20),
-    )(info, rows, *held, *own, *crossed)
+        compiler_params=pltpu.CompilerParams(vmem_limit_bytes=24 << 20),
+    )(info, rows, *held, *blocks)
 
 
 def line_kernel(info, *refs):
@@ -248,35 +258,25 @@
     a_own, b_own = wa_local[0, 0], wb_local[0, 0].T
     a_got = send(a_own, core_swap((1,)))
     b_got = send(b_own, core_swap((0,)))
-    layers = [counts] + [
-        send(counts, route(lambda x, y, z, core, by=by: (x, y, z // 4 * 4 + (z + by) % 4, core)))
-        for by in (1, 2, 3)
-    ]
-    def y_sends(across, ahead, behind):
-        return send(across, y_step(2)), send(ahead, y_step(1)), send(behind, y_step(-1))
-
-    *away, away_mine, across, ahead, behind, mine = pair_sum(
-        jnp.stack([y, core, z_high]), a_own, b_own, a_got, b_got
-    )
-    away_gots = y_sends(*away)
-    info = jnp.concatenate(
-        [jnp.stack([x, z_low, y, core]), *layers, jnp.array(PLACE, jnp.int32)]
-    )
-    away_gots, kept_parts, info, wa_master, wb_master, wa_moment, wb_moment = (
-        lax.optimization_barrier(
-            (away_gots, (across, ahead, behind), info, wa_master, wb_master, wa_moment, wb_moment)
-        )
-    )
-    away_total = away_mine.astype(F32) + sum(got.astype(F32) for got in away_gots)
-    z_got = send(away_total.astype(BF16), z_step(4))
-    total = mine.astype(F32) + sum(got.astype(F32) for got in y_sends(*kept_parts))
-
     gain = 0.7 * 1.9
     a_state = (1.0 - gain) * wa_master[0] - (0.7 * 0.81) * wa_moment[0]
     b_state = ((1.0 - gain) * wb_master[0] - (0.7 * 0.81) * wb_moment[0]).T
     kept = jnp.where(first, a_state, b_state)
     state_got = send(jnp.where(first, b_state, a_state), core_swap())
     state = jnp.concatenate([jnp.where(first, kept, state_got), jnp.where(first, state_got, kept)])
+    a_got, b_got, state = lax.optimization_barrier((a_got, b_got, state))
+    def y_sends(across, ahead, behind):
+        return send(across, y_step(2)), send(ahead, y_step(1)), send(behind, y_step(-1))
+
+    *away, away_mine, across, ahead, behind, mine = pair_sum(
+        jnp.stack([y, core, z_high]), a_own, b_own, a_got, b_got
+    )
+    away_gots = y_sends(*away)
+    away_gots, kept_parts = lax.optimization_barrier((away_gots, (across, ahead, behind)))
+    away_total = away_mine.astype(F32) + sum(got.astype(F32) for got in away_gots)
+    z_got = send(away_total.astype(BF16), z_step(4))
+    total = mine.astype(F32) + sum(got.astype(F32) for got in y_sends(*kept_parts))
+
     updated = state + (gain / replicas) * (total + z_got.astype(F32))
     w = updated.astype(BF16)
     ours = jnp.where(first, updated[:owned], updated[owned:])
@@ -288,24 +288,28 @@
     def cross(by):
         return z_step(by, (0,)) + y_step(by, (1,))
 
-    w_far, theirs = lax.optimization_barrier((send(w, z_step(4)), theirs))
+    layers = [counts] + [
+        send(counts, route(lambda x, y, z, core, by=by: (x, y, z // 4 * 4 + (z + by) % 4, core)))
+        for by in (1, 2, 3)
+    ]
+    w_far, theirs, layers = lax.optimization_barrier((send(w, z_step(4)), theirs, layers))
     wa_next = with_layout_constraint(
         jnp.where(first, ours, theirs)[None], Layout((1, 0, 2))
     )
     wb_next = with_layout_constraint(
         jnp.where(first, theirs, ours).T[None], Layout((2, 0, 1))
     )
-    k_low, k_high = jnp.where(low, w, w_far), jnp.where(low, w_far, w)
-    k0 = jnp.stack([k_low, k_high])
+    k0 = jnp.where(low, jnp.stack([w, w_far]), jnp.stack([w_far, w]))
     k_behind, k_ahead = send(k0, turn(1)), send(k0, turn(-1))
-    k_across = jnp.stack([send(k_low, turn(2)), send(k_high, turn(-2))])
+    k_across = jnp.stack([send(k_behind[0], turn(1)), send(k_ahead[1], turn(-1))])
     shape = (2, 2 * chunk, hidden)
     near = jnp.stack([k0, k_behind]).reshape(shape)
     far = jnp.stack([k_ahead, k_across]).reshape(shape)
     rows_each = inputs.shape[0] // 4
     rows = lax.dynamic_slice_in_dim(inputs, z_low * rows_each, rows_each, 0)
-    near_behind, far_later, wa_next, wb_next, rows = lax.optimization_barrier(
-        (send(near, cross(1)), far, wa_next, wb_next, rows)
+    info = jnp.concatenate([jnp.stack([x, z_low, y, core]), *layers])
+    near_behind, far_later, wa_next, wb_next, rows, info = lax.optimization_barrier(
+        (send(near, cross(1)), far, wa_next, wb_next, rows, info)
     )
     far_ahead, near_later = lax.optimization_barrier((send(far, cross(-1)), near))
     near_across, far_behind = send(near_behind, cross(1)), send(far_later, cross(1))

time: 250 us -> 218 us (0.87)
  waiting for transfers between devices: 144 us -> 118 us
  Pallas kernels: 30.8 us -> 23.5 us
  starting transfers between devices: 63.6 us -> 60.8 us
    ppermute x39, waiting for transfers between devices: 144 us -> 118 us  [send(): return lax.ppermute(block, AXES, pairs)]
    pallas_call x4, Pallas kernels: 26.5 us -> 18.2 us  [relay(): pl.pallas_call(functools.partial(relay_kernel, step, len(held) > 0), name...]
    ppermute x39, starting transfers between devices: 63.6 us -> 60.8 us  [send(): return lax.ppermute(block, AXES, pairs)]
  transfers between devices with their start and end apart: 39 -> 39, of which waited for: 20 -> 21; matrix products, arithmetic and copies ran while one was open for 3% -> 5% of each run, Pallas kernels for 0% -> 0%
where the time goes in v2:
time: 218 us; the launch traced here: 216 us
  waiting for transfers between devices  118 us (54%)
  starting transfers between devices  60.8 us (28%)
  Pallas kernels  23.5 us (11%)
  local copies, waits for them, and re-layouts  7.08 us (3%)
  other arithmetic  4.54 us (2%)
    ppermute x39, waiting for transfers between devices, send(): return lax.ppermute(block, AXES, pairs)  118 us
    ppermute x39, starting transfers between devices, send(): return lax.ppermute(block, AXES, pairs)  60.8 us
    pallas_call x4, Pallas kernels, relay(): pl.pallas_call(functools.partial(relay_kernel, step, len(held) > 0), name...  18.2 us
  transfers between devices with their start and end apart: 39, of which 21 were waited for; matrix products, arithmetic and copies ran while one was open for 5% of the time, Pallas kernels for 0%

profile of v2, /device:TPU:6, one launch (start us, length us, event | category | flops | bytes accessed | tf_op | source)
XLA Modules:
  0.0 215.5 jit_solution(7667002243752403383)
XLA Ops:
  2.1 4.4 %collective-permute-start.1 = (bf16[576,1536]{1,0:T(8,128)(2,1)}, bf16[576,1536]{1,0:T(8,128)(2,1)}, u32[]{:S(2)}, u32[]{:S(2)}) collective-permute-start(bf16[576,1536]{1,0:T(8,128)(2,1)} %bitcast.52), channel_id=1, source_target_pairs={{0,1},{16,17},{32,33},{48,49},{2,3},{18,19},{34,35},{50,51},{4,5},... | collective-permute-start | bytes 5308424 | tf_op jit(solution)/shard_map/ppermute | solution.py:47
  10.9 3.8 %pair_sum.1 = (bf16[72,1536]{1,0:T(8,128)(2,1)S(1)}, bf16[72,1536]{1,0:T(8,128)(2,1)S(1)}, bf16[72,1536]{1,0:T(8,128)(2,1)S(1)}, bf16[72,1536]{1,0:T(8,128)(2,1)...) custom-call(s32[3]{0:T(128)S(1)} %pad_add_fusion.place, ...), custom_call_target="tpu_custom_call" | custom-call | tf_op jit(solution)/shard_map/pair_sum/pallas_call | solution.py:83
  14.7 3.3 %collective-permute-start.3 = (bf16[72,1536]{1,0:T(8,128)(2,1)S(1)}, bf16[72,1536]{1,0:T(8,128)(2,1)S(1)}, u32[]{:S(2)}, u32[]{:S(2)}) collective-permute-start(bf16[72,1536]{1,0:T(8,128)(2,1)S(1)} %get-tuple-element.57), channel_id=1, source_target_pairs={{0,8},{1,9},{16,24},{17,25},{32,40},{33,41},{48,56},{49,57},{2,10}... | collective-permute-start | bytes 663560 | tf_op jit(solution)/shard_map/ppermute | solution.py:47
  18.6 2.6 %collective-permute-start.5 = (bf16[72,1536]{1,0:T(8,128)(2,1)S(1)}, bf16[72,1536]{1,0:T(8,128)(2,1)S(1)}, u32[]{:S(2)}, u32[]{:S(2)}) collective-permute-start(bf16[72,1536]{1,0:T(8,128)(2,1)S(1)} %get-tuple-element.59), channel_id=1, source_target_pairs={{0,12},{1,13},{16,28},{17,29},{32,44},{33,45},{48,60},{49,61},{2,1... | collective-permute-start | bytes 663560 | tf_op jit(solution)/shard_map/ppermute | solution.py:47
  21.2 3.4 %collective-permute-done.3 = bf16[72,1536]{1,0:T(8,128)(2,1)S(1)} collective-permute-done((bf16[72,1536]{1,0:T(8,128)(2,1)S(1)}, bf16[72,1536]{1,0:T(8,128)(2,1)S(1)}, u32[]{:S(2)}, u32[]{:S(2)}) %collective-permute-start.3) | collective-permute-done | bytes 221216 | tf_op jit(solution)/shard_map/ppermute | solution.py:47
  24.6 2.9 %collective-permute-done.4 = bf16[72,1536]{1,0:T(8,128)(2,1)S(1)} collective-permute-done((bf16[72,1536]{1,0:T(8,128)(2,1)S(1)}, bf16[72,1536]{1,0:T(8,128)(2,1)S(1)}, u32[]{:S(2)}, u32[]{:S(2)}) %collective-permute-start.4) | collective-permute-done | bytes 221216 | tf_op jit(solution)/shard_map/ppermute | solution.py:47
  27.9 2.1 collective-permute-start.6
  33.3 7.3 %collective-permute-start.9 = (bf16[72,1536]{1,0:T(8,128)(2,1)S(1)}, bf16[72,1536]{1,0:T(8,128)(2,1)S(1)}, u32[]{:S(2)}, u32[]{:S(2)}) collective-permute-start(bf16[72,1536]{1,0:T(8,128)(2,1)S(1)} %add_convert_fusion), channel_id=1, source_target_pairs={{0,2},{1,3},{16,18},{17,19},{32,34},{33,35},{48,50},{49,51},{2,0},... | collective-permute-start | bytes 663560 | tf_op jit(solution)/shard_map/ppermute | solution.py:47
  40.6 7.5 %collective-permute-done.9 = bf16[72,1536]{1,0:T(8,128)(2,1)S(1)} collective-permute-done((bf16[72,1536]{1,0:T(8,128)(2,1)S(1)}, bf16[72,1536]{1,0:T(8,128)(2,1)S(1)}, u32[]{:S(2)}, u32[]{:S(2)}) %collective-permute-start.9) | collective-permute-done | bytes 221216 | tf_op jit(solution)/shard_map/ppermute | solution.py:47
  48.3 6.4 %collective-permute-start.10 = (bf16[72,1536]{1,0:T(8,128)(2,1)S(1)}, bf16[72,1536]{1,0:T(8,128)(2,1)S(1)}, u32[]{:S(2)}, u32[]{:S(2)}) collective-permute-start(bf16[72,1536]{1,0:T(8,128)(2,1)S(1)} %get-tuple-element.103), channel_id=1, source_target_pairs={{0,2},{1,3},{16,18},{17,19},{32,34},{33,35},{48,50},{49,51},{2,0},... | collective-permute-start | bytes 663560 | tf_op jit(solution)/shard_map/ppermute | solution.py:47
  56.6 3.7 %collective-permute-start.14 = (s32[1]{0:T(128)}, s32[1]{0:T(128)}, u32[]{:S(2)}, u32[]{:S(2)}) collective-permute-start(s32[1]{0:T(128)} %param.14), channel_id=1, source_target_pairs={{0,48},{1,49},{16,0},{17,1},{32,16},{33,17},{48,32},{49,33},{2,50}... | collective-permute-start | bytes 20 | tf_op jit(solution)/shard_map/ppermute | solution.py:47
  63.2 2.0 collective-permute-start.17
  65.3 6.2 %collective-permute-done.17 = bf16[2,72,1536]{2,1,0:T(8,128)(2,1)S(1)} collective-permute-done((bf16[2,72,1536]{2,1,0:T(8,128)(2,1)S(1)}, bf16[2,72,1536]{2,1,0:T(8,128)(2,1)S(1)}, u32[]{:S(2)}, u32[]{:S(2)}) %collective-permute-start.17) | collective-permute-done | bytes 442400 | tf_op jit(solution)/shard_map/ppermute | solution.py:47
  71.5 3.4 %collective-permute-start.19 = (bf16[72,1536]{1,0:T(8,128)(2,1)S(1)}, bf16[72,1536]{1,0:T(8,128)(2,1)S(1)}, u32[]{:S(2)}, u32[]{:S(2)}) collective-permute-start(bf16[72,1536]{1,0:T(8,128)(2,1)S(1)} %slice_bitcast_fusion), channel_id=1, source_target_pairs={{0,12},{16,28},{32,44},{48,60},{2,14},{18,30},{34,46},{50,62},{4,0... | collective-permute-start | bytes 663560 | tf_op jit(solution)/shard_map/ppermute | solution.py:47
  78.4 6.2 %collective-permute-done.18 = bf16[72,1536]{1,0:T(8,128)(2,1)S(1)} collective-permute-done((bf16[72,1536]{1,0:T(8,128)(2,1)S(1)}, bf16[72,1536]{1,0:T(8,128)(2,1)S(1)}, u32[]{:S(2)}, u32[]{:S(2)}) %collective-permute-start.18) | collective-permute-done | bytes 221216 | tf_op jit(solution)/shard_map/ppermute | solution.py:47
  91.7 1.9 concatenate.11.info
  94.8 3.3 %collective-permute-done.21.refs_5_.refs_9_ = bf16[2,144,1536]{2,1,0:T(8,128)(2,1)} collective-permute-done((bf16[2,144,1536]{2,1,0:T(8,128)(2,1)S(1)}, bf16[2,144,1536]{2,1,0:T(8,128)(2,1)}, u32[]{:S(2)}, u32[]{:S(2)}) %collective-permute-start.21) | collective-permute-done | bytes 884768 | tf_op jit(solution)/shard_map/ppermute | solution.py:47
  99.5 1.8 collective-permute-start.22
  102.5 15.1 %collective-permute-done.20.refs_3_.refs_7_ = bf16[2,144,1536]{2,1,0:T(8,128)(2,1)S(1)} collective-permute-done((bf16[2,144,1536]{2,1,0:T(8,128)(2,1)S(1)}, bf16[2,144,1536]{2,1,0:T(8,128)(2,1)S(1)}, u32[]{:S(2)}, u32[]{:S(2)}) %collective-permute-start.20) | collective-permute-done | bytes 884768 | tf_op jit(solution)/shard_map/ppermute | solution.py:47
  118.6 3.4 %collective-permute-done.24.refs_7_.refs_11_ = bf16[2,144,1536]{2,1,0:T(8,128)(2,1)S(1)} collective-permute-done((bf16[2,144,1536]{2,1,0:T(8,128)(2,1)}, bf16[2,144,1536]{2,1,0:T(8,128)(2,1)S(1)}, u32[]{:S(2)}, u32[]{:S(2)}) %collective-permute-start.24) | collective-permute-done | bytes 884768 | tf_op jit(solution)/shard_map/ppermute | solution.py:47
  131.0 56.5 %collective-permute-done.35.rows_ref = bf16[64,576]{1,0:T(8,128)(2,1)S(1)} collective-permute-done((bf16[64,576]{1,0:T(8,128)(2,1)S(1)}, bf16[64,576]{1,0:T(8,128)(2,1)S(1)}, u32[]{:S(2)}, u32[]{:S(2)}) %collective-permute-start.35) | collective-permute-done | bytes 73760 | tf_op jit(solution)/shard_map/ppermute | solution.py:47
  187.4 16.1 %relay.7 = (bf16[64,576]{1,0:T(8,128)(2,1)S(1)}, bf16[64,576]{1,0:T(8,128)(2,1)S(1)}, bf16[64,576]{1,0:T(8,128)(2,1)S(1)}, bf16[64,576]{1,0:T(8,128)(2,1)S(1)}, bf16[64,576]{1,0:T(8,128)(2,1)}) custom-call(s32[8]{0:T(128)S(1)} %concatenate.11.info, bf16[64,576]{1,0:T(8,128)(2,1)S(1)} %collective-permute-done.35.rows_ref, ...), custom_call_target="tpu_custom_call" | custom-call | tf_op jit(solution)/shard_map/relay/pallas_call | solution.py:206
  205.2 3.8 %collective-permute-start.37 = (bf16[64,576]{1,0:T(8,128)(2,1)S(1)}, bf16[64,576]{1,0:T(8,128)(2,1)S(1)}, u32[]{:S(2)}, u32[]{:S(2)}) collective-permute-start(bf16[64,576]{1,0:T(8,128)(2,1)S(1)} %get-tuple-element.101), channel_id=1, source_target_pairs={{0,32},{1,33},{16,48},{17,49},{32,0},{33,1},{48,16},{49,17},{2,34}... | collective-permute-start | bytes 221192 | tf_op jit(solution)/shard_map/ppermute | solution.py:47
  211.1 2.5 %collective-permute-done.37.refs_2_ = bf16[64,576]{1,0:T(8,128)(2,1)S(1)} collective-permute-done((bf16[64,576]{1,0:T(8,128)(2,1)S(1)}, bf16[64,576]{1,0:T(8,128)(2,1)S(1)}, u32[]{:S(2)}, u32[]{:S(2)}) %collective-permute-start.37) | collective-permute-done | bytes 73760 | tf_op jit(solution)/shard_map/ppermute | solution.py:47
  (110 shorter events, 44.3 us)
Async XLA Ops:
  0.6 10.2 %collective-permute-start = (bf16[576,1536]{1,0:T(8,128)(2,1)}, bf16[576,1536]{1,0:T(8,128)(2,1)S(1)}, u32[]{:S(2)}, u32[]{:S(2)}) collective-permute-start(bf16[576,1536]{1,0:T(8,128)(2,1)} %bitcast.50), channel_id=1, source_target_pairs={{1,0},{17,16},{33,32},{49,48},{3,2},{19,18},{35,34},{51,50},{5,4},... | collective-permute-start | bytes 5308424 | tf_op jit(solution)/shard_map/ppermute | solution.py:47
  2.1 8.8 %collective-permute-start.1 = (bf16[576,1536]{1,0:T(8,128)(2,1)}, bf16[576,1536]{1,0:T(8,128)(2,1)}, u32[]{:S(2)}, u32[]{:S(2)}) collective-permute-start(bf16[576,1536]{1,0:T(8,128)(2,1)} %bitcast.52), channel_id=1, source_target_pairs={{0,1},{16,17},{32,33},{48,49},{2,3},{18,19},{34,35},{50,51},{4,5},... | collective-permute-start | bytes 5308424 | tf_op jit(solution)/shard_map/ppermute | solution.py:47
  14.7 10.0 %collective-permute-start.3 = (bf16[72,1536]{1,0:T(8,128)(2,1)S(1)}, bf16[72,1536]{1,0:T(8,128)(2,1)S(1)}, u32[]{:S(2)}, u32[]{:S(2)}) collective-permute-start(bf16[72,1536]{1,0:T(8,128)(2,1)S(1)} %get-tuple-element.57), channel_id=1, source_target_pairs={{0,8},{1,9},{16,24},{17,25},{32,40},{33,41},{48,56},{49,57},{2,10}... | collective-permute-start | bytes 663560 | tf_op jit(solution)/shard_map/ppermute | solution.py:47
  18.0 9.6 %collective-permute-start.4 = (bf16[72,1536]{1,0:T(8,128)(2,1)S(1)}, bf16[72,1536]{1,0:T(8,128)(2,1)S(1)}, u32[]{:S(2)}, u32[]{:S(2)}) collective-permute-start(bf16[72,1536]{1,0:T(8,128)(2,1)S(1)} %get-tuple-element.58), channel_id=1, source_target_pairs={{0,4},{1,5},{16,20},{17,21},{32,36},{33,37},{48,52},{49,53},{2,6},... | collective-permute-start | bytes 663560 | tf_op jit(solution)/shard_map/ppermute | solution.py:47
  18.6 9.2 %collective-permute-start.5 = (bf16[72,1536]{1,0:T(8,128)(2,1)S(1)}, bf16[72,1536]{1,0:T(8,128)(2,1)S(1)}, u32[]{:S(2)}, u32[]{:S(2)}) collective-permute-start(bf16[72,1536]{1,0:T(8,128)(2,1)S(1)} %get-tuple-element.59), channel_id=1, source_target_pairs={{0,12},{1,13},{16,28},{17,29},{32,44},{33,45},{48,60},{49,61},{2,1... | collective-permute-start | bytes 663560 | tf_op jit(solution)/shard_map/ppermute | solution.py:47
  27.9 12.7 %collective-permute-start.6 = (bf16[72,1536]{1,0:T(8,128)(2,1)S(1)}, bf16[72,1536]{1,0:T(8,128)(2,1)S(1)}, u32[]{:S(2)}, u32[]{:S(2)}) collective-permute-start(bf16[72,1536]{1,0:T(8,128)(2,1)S(1)} %get-tuple-element.63), channel_id=1, source_target_pairs={{0,8},{1,9},{16,24},{17,25},{32,40},{33,41},{48,56},{49,57},{2,10}... | collective-permute-start | bytes 663560 | tf_op jit(solution)/shard_map/ppermute | solution.py:47
  29.9 10.6 %collective-permute-start.7 = (bf16[72,1536]{1,0:T(8,128)(2,1)S(1)}, bf16[72,1536]{1,0:T(8,128)(2,1)S(1)}, u32[]{:S(2)}, u32[]{:S(2)}) collective-permute-start(bf16[72,1536]{1,0:T(8,128)(2,1)S(1)} %get-tuple-element.64), channel_id=1, source_target_pairs={{0,4},{1,5},{16,20},{17,21},{32,36},{33,37},{48,52},{49,53},{2,6},... | collective-permute-start | bytes 663560 | tf_op jit(solution)/shard_map/ppermute | solution.py:47
  31.4 9.2 %collective-permute-start.8 = (bf16[72,1536]{1,0:T(8,128)(2,1)S(1)}, bf16[72,1536]{1,0:T(8,128)(2,1)S(1)}, u32[]{:S(2)}, u32[]{:S(2)}) collective-permute-start(bf16[72,1536]{1,0:T(8,128)(2,1)S(1)} %get-tuple-element.65), channel_id=1, source_target_pairs={{0,12},{1,13},{16,28},{17,29},{32,44},{33,45},{48,60},{49,61},{2,1... | collective-permute-start | bytes 663560 | tf_op jit(solution)/shard_map/ppermute | solution.py:47
  33.3 14.8 %collective-permute-start.9 = (bf16[72,1536]{1,0:T(8,128)(2,1)S(1)}, bf16[72,1536]{1,0:T(8,128)(2,1)S(1)}, u32[]{:S(2)}, u32[]{:S(2)}) collective-permute-start(bf16[72,1536]{1,0:T(8,128)(2,1)S(1)} %add_convert_fusion), channel_id=1, source_target_pairs={{0,2},{1,3},{16,18},{17,19},{32,34},{33,35},{48,50},{49,51},{2,0},... | collective-permute-start | bytes 663560 | tf_op jit(solution)/shard_map/ppermute | solution.py:47
  48.3 14.2 %collective-permute-start.10 = (bf16[72,1536]{1,0:T(8,128)(2,1)S(1)}, bf16[72,1536]{1,0:T(8,128)(2,1)S(1)}, u32[]{:S(2)}, u32[]{:S(2)}) collective-permute-start(bf16[72,1536]{1,0:T(8,128)(2,1)S(1)} %get-tuple-element.103), channel_id=1, source_target_pairs={{0,2},{1,3},{16,18},{17,19},{32,34},{33,35},{48,50},{49,51},{2,0},... | collective-permute-start | bytes 663560 | tf_op jit(solution)/shard_map/ppermute | solution.py:47
  63.2 8.3 %collective-permute-start.17 = (bf16[2,72,1536]{2,1,0:T(8,128)(2,1)S(1)}, bf16[2,72,1536]{2,1,0:T(8,128)(2,1)S(1)}, u32[]{:S(2)}, u32[]{:S(2)}) collective-permute-start(bf16[2,72,1536]{2,1,0:T(8,128)(2,1)S(1)} %maximum_select_fusion.1), channel_id=1, source_target_pairs={{0,12},{16,28},{32,44},{48,60},{2,14},{18,30},{34,46},{50,62},{4,0... | collective-permute-start | bytes 1327112 | tf_op jit(solution)/shard_map/ppermute | solution.py:47
  65.2 9.8 %collective-permute-start.15 = (bf16[2,72,1536]{2,1,0:T(8,128)(2,1)S(1)}, bf16[2,72,1536]{2,1,0:T(8,128)(2,1)S(1)}, u32[]{:S(2)}, u32[]{:S(2)}) collective-permute-start(bf16[2,72,1536]{2,1,0:T(8,128)(2,1)S(1)} %maximum_select_fusion.1), channel_id=1, source_target_pairs={{0,4},{16,20},{32,36},{48,52},{2,6},{18,22},{34,38},{50,54},{4,8},... | collective-permute-start | bytes 1327112 | tf_op jit(solution)/shard_map/ppermute | solution.py:47
  75.0 9.7 %collective-permute-start.18 = (bf16[72,1536]{1,0:T(8,128)(2,1)S(1)}, bf16[72,1536]{1,0:T(8,128)(2,1)S(1)}, u32[]{:S(2)}, u32[]{:S(2)}) collective-permute-start(bf16[72,1536]{1,0:T(8,128)(2,1)S(1)} %slice_bitcast_fusion.1), channel_id=1, source_target_pairs={{0,4},{16,20},{32,36},{48,52},{2,6},{18,22},{34,38},{50,54},{4,8},... | collective-permute-start | bytes 663560 | tf_op jit(solution)/shard_map/ppermute | solution.py:47
  75.2 18.4 %collective-permute-start.16 = (bf16[2,144,1536]{2,1,0:T(8,128)(2,1)S(1)}, bf16[2,144,1536]{2,1,0:T(8,128)(2,1)S(1)}, u32[]{:S(2)}, u32[]{:S(2)}) collective-permute-start(bf16[2,144,1536]{2,1,0:T(8,128)(2,1)S(1)} %pad_maximum_fusion.refs_0_.refs_4_), channel_id=1, source_target_pairs={{0,16},{16,32},{32,48},{48,2},{2,18},{18,34},{34,50},{50,0},{4,20}... | collective-permute-start | bytes 2654216 | tf_op jit(solution)/shard_map/ppermute | solution.py:47
  84.8 13.2 %collective-permute-start.21 = (bf16[2,144,1536]{2,1,0:T(8,128)(2,1)S(1)}, bf16[2,144,1536]{2,1,0:T(8,128)(2,1)}, u32[]{:S(2)}, u32[]{:S(2)}) collective-permute-start(bf16[2,144,1536]{2,1,0:T(8,128)(2,1)S(1)} %pad_maximum_fusion.1.refs_1_.refs_5_), channel_id=1, source_target_pairs={{0,50},{16,0},{32,16},{48,32},{2,48},{18,2},{34,18},{50,34},{4,54}... | collective-permute-start | bytes 2654216 | tf_op jit(solution)/shard_map/ppermute | solution.py:47
  86.0 13.5 %collective-permute-start.25 = (bf16[2,144,1536]{2,1,0:T(8,128)(2,1)S(1)}, bf16[2,144,1536]{2,1,0:T(8,128)(2,1)}, u32[]{:S(2)}, u32[]{:S(2)}) collective-permute-start(bf16[2,144,1536]{2,1,0:T(8,128)(2,1)S(1)} %pad_maximum_fusion.refs_0_.refs_4_), channel_id=1, source_target_pairs={{0,1},{1,0},{16,17},{17,16},{32,33},{33,32},{48,49},{49,48},{2,3},... | collective-permute-start | bytes 2654216 | tf_op jit(solution)/shard_map/ppermute | solution.py:47
  86.0 15.3 %collective-permute-start.26 = (bf16[2,144,1536]{2,1,0:T(8,128)(2,1)S(1)}, bf16[2,144,1536]{2,1,0:T(8,128)(2,1)}, u32[]{:S(2)}, u32[]{:S(2)}) collective-permute-start(bf16[2,144,1536]{2,1,0:T(8,128)(2,1)S(1)} %pad_maximum_fusion.1.refs_1_.refs_5_), channel_id=1, source_target_pairs={{0,1},{1,0},{16,17},{17,16},{32,33},{33,32},{48,49},{49,48},{2,3},... | collective-permute-start | bytes 2654216 | tf_op jit(solution)/shard_map/ppermute | solution.py:47
  93.6 23.9 %collective-permute-start.27 = (bf16[2,144,1536]{2,1,0:T(8,128)(2,1)S(1)}, bf16[2,144,1536]{2,1,0:T(8,128)(2,1)S(1)}, u32[]{:S(2)}, u32[]{:S(2)}) collective-permute-start(bf16[2,144,1536]{2,1,0:T(8,128)(2,1)S(1)} %collective-permute-done.16.refs_2_.refs_6_), channel_id=1, source_target_pairs={{0,1},{1,0},{16,17},{17,16},{32,33},{33,32},{48,49},{49,48},{2,3},... | collective-permute-start | bytes 2654216 | tf_op jit(solution)/shard_map/ppermute | solution.py:47
  93.7 24.4 %collective-permute-start.23 = (bf16[2,144,1536]{2,1,0:T(8,128)(2,1)S(1)}, bf16[2,144,1536]{2,1,0:T(8,128)(2,1)S(1)}, u32[]{:S(2)}, u32[]{:S(2)}) collective-permute-start(bf16[2,144,1536]{2,1,0:T(8,128)(2,1)S(1)} %collective-permute-done.16.refs_2_.refs_6_), channel_id=1, source_target_pairs={{0,16},{16,32},{32,48},{48,2},{2,18},{18,34},{34,50},{50,0},{4,20}... | collective-permute-start | bytes 2654216 | tf_op jit(solution)/shard_map/ppermute | solution.py:47
  98.0 19.5 %collective-permute-start.20 = (bf16[2,144,1536]{2,1,0:T(8,128)(2,1)S(1)}, bf16[2,144,1536]{2,1,0:T(8,128)(2,1)S(1)}, u32[]{:S(2)}, u32[]{:S(2)}) collective-permute-start(bf16[2,144,1536]{2,1,0:T(8,128)(2,1)S(1)} %pad_maximum_fusion.1.refs_1_.refs_5_), channel_id=1, source_target_pairs={{0,16},{16,32},{32,48},{48,2},{2,18},{18,34},{34,50},{50,0},{4,20}... | collective-permute-start | bytes 2654216 | tf_op jit(solution)/shard_map/ppermute | solution.py:47
  99.5 18.8 %collective-permute-start.22 = (bf16[2,144,1536]{2,1,0:T(8,128)(2,1)S(1)}, bf16[2,144,1536]{2,1,0:T(8,128)(2,1)S(1)}, u32[]{:S(2)}, u32[]{:S(2)}) collective-permute-start(bf16[2,144,1536]{2,1,0:T(8,128)(2,1)S(1)} %pad_maximum_fusion.refs_0_.refs_4_), channel_id=1, source_target_pairs={{0,50},{16,0},{32,16},{48,32},{2,48},{18,2},{34,18},{50,34},{4,54}... | collective-permute-start | bytes 2654216 | tf_op jit(solution)/shard_map/ppermute | solution.py:47
  101.3 20.7 %collective-permute-start.24 = (bf16[2,144,1536]{2,1,0:T(8,128)(2,1)}, bf16[2,144,1536]{2,1,0:T(8,128)(2,1)S(1)}, u32[]{:S(2)}, u32[]{:S(2)}) collective-permute-start(bf16[2,144,1536]{2,1,0:T(8,128)(2,1)} %collective-permute-done.21.refs_5_.refs_9_), channel_id=1, source_target_pairs={{0,50},{16,0},{32,16},{48,32},{2,48},{18,2},{34,18},{50,34},{4,54}... | collective-permute-start | bytes 2654216 | tf_op jit(solution)/shard_map/ppermute | solution.py:47
  129.7 57.8 %collective-permute-start.35 = (bf16[64,576]{1,0:T(8,128)(2,1)S(1)}, bf16[64,576]{1,0:T(8,128)(2,1)S(1)}, u32[]{:S(2)}, u32[]{:S(2)}) collective-permute-start(bf16[64,576]{1,0:T(8,128)(2,1)S(1)} %get-tuple-element.94), channel_id=1, source_target_pairs={{128,192},{129,193},{144,208},{145,209},{160,224},{161,225},{176,2... | collective-permute-start | bytes 221192 | tf_op jit(solution)/shard_map/ppermute | solution.py:47
  205.2 8.4 %collective-permute-start.37 = (bf16[64,576]{1,0:T(8,128)(2,1)S(1)}, bf16[64,576]{1,0:T(8,128)(2,1)S(1)}, u32[]{:S(2)}, u32[]{:S(2)}) collective-permute-start(bf16[64,576]{1,0:T(8,128)(2,1)S(1)} %get-tuple-element.101), channel_id=1, source_target_pairs={{0,32},{1,33},{16,48},{17,49},{32,0},{33,1},{48,16},{49,17},{2,34}... | collective-permute-start | bytes 221192 | tf_op jit(solution)/shard_map/ppermute | solution.py:47
  (30 other events, 296.7 us)

commit v3 on v2

--- a/solution.py
+++ b/solution.py
@@ -105,12 +105,12 @@
 
 def relay_kernel(step, has_held, info, rows_ref, *refs):
     held, refs = (refs[:4], refs[4:]) if has_held else ((), refs)
-    own, crossed, outs = refs[:8], refs[8:16], refs[16:20]
-    last_ref, wa_v, wb_v, stream, done_v, sem_a, sem_b = refs[20:]
+    own, crossed, outs = refs[:12], refs[12:24], refs[24:28]
+    last_ref, wa_v, wb_v, stream, done_v, sem_a, sem_b = refs[28:]
     x, z_low, y, core = info[0], info[1], info[2], info[3]
     hidden = wa_v.shape[2]
     half = hidden // 2
-    quarter = own[0].shape[1]
+    quarter = own[0].shape[0]
 
     def load(section):
         place = pick(lax.rem(section - z_low + 4, 4), PLACE)
@@ -123,20 +123,19 @@
                 sem.at[section],
             ).start()
 
+        def piece(bufs, message, at):
+            here, middle, far = bufs[3 * message : 3 * message + 3]
+            return (here, middle.at[0], middle.at[1], far)[at]
+
         def fetch(a_bufs, b_bufs):
-            for message in range(4):
-
-                @pl.when(place == message)
-                def _(message=message):
+            for at in range(4):
+
+                @pl.when(place == at)
+                def _(at=at):
                     for side in range(4):
-                        copy(a_bufs[2 * message + side // 2].at[side % 2], wa_v, side, sem_a)
-
-            for part in range(2):
-
-                @pl.when(place // 2 == part)
-                def _(part=part):
+                        copy(piece(a_bufs, at, side), wa_v, side, sem_a)
                     for side in range(4):
-                        copy(b_bufs[2 * side + part].at[lax.rem(place, 2)], wb_v, side, sem_b)
+                        copy(piece(b_bufs, side, at), wb_v, side, sem_b)
 
         @pl.when(core == 0)
         def _():
@@ -202,7 +201,7 @@
     blocks = [pltpu.with_memory_space_constraint(block, pltpu.HBM) for block in own + crossed]
     vmem, hbm = pl.BlockSpec(memory_space=pltpu.VMEM), pl.BlockSpec(memory_space=pltpu.HBM)
     count, width = rows.shape
-    height, hidden = 4 * own[0].shape[1], own[0].shape[2]
+    height, hidden = 4 * own[0].shape[0], own[0].shape[1]
     return pl.pallas_call(
         functools.partial(relay_kernel, step, len(held) > 0),
         name="relay",
@@ -272,9 +271,11 @@
         jnp.stack([y, core, z_high]), a_own, b_own, a_got, b_got
     )
     away_gots = y_sends(*away)
-    away_gots, kept_parts = lax.optimization_barrier((away_gots, (across, ahead, behind)))
     away_total = away_mine.astype(F32) + sum(got.astype(F32) for got in away_gots)
-    z_got = send(away_total.astype(BF16), z_step(4))
+    away_total, kept_parts = lax.optimization_barrier(
+        (away_total.astype(BF16), (across, ahead, behind))
+    )
+    z_got = send(away_total, z_step(4))
     total = mine.astype(F32) + sum(got.astype(F32) for got in y_sends(*kept_parts))
 
     updated = state + (gain / replicas) * (total + z_got.astype(F32))
@@ -299,22 +300,28 @@
     wb_next = with_layout_constraint(
         jnp.where(first, theirs, ours).T[None], Layout((2, 0, 1))
     )
-    k0 = jnp.where(low, jnp.stack([w, w_far]), jnp.stack([w_far, w]))
+    flat = (2 * chunk, hidden)
+    k0 = jnp.where(low, jnp.stack([w, w_far]), jnp.stack([w_far, w])).reshape(flat)
     k_behind, k_ahead = send(k0, turn(1)), send(k0, turn(-1))
-    k_across = jnp.stack([send(k_behind[0], turn(1)), send(k_ahead[1], turn(-1))])
-    shape = (2, 2 * chunk, hidden)
-    near = jnp.stack([k0, k_behind]).reshape(shape)
-    far = jnp.stack([k_ahead, k_across]).reshape(shape)
+    k0_behind, k0_ahead = send(k0, cross(1)), send(k0, cross(-1))
+    far = jnp.concatenate([send(k_behind[:chunk], turn(1)), send(k_ahead[chunk:], turn(-1))])
+    middle = jnp.stack([k_behind, k_ahead])
+    info = jnp.concatenate([jnp.stack([x, z_low, y, core]), *layers])
     rows_each = inputs.shape[0] // 4
     rows = lax.dynamic_slice_in_dim(inputs, z_low * rows_each, rows_each, 0)
-    info = jnp.concatenate([jnp.stack([x, z_low, y, core]), *layers])
-    near_behind, far_later, wa_next, wb_next, rows, info = lax.optimization_barrier(
-        (send(near, cross(1)), far, wa_next, wb_next, rows, info)
-    )
-    far_ahead, near_later = lax.optimization_barrier((send(far, cross(-1)), near))
-    near_across, far_behind = send(near_behind, cross(1)), send(far_later, cross(1))
-    far_across, near_ahead = send(far_ahead, cross(-1)), send(near_later, cross(-1))
-    own = [near, far, near_behind, far_behind, near_ahead, far_ahead, near_across, far_across]
+    middle_behind, middle_ahead = send(middle, cross(1)), send(middle, cross(-1))
+    k0_across = send(k0_behind, cross(1))
+    far_behind, far_ahead = send(far, cross(1)), send(far, cross(-1))
+    early, middle_ahead = lax.optimization_barrier(
+        ([k0, middle, far, k0_behind, k0_ahead], middle_ahead)
+    )
+    k0, middle, far, k0_behind, k0_ahead = early
+    middle_across, far_across = send(middle_ahead, cross(-1)), send(far_behind, cross(1))
+    far_across, wa_next, wb_next, rows, info = lax.optimization_barrier(
+        (far_across, wa_next, wb_next, rows, info)
+    )
+    own = [k0, middle, far, k0_behind, middle_behind, far_behind]
+    own += [k0_ahead, middle_ahead, far_ahead, k0_across, middle_across, far_across]
     crossed = [send(block, core_swap()) for block in own]
 
     held = ()

time: 218 us -> 210 us (0.963); the launches traced: 216 us -> 212 us
  waiting for transfers between devices: 118 us -> 109 us
  starting transfers between devices: 60.8 us -> 67.3 us
  Pallas kernels: 23.5 us -> 19.6 us
    ppermute x39 -> x46, waiting for transfers between devices: 118 us -> 109 us  [send(): return lax.ppermute(block, AXES, pairs)]
    ppermute x39 -> x46, starting transfers between devices: 60.8 us -> 67.3 us  [send(): return lax.ppermute(block, AXES, pairs)]
    pallas_call x4, Pallas kernels: 18.2 us -> 14.4 us  [relay(): pl.pallas_call(functools.partial(relay_kernel, step, len(held) > 0), name...]
  transfers between devices with their start and end apart: 39 -> 46, of which waited for: 21 -> 21; matrix products, arithmetic and copies ran while one was open for 5% -> 5% of each run, Pallas kernels for 0% -> 0%
where the time goes in v3:
time: 210 us; the launch traced here: 212 us
  waiting for transfers between devices  109 us (52%)
  starting transfers between devices  67.3 us (32%)
  Pallas kernels  19.6 us (9%)
  local copies, waits for them, and re-layouts  9.17 us (4%)
  other arithmetic  4.57 us (2%)
    ppermute x46, waiting for transfers between devices, send(): return lax.ppermute(block, AXES, pairs)  109 us
    ppermute x46, starting transfers between devices, send(): return lax.ppermute(block, AXES, pairs)  67.3 us
    pallas_call x4, Pallas kernels, relay(): pl.pallas_call(functools.partial(relay_kernel, step, len(held) > 0), name...  14.4 us
  transfers between devices with their start and end apart: 46, of which 21 were waited for; matrix products, arithmetic and copies ran while one was open for 5% of the time, Pallas kernels for 0%

profile of v3, /device:TPU:6, one launch (start us, length us, event | category | flops | bytes accessed | tf_op | source)
XLA Modules:
  0.0 211.8 jit_solution(546583311860503369)
XLA Ops:
  2.1 4.4 %collective-permute-start.1 = (bf16[576,1536]{1,0:T(8,128)(2,1)}, bf16[576,1536]{1,0:T(8,128)(2,1)}, u32[]{:S(2)}, u32[]{:S(2)}) collective-permute-start(bf16[576,1536]{1,0:T(8,128)(2,1)} %bitcast.50), channel_id=1, source_target_pairs={{0,1},{16,17},{32,33},{48,49},{2,3},{18,19},{34,35},{50,51},{4,5},... | collective-permute-start | bytes 5308424 | tf_op jit(solution)/shard_map/ppermute | solution.py:47
  10.9 3.8 %pair_sum.1 = (bf16[72,1536]{1,0:T(8,128)(2,1)S(1)}, bf16[72,1536]{1,0:T(8,128)(2,1)S(1)}, bf16[72,1536]{1,0:T(8,128)(2,1)S(1)}, bf16[72,1536]{1,0:T(8,128)(2,1)...) custom-call(s32[3]{0:T(128)S(1)} %pad_add_fusion.place, ...), custom_call_target="tpu_custom_call" | custom-call | tf_op jit(solution)/shard_map/pair_sum/pallas_call | solution.py:83
  14.7 3.3 %collective-permute-start.3 = (bf16[72,1536]{1,0:T(8,128)(2,1)S(1)}, bf16[72,1536]{1,0:T(8,128)(2,1)S(1)}, u32[]{:S(2)}, u32[]{:S(2)}) collective-permute-start(bf16[72,1536]{1,0:T(8,128)(2,1)S(1)} %get-tuple-element.59), channel_id=1, source_target_pairs={{0,8},{1,9},{16,24},{17,25},{32,40},{33,41},{48,56},{49,57},{2,10}... | collective-permute-start | bytes 663560 | tf_op jit(solution)/shard_map/ppermute | solution.py:47
  18.6 2.6 %collective-permute-start.5 = (bf16[72,1536]{1,0:T(8,128)(2,1)S(1)}, bf16[72,1536]{1,0:T(8,128)(2,1)S(1)}, u32[]{:S(2)}, u32[]{:S(2)}) collective-permute-start(bf16[72,1536]{1,0:T(8,128)(2,1)S(1)} %get-tuple-element.61), channel_id=1, source_target_pairs={{0,12},{1,13},{16,28},{17,29},{32,44},{33,45},{48,60},{49,61},{2,1... | collective-permute-start | bytes 663560 | tf_op jit(solution)/shard_map/ppermute | solution.py:47
  21.2 3.4 %collective-permute-done.3 = bf16[72,1536]{1,0:T(8,128)(2,1)S(1)} collective-permute-done((bf16[72,1536]{1,0:T(8,128)(2,1)S(1)}, bf16[72,1536]{1,0:T(8,128)(2,1)S(1)}, u32[]{:S(2)}, u32[]{:S(2)}) %collective-permute-start.3) | collective-permute-done | bytes 221216 | tf_op jit(solution)/shard_map/ppermute | solution.py:47
  24.6 2.9 %collective-permute-done.4 = bf16[72,1536]{1,0:T(8,128)(2,1)S(1)} collective-permute-done((bf16[72,1536]{1,0:T(8,128)(2,1)S(1)}, bf16[72,1536]{1,0:T(8,128)(2,1)S(1)}, u32[]{:S(2)}, u32[]{:S(2)}) %collective-permute-start.4) | collective-permute-done | bytes 221216 | tf_op jit(solution)/shard_map/ppermute | solution.py:47
  33.4 7.2 %collective-permute-start.9 = (bf16[72,1536]{1,0:T(8,128)(2,1)S(1)}, bf16[72,1536]{1,0:T(8,128)(2,1)S(1)}, u32[]{:S(2)}, u32[]{:S(2)}) collective-permute-start(bf16[72,1536]{1,0:T(8,128)(2,1)S(1)} %add_convert_fusion), channel_id=1, source_target_pairs={{0,2},{1,3},{16,18},{17,19},{32,34},{33,35},{48,50},{49,51},{2,0},... | collective-permute-start | bytes 663560 | tf_op jit(solution)/shard_map/ppermute | solution.py:47
  40.7 7.4 %collective-permute-done.9 = bf16[72,1536]{1,0:T(8,128)(2,1)S(1)} collective-permute-done((bf16[72,1536]{1,0:T(8,128)(2,1)S(1)}, bf16[72,1536]{1,0:T(8,128)(2,1)S(1)}, u32[]{:S(2)}, u32[]{:S(2)}) %collective-permute-start.9) | collective-permute-done | bytes 221216 | tf_op jit(solution)/shard_map/ppermute | solution.py:47
  48.3 6.4 %collective-permute-start.10 = (bf16[72,1536]{1,0:T(8,128)(2,1)S(1)}, bf16[72,1536]{1,0:T(8,128)(2,1)S(1)}, u32[]{:S(2)}, u32[]{:S(2)}) collective-permute-start(bf16[72,1536]{1,0:T(8,128)(2,1)S(1)} %get-tuple-element.105), channel_id=1, source_target_pairs={{0,2},{1,3},{16,18},{17,19},{32,34},{33,35},{48,50},{49,51},{2,0},... | collective-permute-start | bytes 663560 | tf_op jit(solution)/shard_map/ppermute | solution.py:47
  56.6 3.7 %collective-permute-start.14 = (s32[1]{0:T(128)}, s32[1]{0:T(128)}, u32[]{:S(2)}, u32[]{:S(2)}) collective-permute-start(s32[1]{0:T(128)} %param.14), channel_id=1, source_target_pairs={{0,48},{1,49},{16,0},{17,1},{32,16},{33,17},{48,32},{49,33},{2,50}... | collective-permute-start | bytes 20 | tf_op jit(solution)/shard_map/ppermute | solution.py:47
  62.7 3.2 %collective-permute-start.17 = (bf16[144,1536]{1,0:T(8,128)(2,1)S(1)}, bf16[144,1536]{1,0:T(8,128)(2,1)S(1)}, u32[]{:S(2)}, u32[]{:S(2)}) collective-permute-start(bf16[144,1536]{1,0:T(8,128)(2,1)S(1)} %bitcast.40), channel_id=1, source_target_pairs={{0,12},{16,28},{32,44},{48,60},{2,14},{18,30},{34,46},{50,62},{4,0... | collective-permute-start | bytes 1327112 | tf_op jit(solution)/shard_map/ppermute | solution.py:47
  69.1 7.6 %collective-permute-done.15 = bf16[144,1536]{1,0:T(8,128)(2,1)S(1)} collective-permute-done((bf16[144,1536]{1,0:T(8,128)(2,1)S(1)}, bf16[144,1536]{1,0:T(8,128)(2,1)S(1)}, u32[]{:S(2)}, u32[]{:S(2)}) %collective-permute-start.15) | collective-permute-done | bytes 442400 | tf_op jit(solution)/shard_map/ppermute | solution.py:47
  77.2 3.0 %collective-permute-start.23 = (bf16[2,144,1536]{2,1,0:T(8,128)(2,1)S(1)}, bf16[2,144,1536]{2,1,0:T(8,128)(2,1)S(1)}, u32[]{:S(2)}, u32[]{:S(2)}) collective-permute-start(bf16[2,144,1536]{2,1,0:T(8,128)(2,1)S(1)} %pad_maximum_fusion.refs_1_.refs_5_), channel_id=1, source_target_pairs={{0,50},{16,0},{32,16},{48,32},{2,48},{18,2},{34,18},{50,34},{4,54}... | collective-permute-start | bytes 2654216 | tf_op jit(solution)/shard_map/ppermute | solution.py:47
  80.3 3.4 %collective-permute-start.18 = (bf16[72,1536]{1,0:T(8,128)(2,1)S(1)}, bf16[72,1536]{1,0:T(8,128)(2,1)S(1)}, u32[]{:S(2)}, u32[]{:S(2)}) collective-permute-start(bf16[72,1536]{1,0:T(8,128)(2,1)S(1)} %slice.21), channel_id=1, source_target_pairs={{0,12},{16,28},{32,44},{48,60},{2,14},{18,30},{34,46},{50,62},{4,0... | collective-permute-start | bytes 663560 | tf_op jit(solution)/shard_map/ppermute | solution.py:47
  83.7 2.7 %collective-permute-done.16 = bf16[72,1536]{1,0:T(8,128)(2,1)S(1)} collective-permute-done((bf16[72,1536]{1,0:T(8,128)(2,1)S(1)}, bf16[72,1536]{1,0:T(8,128)(2,1)S(1)}, u32[]{:S(2)}, u32[]{:S(2)}) %collective-permute-start.16) | collective-permute-done | bytes 221216 | tf_op jit(solution)/shard_map/ppermute | solution.py:47
  92.3 3.8 %collective-permute-done.26.refs_9_.refs_13_ = bf16[144,1536]{1,0:T(8,128)(2,1)S(1)} collective-permute-done((bf16[144,1536]{1,0:T(8,128)(2,1)}, bf16[144,1536]{1,0:T(8,128)(2,1)S(1)}, u32[]{:S(2)}, u32[]{:S(2)}) %collective-permute-start.26) | collective-permute-done | bytes 442400 | tf_op jit(solution)/shard_map/ppermute | solution.py:47
  96.1 2.7 %collective-permute-done.25.refs_8_.refs_12_ = bf16[144,1536]{1,0:T(8,128)(2,1)S(1)} collective-permute-done((bf16[144,1536]{1,0:T(8,128)(2,1)}, bf16[144,1536]{1,0:T(8,128)(2,1)S(1)}, u32[]{:S(2)}, u32[]{:S(2)}) %collective-permute-start.25) | collective-permute-done | bytes 442400 | tf_op jit(solution)/shard_map/ppermute | solution.py:47
  98.8 2.5 %collective-permute-done.19.refs_5_.refs_9_ = bf16[144,1536]{1,0:T(8,128)(2,1)} collective-permute-done((bf16[144,1536]{1,0:T(8,128)(2,1)}, bf16[144,1536]{1,0:T(8,128)(2,1)}, u32[]{:S(2)}, u32[]{:S(2)}) %collective-permute-start.19) | collective-permute-done | bytes 442400 | tf_op jit(solution)/shard_map/ppermute | solution.py:47
  109.6 2.5 %collective-permute-done.20.refs_11_.refs_15_ = bf16[144,1536]{1,0:T(8,128)(2,1)} collective-permute-done((bf16[144,1536]{1,0:T(8,128)(2,1)}, bf16[144,1536]{1,0:T(8,128)(2,1)}, u32[]{:S(2)}, u32[]{:S(2)}) %collective-permute-start.20) | collective-permute-done | bytes 442400 | tf_op jit(solution)/shard_map/ppermute | solution.py:47
  127.7 60.5 %collective-permute-done.42.rows_ref = bf16[64,576]{1,0:T(8,128)(2,1)S(1)} collective-permute-done((bf16[64,576]{1,0:T(8,128)(2,1)S(1)}, bf16[64,576]{1,0:T(8,128)(2,1)S(1)}, u32[]{:S(2)}, u32[]{:S(2)}) %collective-permute-start.42) | collective-permute-done | bytes 73760 | tf_op jit(solution)/shard_map/ppermute | solution.py:47
  188.2 12.3 %relay.7 = (bf16[64,576]{1,0:T(8,128)(2,1)S(1)}, bf16[64,576]{1,0:T(8,128)(2,1)S(1)}, bf16[64,576]{1,0:T(8,128)(2,1)S(1)}, bf16[64,576]{1,0:T(8,128)(2,1)S(1)}, bf16[64,576]{1,0:T(8,128)(2,1)}) custom-call(s32[8]{0:T(128)S(1)} %concatenate.11.info, bf16[64,576]{1,0:T(8,128)(2,1)S(1)} %collective-permute-done.42.rows_ref, ...), custom_call_target="tpu_custom_call" | custom-call | tf_op jit(solution)/shard_map/relay/pallas_call | solution.py:205
  200.6 4.6 %collective-permute-start.44 = (bf16[64,576]{1,0:T(8,128)(2,1)S(1)}, bf16[64,576]{1,0:T(8,128)(2,1)S(1)}, u32[]{:S(2)}, u32[]{:S(2)}) collective-permute-start(bf16[64,576]{1,0:T(8,128)(2,1)S(1)} %get-tuple-element.103), channel_id=1, source_target_pairs={{0,32},{1,33},{16,48},{17,49},{32,0},{33,1},{48,16},{49,17},{2,34}... | collective-permute-start | bytes 221192 | tf_op jit(solution)/shard_map/ppermute | solution.py:47
  205.2 2.3 %collective-permute-done.43.refs_1_ = bf16[64,576]{1,0:T(8,128)(2,1)S(1)} collective-permute-done((bf16[64,576]{1,0:T(8,128)(2,1)S(1)}, bf16[64,576]{1,0:T(8,128)(2,1)S(1)}, u32[]{:S(2)}, u32[]{:S(2)}) %collective-permute-start.43) | collective-permute-done | bytes 73760 | tf_op jit(solution)/shard_map/ppermute | solution.py:47
  207.5 2.6 %collective-permute-done.44.refs_2_ = bf16[64,576]{1,0:T(8,128)(2,1)S(1)} collective-permute-done((bf16[64,576]{1,0:T(8,128)(2,1)S(1)}, bf16[64,576]{1,0:T(8,128)(2,1)S(1)}, u32[]{:S(2)}, u32[]{:S(2)}) %collective-permute-start.44) | collective-permute-done | bytes 73760 | tf_op jit(solution)/shard_map/ppermute | solution.py:47
  (121 shorter events, 51.5 us)
Async XLA Ops:
  0.6 10.2 %collective-permute-start = (bf16[576,1536]{1,0:T(8,128)(2,1)}, bf16[576,1536]{1,0:T(8,128)(2,1)S(1)}, u32[]{:S(2)}, u32[]{:S(2)}) collective-permute-start(bf16[576,1536]{1,0:T(8,128)(2,1)} %bitcast.48), channel_id=1, source_target_pairs={{1,0},{17,16},{33,32},{49,48},{3,2},{19,18},{35,34},{51,50},{5,4},... | collective-permute-start | bytes 5308424 | tf_op jit(solution)/shard_map/ppermute | solution.py:47
  14.7 10.0 %collective-permute-start.3 = (bf16[72,1536]{1,0:T(8,128)(2,1)S(1)}, bf16[72,1536]{1,0:T(8,128)(2,1)S(1)}, u32[]{:S(2)}, u32[]{:S(2)}) collective-permute-start(bf16[72,1536]{1,0:T(8,128)(2,1)S(1)} %get-tuple-element.59), channel_id=1, source_target_pairs={{0,8},{1,9},{16,24},{17,25},{32,40},{33,41},{48,56},{49,57},{2,10}... | collective-permute-start | bytes 663560 | tf_op jit(solution)/shard_map/ppermute | solution.py:47
  17.9 9.6 %collective-permute-start.4 = (bf16[72,1536]{1,0:T(8,128)(2,1)S(1)}, bf16[72,1536]{1,0:T(8,128)(2,1)S(1)}, u32[]{:S(2)}, u32[]{:S(2)}) collective-permute-start(bf16[72,1536]{1,0:T(8,128)(2,1)S(1)} %get-tuple-element.60), channel_id=1, source_target_pairs={{0,4},{1,5},{16,20},{17,21},{32,36},{33,37},{48,52},{49,53},{2,6},... | collective-permute-start | bytes 663560 | tf_op jit(solution)/shard_map/ppermute | solution.py:47
  18.6 9.2 %collective-permute-start.5 = (bf16[72,1536]{1,0:T(8,128)(2,1)S(1)}, bf16[72,1536]{1,0:T(8,128)(2,1)S(1)}, u32[]{:S(2)}, u32[]{:S(2)}) collective-permute-start(bf16[72,1536]{1,0:T(8,128)(2,1)S(1)} %get-tuple-element.61), channel_id=1, source_target_pairs={{0,12},{1,13},{16,28},{17,29},{32,44},{33,45},{48,60},{49,61},{2,1... | collective-permute-start | bytes 663560 | tf_op jit(solution)/shard_map/ppermute | solution.py:47
  28.0 12.6 %collective-permute-start.6 = (bf16[72,1536]{1,0:T(8,128)(2,1)S(1)}, bf16[72,1536]{1,0:T(8,128)(2,1)S(1)}, u32[]{:S(2)}, u32[]{:S(2)}) collective-permute-start(bf16[72,1536]{1,0:T(8,128)(2,1)S(1)} %get-tuple-element.65), channel_id=1, source_target_pairs={{0,8},{1,9},{16,24},{17,25},{32,40},{33,41},{48,56},{49,57},{2,10}... | collective-permute-start | bytes 663560 | tf_op jit(solution)/shard_map/ppermute | solution.py:47
  30.1 10.4 %collective-permute-start.7 = (bf16[72,1536]{1,0:T(8,128)(2,1)S(1)}, bf16[72,1536]{1,0:T(8,128)(2,1)S(1)}, u32[]{:S(2)}, u32[]{:S(2)}) collective-permute-start(bf16[72,1536]{1,0:T(8,128)(2,1)S(1)} %get-tuple-element.66), channel_id=1, source_target_pairs={{0,4},{1,5},{16,20},{17,21},{32,36},{33,37},{48,52},{49,53},{2,6},... | collective-permute-start | bytes 663560 | tf_op jit(solution)/shard_map/ppermute | solution.py:47
  33.4 14.7 %collective-permute-start.9 = (bf16[72,1536]{1,0:T(8,128)(2,1)S(1)}, bf16[72,1536]{1,0:T(8,128)(2,1)S(1)}, u32[]{:S(2)}, u32[]{:S(2)}) collective-permute-start(bf16[72,1536]{1,0:T(8,128)(2,1)S(1)} %add_convert_fusion), channel_id=1, source_target_pairs={{0,2},{1,3},{16,18},{17,19},{32,34},{33,35},{48,50},{49,51},{2,0},... | collective-permute-start | bytes 663560 | tf_op jit(solution)/shard_map/ppermute | solution.py:47
  48.3 14.2 %collective-permute-start.10 = (bf16[72,1536]{1,0:T(8,128)(2,1)S(1)}, bf16[72,1536]{1,0:T(8,128)(2,1)S(1)}, u32[]{:S(2)}, u32[]{:S(2)}) collective-permute-start(bf16[72,1536]{1,0:T(8,128)(2,1)S(1)} %get-tuple-element.105), channel_id=1, source_target_pairs={{0,2},{1,3},{16,18},{17,19},{32,34},{33,35},{48,50},{49,51},{2,0},... | collective-permute-start | bytes 663560 | tf_op jit(solution)/shard_map/ppermute | solution.py:47
  62.6 14.1 %collective-permute-start.15 = (bf16[144,1536]{1,0:T(8,128)(2,1)S(1)}, bf16[144,1536]{1,0:T(8,128)(2,1)S(1)}, u32[]{:S(2)}, u32[]{:S(2)}) collective-permute-start(bf16[144,1536]{1,0:T(8,128)(2,1)S(1)} %bitcast.39), channel_id=1, source_target_pairs={{0,4},{16,20},{32,36},{48,52},{2,6},{18,22},{34,38},{50,54},{4,8},... | collective-permute-start | bytes 1327112 | tf_op jit(solution)/shard_map/ppermute | solution.py:47
  62.7 14.1 %collective-permute-start.17 = (bf16[144,1536]{1,0:T(8,128)(2,1)S(1)}, bf16[144,1536]{1,0:T(8,128)(2,1)S(1)}, u32[]{:S(2)}, u32[]{:S(2)}) collective-permute-start(bf16[144,1536]{1,0:T(8,128)(2,1)S(1)} %bitcast.40), channel_id=1, source_target_pairs={{0,12},{16,28},{32,44},{48,60},{2,14},{18,30},{34,46},{50,62},{4,0... | collective-permute-start | bytes 1327112 | tf_op jit(solution)/shard_map/ppermute | solution.py:47
  65.9 14.4 %collective-permute-start.21 = (bf16[144,1536]{1,0:T(8,128)(2,1)S(1)}, bf16[144,1536]{1,0:T(8,128)(2,1)}, u32[]{:S(2)}, u32[]{:S(2)}) collective-permute-start(bf16[144,1536]{1,0:T(8,128)(2,1)S(1)} %bitcast.41), channel_id=1, source_target_pairs={{0,16},{16,32},{32,48},{48,2},{2,18},{18,34},{34,50},{50,0},{4,20}... | collective-permute-start | bytes 1327112 | tf_op jit(solution)/shard_map/ppermute | solution.py:47
  67.3 24.1 %collective-permute-start.22 = (bf16[144,1536]{1,0:T(8,128)(2,1)S(1)}, bf16[144,1536]{1,0:T(8,128)(2,1)S(1)}, u32[]{:S(2)}, u32[]{:S(2)}) collective-permute-start(bf16[144,1536]{1,0:T(8,128)(2,1)S(1)} %bitcast.42), channel_id=1, source_target_pairs={{0,50},{16,0},{32,16},{48,32},{2,48},{18,2},{34,18},{50,34},{4,54}... | collective-permute-start | bytes 1327112 | tf_op jit(solution)/shard_map/ppermute | solution.py:47
  76.7 9.7 %collective-permute-start.16 = (bf16[72,1536]{1,0:T(8,128)(2,1)S(1)}, bf16[72,1536]{1,0:T(8,128)(2,1)S(1)}, u32[]{:S(2)}, u32[]{:S(2)}) collective-permute-start(bf16[72,1536]{1,0:T(8,128)(2,1)S(1)} %slice.20), channel_id=1, source_target_pairs={{0,4},{16,20},{32,36},{48,52},{2,6},{18,22},{34,38},{50,54},{4,8},... | collective-permute-start | bytes 663560 | tf_op jit(solution)/shard_map/ppermute | solution.py:47
  76.9 26.5 %collective-permute-start.24 = (bf16[2,144,1536]{2,1,0:T(8,128)(2,1)S(1)}, bf16[2,144,1536]{2,1,0:T(8,128)(2,1)S(1)}, u32[]{:S(2)}, u32[]{:S(2)}) collective-permute-start(bf16[2,144,1536]{2,1,0:T(8,128)(2,1)S(1)} %pad_maximum_fusion.refs_1_.refs_5_), channel_id=1, source_target_pairs={{0,16},{16,32},{32,48},{48,2},{2,18},{18,34},{34,50},{50,0},{4,20}... | collective-permute-start | bytes 2654216 | tf_op jit(solution)/shard_map/ppermute | solution.py:47
  77.2 24.0 %collective-permute-start.23 = (bf16[2,144,1536]{2,1,0:T(8,128)(2,1)S(1)}, bf16[2,144,1536]{2,1,0:T(8,128)(2,1)S(1)}, u32[]{:S(2)}, u32[]{:S(2)}) collective-permute-start(bf16[2,144,1536]{2,1,0:T(8,128)(2,1)S(1)} %pad_maximum_fusion.refs_1_.refs_5_), channel_id=1, source_target_pairs={{0,50},{16,0},{32,16},{48,32},{2,48},{18,2},{34,18},{50,34},{4,54}... | collective-permute-start | bytes 2654216 | tf_op jit(solution)/shard_map/ppermute | solution.py:47
  80.3 9.3 %collective-permute-start.18 = (bf16[72,1536]{1,0:T(8,128)(2,1)S(1)}, bf16[72,1536]{1,0:T(8,128)(2,1)S(1)}, u32[]{:S(2)}, u32[]{:S(2)}) collective-permute-start(bf16[72,1536]{1,0:T(8,128)(2,1)S(1)} %slice.21), channel_id=1, source_target_pairs={{0,12},{16,28},{32,44},{48,60},{2,14},{18,30},{34,46},{50,62},{4,0... | collective-permute-start | bytes 663560 | tf_op jit(solution)/shard_map/ppermute | solution.py:47
  86.4 9.7 %collective-permute-start.26 = (bf16[144,1536]{1,0:T(8,128)(2,1)}, bf16[144,1536]{1,0:T(8,128)(2,1)S(1)}, u32[]{:S(2)}, u32[]{:S(2)}) collective-permute-start(bf16[144,1536]{1,0:T(8,128)(2,1)} %collective-permute-done.21.refs_3_.refs_7_), channel_id=1, source_target_pairs={{0,16},{16,32},{32,48},{48,2},{2,18},{18,34},{34,50},{50,0},{4,20}... | collective-permute-start | bytes 1327112 | tf_op jit(solution)/shard_map/ppermute | solution.py:47
  91.4 9.8 %collective-permute-start.19 = (bf16[144,1536]{1,0:T(8,128)(2,1)}, bf16[144,1536]{1,0:T(8,128)(2,1)}, u32[]{:S(2)}, u32[]{:S(2)}) collective-permute-start(bf16[144,1536]{1,0:T(8,128)(2,1)} %constant_dynamic-update-slice_fusion.refs_2_.refs_6_), channel_id=1, source_target_pairs={{0,16},{16,32},{32,48},{48,2},{2,18},{18,34},{34,50},{50,0},{4,20}... | collective-permute-start | bytes 1327112 | tf_op jit(solution)/shard_map/ppermute | solution.py:47
  101.3 13.2 %collective-permute-start.27 = (bf16[2,144,1536]{2,1,0:T(8,128)(2,1)S(1)}, bf16[2,144,1536]{2,1,0:T(8,128)(2,1)}, u32[]{:S(2)}, u32[]{:S(2)}) collective-permute-start(bf16[2,144,1536]{2,1,0:T(8,128)(2,1)S(1)} %collective-permute-done.23.refs_7_.refs_11_), channel_id=1, source_target_pairs={{0,50},{16,0},{32,16},{48,32},{2,48},{18,2},{34,18},{50,34},{4,54}... | collective-permute-start | bytes 2654216 | tf_op jit(solution)/shard_map/ppermute | solution.py:47
  102.2 9.8 %collective-permute-start.20 = (bf16[144,1536]{1,0:T(8,128)(2,1)}, bf16[144,1536]{1,0:T(8,128)(2,1)}, u32[]{:S(2)}, u32[]{:S(2)}) collective-permute-start(bf16[144,1536]{1,0:T(8,128)(2,1)} %collective-permute-done.19.refs_5_.refs_9_), channel_id=1, source_target_pairs={{0,16},{16,32},{32,48},{48,2},{2,18},{18,34},{34,50},{50,0},{4,20}... | collective-permute-start | bytes 1327112 | tf_op jit(solution)/shard_map/ppermute | solution.py:47
  103.4 10.5 %collective-permute-start.28 = (bf16[144,1536]{1,0:T(8,128)(2,1)S(1)}, bf16[144,1536]{1,0:T(8,128)(2,1)}, u32[]{:S(2)}, u32[]{:S(2)}) collective-permute-start(bf16[144,1536]{1,0:T(8,128)(2,1)S(1)} %bitcast.43), channel_id=1, source_target_pairs={{0,1},{1,0},{16,17},{17,16},{32,33},{33,32},{48,49},{49,48},{2,3},... | collective-permute-start | bytes 1327112 | tf_op jit(solution)/shard_map/ppermute | solution.py:47
  112.1 10.2 %collective-permute-start.35 = (bf16[2,144,1536]{2,1,0:T(8,128)(2,1)S(1)}, bf16[2,144,1536]{2,1,0:T(8,128)(2,1)}, u32[]{:S(2)}, u32[]{:S(2)}) collective-permute-start(bf16[2,144,1536]{2,1,0:T(8,128)(2,1)S(1)} %collective-permute-done.23.refs_7_.refs_11_), channel_id=1, source_target_pairs={{0,1},{1,0},{16,17},{17,16},{32,33},{33,32},{48,49},{49,48},{2,3},... | collective-permute-start | bytes 2654216 | tf_op jit(solution)/shard_map/ppermute | solution.py:47
  126.4 61.8 %collective-permute-start.42 = (bf16[64,576]{1,0:T(8,128)(2,1)S(1)}, bf16[64,576]{1,0:T(8,128)(2,1)S(1)}, u32[]{:S(2)}, u32[]{:S(2)}) collective-permute-start(bf16[64,576]{1,0:T(8,128)(2,1)S(1)} %get-tuple-element.96), channel_id=1, source_target_pairs={{128,192},{129,193},{144,208},{145,209},{160,224},{161,225},{176,2... | collective-permute-start | bytes 221192 | tf_op jit(solution)/shard_map/ppermute | solution.py:47
  200.6 9.5 %collective-permute-start.44 = (bf16[64,576]{1,0:T(8,128)(2,1)S(1)}, bf16[64,576]{1,0:T(8,128)(2,1)S(1)}, u32[]{:S(2)}, u32[]{:S(2)}) collective-permute-start(bf16[64,576]{1,0:T(8,128)(2,1)S(1)} %get-tuple-element.103), channel_id=1, source_target_pairs={{0,32},{1,33},{16,48},{17,49},{32,0},{33,1},{48,16},{49,17},{2,34}... | collective-permute-start | bytes 221192 | tf_op jit(solution)/shard_map/ppermute | solution.py:47
  (36 other events, 416.9 us)

commit v4 on v3

--- a/solution.py
+++ b/solution.py
@@ -262,8 +262,8 @@
     b_state = ((1.0 - gain) * wb_master[0] - (0.7 * 0.81) * wb_moment[0]).T
     kept = jnp.where(first, a_state, b_state)
     state_got = send(jnp.where(first, b_state, a_state), core_swap())
+    a_got, b_got, state_got = lax.optimization_barrier((a_got, b_got, state_got))
     state = jnp.concatenate([jnp.where(first, kept, state_got), jnp.where(first, state_got, kept)])
-    a_got, b_got, state = lax.optimization_barrier((a_got, b_got, state))
     def y_sends(across, ahead, behind):
         return send(across, y_step(2)), send(ahead, y_step(1)), send(behind, y_step(-1))
 
@@ -271,14 +271,16 @@
         jnp.stack([y, core, z_high]), a_own, b_own, a_got, b_got
     )
     away_gots = y_sends(*away)
+    away_gots, state = lax.optimization_barrier((away_gots, state))
     away_total = away_mine.astype(F32) + sum(got.astype(F32) for got in away_gots)
     away_total, kept_parts = lax.optimization_barrier(
         (away_total.astype(BF16), (across, ahead, behind))
     )
     z_got = send(away_total, z_step(4))
-    total = mine.astype(F32) + sum(got.astype(F32) for got in y_sends(*kept_parts))
-
-    updated = state + (gain / replicas) * (total + z_got.astype(F32))
+    kept_gots = y_sends(*kept_parts)
+    partial = state + (gain / replicas) * (mine.astype(F32) + z_got.astype(F32))
+    partial, kept_gots = lax.optimization_barrier((partial, kept_gots))
+    updated = partial + (gain / replicas) * sum(got.astype(F32) for got in kept_gots)
     w = updated.astype(BF16)
     ours = jnp.where(first, updated[:owned], updated[owned:])
     theirs = send(jnp.where(first, updated[owned:], updated[:owned]), core_swap())

time: 210 us -> 209 us (level)
  transfers between devices with their start and end apart: 46 -> 46, of which waited for: 21 -> 23; matrix products, arithmetic and copies ran while one was open for 5% -> 5% of each run, Pallas kernels for 0% -> 0%
where the time goes in v4:
time: 209 us; the launch traced here: 211 us
  waiting for transfers between devices  111 us (53%)
  starting transfers between devices  66.2 us (32%)
  Pallas kernels  19.4 us (9%)
  local copies, waits for them, and re-layouts  8.91 us (4%)
  other arithmetic  3.34 us (2%)
    ppermute x46, waiting for transfers between devices, send(): return lax.ppermute(block, AXES, pairs)  111 us
    ppermute x46, starting transfers between devices, send(): return lax.ppermute(block, AXES, pairs)  66.2 us
    pallas_call x4, Pallas kernels, relay(): pl.pallas_call(functools.partial(relay_kernel, step, len(held) > 0), name...  14.2 us
  transfers between devices with their start and end apart: 46, of which 23 were waited for; matrix products, arithmetic and copies ran while one was open for 5% of the time, Pallas kernels for 0%

profile of v4, /device:TPU:6, one launch (start us, length us, event | category | flops | bytes accessed | tf_op | source)
XLA Modules:
  0.0 210.6 jit_solution(2974855537498979707)
XLA Ops:
  2.1 4.4 %collective-permute-start.1 = (bf16[576,1536]{1,0:T(8,128)(2,1)}, bf16[576,1536]{1,0:T(8,128)(2,1)}, u32[]{:S(2)}, u32[]{:S(2)}) collective-permute-start(bf16[576,1536]{1,0:T(8,128)(2,1)} %bitcast.50), channel_id=1, source_target_pairs={{0,1},{16,17},{32,33},{48,49},{2,3},{18,19},{34,35},{50,51},{4,5},... | collective-permute-start | bytes 5308424 | tf_op jit(solution)/shard_map/ppermute | solution.py:47
  9.4 3.8 %pair_sum.1 = (bf16[72,1536]{1,0:T(8,128)(2,1)S(1)}, bf16[72,1536]{1,0:T(8,128)(2,1)S(1)}, bf16[72,1536]{1,0:T(8,128)(2,1)S(1)}, bf16[72,1536]{1,0:T(8,128)(2,1)...) custom-call(s32[3]{0:T(128)S(1)} %pad_add_fusion.place, ...), custom_call_target="tpu_custom_call" | custom-call | tf_op jit(solution)/shard_map/pair_sum/pallas_call | solution.py:83
  13.2 3.3 %collective-permute-start.3 = (bf16[72,1536]{1,0:T(8,128)(2,1)S(1)}, bf16[72,1536]{1,0:T(8,128)(2,1)S(1)}, u32[]{:S(2)}, u32[]{:S(2)}) collective-permute-start(bf16[72,1536]{1,0:T(8,128)(2,1)S(1)} %get-tuple-element.64), channel_id=1, source_target_pairs={{0,8},{1,9},{16,24},{17,25},{32,40},{33,41},{48,56},{49,57},{2,10}... | collective-permute-start | bytes 663560 | tf_op jit(solution)/shard_map/ppermute | solution.py:47
  17.2 2.6 %collective-permute-start.5 = (bf16[72,1536]{1,0:T(8,128)(2,1)S(1)}, bf16[72,1536]{1,0:T(8,128)(2,1)S(1)}, u32[]{:S(2)}, u32[]{:S(2)}) collective-permute-start(bf16[72,1536]{1,0:T(8,128)(2,1)S(1)} %get-tuple-element.66), channel_id=1, source_target_pairs={{0,12},{1,13},{16,28},{17,29},{32,44},{33,45},{48,60},{49,61},{2,1... | collective-permute-start | bytes 663560 | tf_op jit(solution)/shard_map/ppermute | solution.py:47
  19.9 3.3 %collective-permute-done.3 = bf16[72,1536]{1,0:T(8,128)(2,1)S(1)} collective-permute-done((bf16[72,1536]{1,0:T(8,128)(2,1)S(1)}, bf16[72,1536]{1,0:T(8,128)(2,1)S(1)}, u32[]{:S(2)}, u32[]{:S(2)}) %collective-permute-start.3) | collective-permute-done | bytes 221216 | tf_op jit(solution)/shard_map/ppermute | solution.py:47
  23.2 2.9 %collective-permute-done.4 = bf16[72,1536]{1,0:T(8,128)(2,1)S(1)} collective-permute-done((bf16[72,1536]{1,0:T(8,128)(2,1)S(1)}, bf16[72,1536]{1,0:T(8,128)(2,1)S(1)}, u32[]{:S(2)}, u32[]{:S(2)}) %collective-permute-start.4) | collective-permute-done | bytes 221216 | tf_op jit(solution)/shard_map/ppermute | solution.py:47
  26.5 7.3 %collective-permute-start.6 = (bf16[72,1536]{1,0:T(8,128)(2,1)S(1)}, bf16[72,1536]{1,0:T(8,128)(2,1)S(1)}, u32[]{:S(2)}, u32[]{:S(2)}) collective-permute-start(bf16[72,1536]{1,0:T(8,128)(2,1)S(1)} %add_convert_fusion), channel_id=1, source_target_pairs={{0,2},{1,3},{16,18},{17,19},{32,34},{33,35},{48,50},{49,51},{2,0},... | collective-permute-start | bytes 663560 | tf_op jit(solution)/shard_map/ppermute | solution.py:47
  33.8 2.1 collective-permute-start.7
  39.5 3.8 %collective-permute-done.7 = bf16[72,1536]{1,0:T(8,128)(2,1)S(1)} collective-permute-done((bf16[72,1536]{1,0:T(8,128)(2,1)S(1)}, bf16[72,1536]{1,0:T(8,128)(2,1)S(1)}, u32[]{:S(2)}, u32[]{:S(2)}) %collective-permute-start.7) | collective-permute-done | bytes 221216 | tf_op jit(solution)/shard_map/ppermute | solution.py:47
  43.3 2.6 %collective-permute-done.8 = bf16[72,1536]{1,0:T(8,128)(2,1)S(1)} collective-permute-done((bf16[72,1536]{1,0:T(8,128)(2,1)S(1)}, bf16[72,1536]{1,0:T(8,128)(2,1)S(1)}, u32[]{:S(2)}, u32[]{:S(2)}) %collective-permute-start.8) | collective-permute-done | bytes 221216 | tf_op jit(solution)/shard_map/ppermute | solution.py:47
  50.5 3.8 %collective-permute-start.14 = (s32[1]{0:T(128)}, s32[1]{0:T(128)}, u32[]{:S(2)}, u32[]{:S(2)}) collective-permute-start(s32[1]{0:T(128)} %param.14), channel_id=1, source_target_pairs={{0,48},{1,49},{16,0},{17,1},{32,16},{33,17},{48,32},{49,33},{2,50}... | collective-permute-start | bytes 20 | tf_op jit(solution)/shard_map/ppermute | solution.py:47
  58.9 6.0 %collective-permute-start.15 = (bf16[144,1536]{1,0:T(8,128)(2,1)S(1)}, bf16[144,1536]{1,0:T(8,128)(2,1)S(1)}, u32[]{:S(2)}, u32[]{:S(2)}) collective-permute-start(bf16[144,1536]{1,0:T(8,128)(2,1)S(1)} %bitcast.39), channel_id=1, source_target_pairs={{0,4},{16,20},{32,36},{48,52},{2,6},{18,22},{34,38},{50,54},{4,8},... | collective-permute-start | bytes 1327112 | tf_op jit(solution)/shard_map/ppermute | solution.py:47
  65.8 2.3 %collective-permute-start.22 = (bf16[144,1536]{1,0:T(8,128)(2,1)S(1)}, bf16[144,1536]{1,0:T(8,128)(2,1)S(1)}, u32[]{:S(2)}, u32[]{:S(2)}) collective-permute-start(bf16[144,1536]{1,0:T(8,128)(2,1)S(1)} %bitcast.42), channel_id=1, source_target_pairs={{0,50},{16,0},{32,16},{48,32},{2,48},{18,2},{34,18},{50,34},{4,54}... | collective-permute-start | bytes 1327112 | tf_op jit(solution)/shard_map/ppermute | solution.py:47
  68.1 5.9 %collective-permute-done.15 = bf16[144,1536]{1,0:T(8,128)(2,1)S(1)} collective-permute-done((bf16[144,1536]{1,0:T(8,128)(2,1)S(1)}, bf16[144,1536]{1,0:T(8,128)(2,1)S(1)}, u32[]{:S(2)}, u32[]{:S(2)}) %collective-permute-start.15) | collective-permute-done | bytes 442400 | tf_op jit(solution)/shard_map/ppermute | solution.py:47
  74.0 2.6 %collective-permute-start.16 = (bf16[72,1536]{1,0:T(8,128)(2,1)S(1)}, bf16[72,1536]{1,0:T(8,128)(2,1)S(1)}, u32[]{:S(2)}, u32[]{:S(2)}) collective-permute-start(bf16[72,1536]{1,0:T(8,128)(2,1)S(1)} %slice.20), channel_id=1, source_target_pairs={{0,4},{16,20},{32,36},{48,52},{2,6},{18,22},{34,38},{50,54},{4,8},... | collective-permute-start | bytes 663560 | tf_op jit(solution)/shard_map/ppermute | solution.py:47
  81.2 2.5 %collective-permute-done.16 = bf16[72,1536]{1,0:T(8,128)(2,1)S(1)} collective-permute-done((bf16[72,1536]{1,0:T(8,128)(2,1)S(1)}, bf16[72,1536]{1,0:T(8,128)(2,1)S(1)}, u32[]{:S(2)}, u32[]{:S(2)}) %collective-permute-start.16) | collective-permute-done | bytes 221216 | tf_op jit(solution)/shard_map/ppermute | solution.py:47
  83.7 2.9 %collective-permute-start.26 = (bf16[144,1536]{1,0:T(8,128)(2,1)}, bf16[144,1536]{1,0:T(8,128)(2,1)S(1)}, u32[]{:S(2)}, u32[]{:S(2)}) collective-permute-start(bf16[144,1536]{1,0:T(8,128)(2,1)} %collective-permute-done.21.refs_3_.refs_7_), channel_id=1, source_target_pairs={{0,16},{16,32},{32,48},{48,2},{2,18},{18,34},{34,50},{50,0},{4,20}... | collective-permute-start | bytes 1327112 | tf_op jit(solution)/shard_map/ppermute | solution.py:47
  91.2 4.6 %collective-permute-done.26.refs_9_.refs_13_ = bf16[144,1536]{1,0:T(8,128)(2,1)S(1)} collective-permute-done((bf16[144,1536]{1,0:T(8,128)(2,1)}, bf16[144,1536]{1,0:T(8,128)(2,1)S(1)}, u32[]{:S(2)}, u32[]{:S(2)}) %collective-permute-start.26) | collective-permute-done | bytes 442400 | tf_op jit(solution)/shard_map/ppermute | solution.py:47
  97.7 2.9 %collective-permute-done.19.refs_5_.refs_9_ = bf16[144,1536]{1,0:T(8,128)(2,1)} collective-permute-done((bf16[144,1536]{1,0:T(8,128)(2,1)}, bf16[144,1536]{1,0:T(8,128)(2,1)}, u32[]{:S(2)}, u32[]{:S(2)}) %collective-permute-start.19) | collective-permute-done | bytes 442400 | tf_op jit(solution)/shard_map/ppermute | solution.py:47
  107.4 3.7 %collective-permute-done.20.refs_11_.refs_15_ = bf16[144,1536]{1,0:T(8,128)(2,1)} collective-permute-done((bf16[144,1536]{1,0:T(8,128)(2,1)}, bf16[144,1536]{1,0:T(8,128)(2,1)}, u32[]{:S(2)}, u32[]{:S(2)}) %collective-permute-start.20) | collective-permute-done | bytes 442400 | tf_op jit(solution)/shard_map/ppermute | solution.py:47
  126.5 61.7 %collective-permute-done.42.rows_ref = bf16[64,576]{1,0:T(8,128)(2,1)S(1)} collective-permute-done((bf16[64,576]{1,0:T(8,128)(2,1)S(1)}, bf16[64,576]{1,0:T(8,128)(2,1)S(1)}, u32[]{:S(2)}, u32[]{:S(2)}) %collective-permute-start.42) | collective-permute-done | bytes 73760 | tf_op jit(solution)/shard_map/ppermute | solution.py:47
  188.3 12.2 %relay.7 = (bf16[64,576]{1,0:T(8,128)(2,1)S(1)}, bf16[64,576]{1,0:T(8,128)(2,1)S(1)}, bf16[64,576]{1,0:T(8,128)(2,1)S(1)}, bf16[64,576]{1,0:T(8,128)(2,1)S(1)}, bf16[64,576]{1,0:T(8,128)(2,1)}) custom-call(s32[8]{0:T(128)S(1)} %concatenate.11.info, bf16[64,576]{1,0:T(8,128)(2,1)S(1)} %collective-permute-done.42.rows_ref, ...), custom_call_target="tpu_custom_call" | custom-call | tf_op jit(solution)/shard_map/relay/pallas_call | solution.py:205
  201.3 2.1 collective-permute-start.44
  206.8 2.2 %collective-permute-done.44.refs_2_ = bf16[64,576]{1,0:T(8,128)(2,1)S(1)} collective-permute-done((bf16[64,576]{1,0:T(8,128)(2,1)S(1)}, bf16[64,576]{1,0:T(8,128)(2,1)S(1)}, u32[]{:S(2)}, u32[]{:S(2)}) %collective-permute-start.44) | collective-permute-done | bytes 73760 | tf_op jit(solution)/shard_map/ppermute | solution.py:47
  (130 shorter events, 57.8 us)
Async XLA Ops:
  13.2 10.0 %collective-permute-start.3 = (bf16[72,1536]{1,0:T(8,128)(2,1)S(1)}, bf16[72,1536]{1,0:T(8,128)(2,1)S(1)}, u32[]{:S(2)}, u32[]{:S(2)}) collective-permute-start(bf16[72,1536]{1,0:T(8,128)(2,1)S(1)} %get-tuple-element.64), channel_id=1, source_target_pairs={{0,8},{1,9},{16,24},{17,25},{32,40},{33,41},{48,56},{49,57},{2,10}... | collective-permute-start | bytes 663560 | tf_op jit(solution)/shard_map/ppermute | solution.py:47
  16.5 9.6 %collective-permute-start.4 = (bf16[72,1536]{1,0:T(8,128)(2,1)S(1)}, bf16[72,1536]{1,0:T(8,128)(2,1)S(1)}, u32[]{:S(2)}, u32[]{:S(2)}) collective-permute-start(bf16[72,1536]{1,0:T(8,128)(2,1)S(1)} %get-tuple-element.65), channel_id=1, source_target_pairs={{0,4},{1,5},{16,20},{17,21},{32,36},{33,37},{48,52},{49,53},{2,6},... | collective-permute-start | bytes 663560 | tf_op jit(solution)/shard_map/ppermute | solution.py:47
  17.2 9.2 %collective-permute-start.5 = (bf16[72,1536]{1,0:T(8,128)(2,1)S(1)}, bf16[72,1536]{1,0:T(8,128)(2,1)S(1)}, u32[]{:S(2)}, u32[]{:S(2)}) collective-permute-start(bf16[72,1536]{1,0:T(8,128)(2,1)S(1)} %get-tuple-element.66), channel_id=1, source_target_pairs={{0,12},{1,13},{16,28},{17,29},{32,44},{33,45},{48,60},{49,61},{2,1... | collective-permute-start | bytes 663560 | tf_op jit(solution)/shard_map/ppermute | solution.py:47
  26.5 12.8 %collective-permute-start.6 = (bf16[72,1536]{1,0:T(8,128)(2,1)S(1)}, bf16[72,1536]{1,0:T(8,128)(2,1)S(1)}, u32[]{:S(2)}, u32[]{:S(2)}) collective-permute-start(bf16[72,1536]{1,0:T(8,128)(2,1)S(1)} %add_convert_fusion), channel_id=1, source_target_pairs={{0,2},{1,3},{16,18},{17,19},{32,34},{33,35},{48,50},{49,51},{2,0},... | collective-permute-start | bytes 663560 | tf_op jit(solution)/shard_map/ppermute | solution.py:47
  33.8 9.5 %collective-permute-start.7 = (bf16[72,1536]{1,0:T(8,128)(2,1)S(1)}, bf16[72,1536]{1,0:T(8,128)(2,1)S(1)}, u32[]{:S(2)}, u32[]{:S(2)}) collective-permute-start(bf16[72,1536]{1,0:T(8,128)(2,1)S(1)} %get-tuple-element.78), channel_id=1, source_target_pairs={{0,8},{1,9},{16,24},{17,25},{32,40},{33,41},{48,56},{49,57},{2,10}... | collective-permute-start | bytes 663560 | tf_op jit(solution)/shard_map/ppermute | solution.py:47
  35.9 10.0 %collective-permute-start.8 = (bf16[72,1536]{1,0:T(8,128)(2,1)S(1)}, bf16[72,1536]{1,0:T(8,128)(2,1)S(1)}, u32[]{:S(2)}, u32[]{:S(2)}) collective-permute-start(bf16[72,1536]{1,0:T(8,128)(2,1)S(1)} %get-tuple-element.79), channel_id=1, source_target_pairs={{0,4},{1,5},{16,20},{17,21},{32,36},{33,37},{48,52},{49,53},{2,6},... | collective-permute-start | bytes 663560 | tf_op jit(solution)/shard_map/ppermute | solution.py:47
  37.3 8.8 %collective-permute-start.9 = (bf16[72,1536]{1,0:T(8,128)(2,1)S(1)}, bf16[72,1536]{1,0:T(8,128)(2,1)S(1)}, u32[]{:S(2)}, u32[]{:S(2)}) collective-permute-start(bf16[72,1536]{1,0:T(8,128)(2,1)S(1)} %get-tuple-element.80), channel_id=1, source_target_pairs={{0,12},{1,13},{16,28},{17,29},{32,44},{33,45},{48,60},{49,61},{2,1... | collective-permute-start | bytes 663560 | tf_op jit(solution)/shard_map/ppermute | solution.py:47
  46.3 12.5 %collective-permute-start.10 = (bf16[72,1536]{1,0:T(8,128)(2,1)S(1)}, bf16[72,1536]{1,0:T(8,128)(2,1)S(1)}, u32[]{:S(2)}, u32[]{:S(2)}) collective-permute-start(bf16[72,1536]{1,0:T(8,128)(2,1)S(1)} %get-tuple-element.121), channel_id=1, source_target_pairs={{0,2},{1,3},{16,18},{17,19},{32,34},{33,35},{48,50},{49,51},{2,0},... | collective-permute-start | bytes 663560 | tf_op jit(solution)/shard_map/ppermute | solution.py:47
  48.3 10.5 %collective-permute-start.11 = (f32[36,1536]{1,0:T(8,128)S(1)}, f32[36,1536]{1,0:T(8,128)S(1)}, u32[]{:S(2)}, u32[]{:S(2)}) collective-permute-start(f32[36,1536]{1,0:T(8,128)S(1)} %slice_select_fusion.1), channel_id=1, source_target_pairs={{0,1},{1,0},{16,17},{17,16},{32,33},{33,32},{48,49},{49,48},{2,3},... | collective-permute-start | bytes 663560 | tf_op jit(solution)/shard_map/ppermute | solution.py:47
  58.9 15.1 %collective-permute-start.15 = (bf16[144,1536]{1,0:T(8,128)(2,1)S(1)}, bf16[144,1536]{1,0:T(8,128)(2,1)S(1)}, u32[]{:S(2)}, u32[]{:S(2)}) collective-permute-start(bf16[144,1536]{1,0:T(8,128)(2,1)S(1)} %bitcast.39), channel_id=1, source_target_pairs={{0,4},{16,20},{32,36},{48,52},{2,6},{18,22},{34,38},{50,54},{4,8},... | collective-permute-start | bytes 1327112 | tf_op jit(solution)/shard_map/ppermute | solution.py:47
  64.9 11.7 %collective-permute-start.17 = (bf16[144,1536]{1,0:T(8,128)(2,1)S(1)}, bf16[144,1536]{1,0:T(8,128)(2,1)S(1)}, u32[]{:S(2)}, u32[]{:S(2)}) collective-permute-start(bf16[144,1536]{1,0:T(8,128)(2,1)S(1)} %bitcast.40), channel_id=1, source_target_pairs={{0,12},{16,28},{32,44},{48,60},{2,14},{18,30},{34,46},{50,62},{4,0... | collective-permute-start | bytes 1327112 | tf_op jit(solution)/shard_map/ppermute | solution.py:47
  64.9 15.1 %collective-permute-start.21 = (bf16[144,1536]{1,0:T(8,128)(2,1)S(1)}, bf16[144,1536]{1,0:T(8,128)(2,1)}, u32[]{:S(2)}, u32[]{:S(2)}) collective-permute-start(bf16[144,1536]{1,0:T(8,128)(2,1)S(1)} %bitcast.41), channel_id=1, source_target_pairs={{0,16},{16,32},{32,48},{48,2},{2,18},{18,34},{34,50},{50,0},{4,20}... | collective-permute-start | bytes 1327112 | tf_op jit(solution)/shard_map/ppermute | solution.py:47
  65.8 23.9 %collective-permute-start.22 = (bf16[144,1536]{1,0:T(8,128)(2,1)S(1)}, bf16[144,1536]{1,0:T(8,128)(2,1)S(1)}, u32[]{:S(2)}, u32[]{:S(2)}) collective-permute-start(bf16[144,1536]{1,0:T(8,128)(2,1)S(1)} %bitcast.42), channel_id=1, source_target_pairs={{0,50},{16,0},{32,16},{48,32},{2,48},{18,2},{34,18},{50,34},{4,54}... | collective-permute-start | bytes 1327112 | tf_op jit(solution)/shard_map/ppermute | solution.py:47
  74.0 9.7 %collective-permute-start.16 = (bf16[72,1536]{1,0:T(8,128)(2,1)S(1)}, bf16[72,1536]{1,0:T(8,128)(2,1)S(1)}, u32[]{:S(2)}, u32[]{:S(2)}) collective-permute-start(bf16[72,1536]{1,0:T(8,128)(2,1)S(1)} %slice.20), channel_id=1, source_target_pairs={{0,4},{16,20},{32,36},{48,52},{2,6},{18,22},{34,38},{50,54},{4,8},... | collective-permute-start | bytes 663560 | tf_op jit(solution)/shard_map/ppermute | solution.py:47
  76.7 26.0 %collective-permute-start.24 = (bf16[2,144,1536]{2,1,0:T(8,128)(2,1)S(1)}, bf16[2,144,1536]{2,1,0:T(8,128)(2,1)S(1)}, u32[]{:S(2)}, u32[]{:S(2)}) collective-permute-start(bf16[2,144,1536]{2,1,0:T(8,128)(2,1)S(1)} %pad_maximum_fusion.refs_1_.refs_5_), channel_id=1, source_target_pairs={{0,16},{16,32},{32,48},{48,2},{2,18},{18,34},{34,50},{50,0},{4,20}... | collective-permute-start | bytes 2654216 | tf_op jit(solution)/shard_map/ppermute | solution.py:47
  78.7 21.9 %collective-permute-start.23 = (bf16[2,144,1536]{2,1,0:T(8,128)(2,1)S(1)}, bf16[2,144,1536]{2,1,0:T(8,128)(2,1)S(1)}, u32[]{:S(2)}, u32[]{:S(2)}) collective-permute-start(bf16[2,144,1536]{2,1,0:T(8,128)(2,1)S(1)} %pad_maximum_fusion.refs_1_.refs_5_), channel_id=1, source_target_pairs={{0,50},{16,0},{32,16},{48,32},{2,48},{18,2},{34,18},{50,34},{4,54}... | collective-permute-start | bytes 2654216 | tf_op jit(solution)/shard_map/ppermute | solution.py:47
  83.7 12.1 %collective-permute-start.26 = (bf16[144,1536]{1,0:T(8,128)(2,1)}, bf16[144,1536]{1,0:T(8,128)(2,1)S(1)}, u32[]{:S(2)}, u32[]{:S(2)}) collective-permute-start(bf16[144,1536]{1,0:T(8,128)(2,1)} %collective-permute-done.21.refs_3_.refs_7_), channel_id=1, source_target_pairs={{0,16},{16,32},{32,48},{48,2},{2,18},{18,34},{34,50},{50,0},{4,20}... | collective-permute-start | bytes 1327112 | tf_op jit(solution)/shard_map/ppermute | solution.py:47
  89.8 10.8 %collective-permute-start.19 = (bf16[144,1536]{1,0:T(8,128)(2,1)}, bf16[144,1536]{1,0:T(8,128)(2,1)}, u32[]{:S(2)}, u32[]{:S(2)}) collective-permute-start(bf16[144,1536]{1,0:T(8,128)(2,1)} %constant_dynamic-update-slice_fusion.refs_2_.refs_6_), channel_id=1, source_target_pairs={{0,16},{16,32},{32,48},{48,2},{2,18},{18,34},{34,50},{50,0},{4,20}... | collective-permute-start | bytes 1327112 | tf_op jit(solution)/shard_map/ppermute | solution.py:47
  100.6 13.2 %collective-permute-start.27 = (bf16[2,144,1536]{2,1,0:T(8,128)(2,1)S(1)}, bf16[2,144,1536]{2,1,0:T(8,128)(2,1)}, u32[]{:S(2)}, u32[]{:S(2)}) collective-permute-start(bf16[2,144,1536]{2,1,0:T(8,128)(2,1)S(1)} %collective-permute-done.23.refs_7_.refs_11_), channel_id=1, source_target_pairs={{0,50},{16,0},{32,16},{48,32},{2,48},{18,2},{34,18},{50,34},{4,54}... | collective-permute-start | bytes 2654216 | tf_op jit(solution)/shard_map/ppermute | solution.py:47
  101.3 9.8 %collective-permute-start.20 = (bf16[144,1536]{1,0:T(8,128)(2,1)}, bf16[144,1536]{1,0:T(8,128)(2,1)}, u32[]{:S(2)}, u32[]{:S(2)}) collective-permute-start(bf16[144,1536]{1,0:T(8,128)(2,1)} %collective-permute-done.19.refs_5_.refs_9_), channel_id=1, source_target_pairs={{0,16},{16,32},{32,48},{48,2},{2,18},{18,34},{34,50},{50,0},{4,20}... | collective-permute-start | bytes 1327112 | tf_op jit(solution)/shard_map/ppermute | solution.py:47
  111.1 10.0 %collective-permute-start.35 = (bf16[2,144,1536]{2,1,0:T(8,128)(2,1)S(1)}, bf16[2,144,1536]{2,1,0:T(8,128)(2,1)}, u32[]{:S(2)}, u32[]{:S(2)}) collective-permute-start(bf16[2,144,1536]{2,1,0:T(8,128)(2,1)S(1)} %collective-permute-done.23.refs_7_.refs_11_), channel_id=1, source_target_pairs={{0,1},{1,0},{16,17},{17,16},{32,33},{33,32},{48,49},{49,48},{2,3},... | collective-permute-start | bytes 2654216 | tf_op jit(solution)/shard_map/ppermute | solution.py:47
  111.6 9.4 %collective-permute-start.29 = (bf16[2,144,1536]{2,1,0:T(8,128)(2,1)S(1)}, bf16[2,144,1536]{2,1,0:T(8,128)(2,1)}, u32[]{:S(2)}, u32[]{:S(2)}) collective-permute-start(bf16[2,144,1536]{2,1,0:T(8,128)(2,1)S(1)} %pad_maximum_fusion.refs_1_.refs_5_), channel_id=1, source_target_pairs={{0,1},{1,0},{16,17},{17,16},{32,33},{33,32},{48,49},{49,48},{2,3},... | collective-permute-start | bytes 2654216 | tf_op jit(solution)/shard_map/ppermute | solution.py:47
  111.7 9.3 %collective-permute-start.32 = (bf16[2,144,1536]{2,1,0:T(8,128)(2,1)S(1)}, bf16[2,144,1536]{2,1,0:T(8,128)(2,1)}, u32[]{:S(2)}, u32[]{:S(2)}) collective-permute-start(bf16[2,144,1536]{2,1,0:T(8,128)(2,1)S(1)} %collective-permute-done.24.refs_4_.refs_8_), channel_id=1, source_target_pairs={{0,1},{1,0},{16,17},{17,16},{32,33},{33,32},{48,49},{49,48},{2,3},... | collective-permute-start | bytes 2654216 | tf_op jit(solution)/shard_map/ppermute | solution.py:47
  125.2 63.0 %collective-permute-start.42 = (bf16[64,576]{1,0:T(8,128)(2,1)S(1)}, bf16[64,576]{1,0:T(8,128)(2,1)S(1)}, u32[]{:S(2)}, u32[]{:S(2)}) collective-permute-start(bf16[64,576]{1,0:T(8,128)(2,1)S(1)} %get-tuple-element.112), channel_id=1, source_target_pairs={{128,192},{129,193},{144,208},{145,209},{160,224},{161,225},{176,2... | collective-permute-start | bytes 221192 | tf_op jit(solution)/shard_map/ppermute | solution.py:47
  (40 other events, 452.7 us)

commit v5 on v4

--- a/solution.py
+++ b/solution.py
@@ -71,7 +71,7 @@
     for at in range(8):
         pltpu.make_async_copy(own_v.at[at], own_v.at[at], own_sem.at[at]).wait()
         pltpu.make_async_copy(got_v.at[at], got_v.at[at], got_sem.at[at]).wait()
-        outs[at][...] = (own_v[at].astype(F32) + got_v[at].astype(F32)).astype(BF16)
+        outs[at][...] = own_v[at] + got_v[at]
 
 
 def pair_sum(place, *blocks):

time: 209 us -> 215 us (1.029); the launches traced: 211 us -> 212 us
  Pallas kernels: 19.4 us -> 25.2 us
  waiting for transfers between devices: 111 us -> 107 us
    pallas_call x4, Pallas kernels: 14.2 us -> 19.9 us  [relay(): pl.pallas_call(functools.partial(relay_kernel, step, len(held) > 0), name...]
    ppermute x46, waiting for transfers between devices: 111 us -> 107 us  [send(): return lax.ppermute(block, AXES, pairs)]
where the time goes in v5:
time: 215 us; the launch traced here: 212 us
  waiting for transfers between devices  107 us (50%)
  starting transfers between devices  66.2 us (31%)
  Pallas kernels  25.2 us (12%)
  local copies, waits for them, and re-layouts  8.91 us (4%)
  other arithmetic  3.34 us (2%)
    ppermute x46, waiting for transfers between devices, send(): return lax.ppermute(block, AXES, pairs)  107 us
    ppermute x46, starting transfers between devices, send(): return lax.ppermute(block, AXES, pairs)  66.2 us
    pallas_call x4, Pallas kernels, relay(): pl.pallas_call(functools.partial(relay_kernel, step, len(held) > 0), name...  19.9 us
  transfers between devices with their start and end apart: 46, of which 23 were waited for; matrix products, arithmetic and copies ran while one was open for 5% of the time, Pallas kernels for 0%

profile of v5, /device:TPU:6, one launch (start us, length us, event | category | flops | bytes accessed | tf_op | source)
XLA Modules:
  0.0 212.2 jit_solution(8025449315371308265)
XLA Ops:
  2.1 4.4 %collective-permute-start.1 = (bf16[576,1536]{1,0:T(8,128)(2,1)}, bf16[576,1536]{1,0:T(8,128)(2,1)}, u32[]{:S(2)}, u32[]{:S(2)}) collective-permute-start(bf16[576,1536]{1,0:T(8,128)(2,1)} %bitcast.50), channel_id=1, source_target_pairs={{0,1},{16,17},{32,33},{48,49},{2,3},{18,19},{34,35},{50,51},{4,5},... | collective-permute-start | bytes 5308424 | tf_op jit(solution)/shard_map/ppermute | solution.py:47
  9.4 3.7 %pair_sum.1 = (bf16[72,1536]{1,0:T(8,128)(2,1)S(1)}, bf16[72,1536]{1,0:T(8,128)(2,1)S(1)}, bf16[72,1536]{1,0:T(8,128)(2,1)S(1)}, bf16[72,1536]{1,0:T(8,128)(2,1)...) custom-call(s32[3]{0:T(128)S(1)} %pad_add_fusion.place, ...), custom_call_target="tpu_custom_call" | custom-call | tf_op jit(solution)/shard_map/pair_sum/pallas_call | solution.py:83
  13.2 3.3 %collective-permute-start.3 = (bf16[72,1536]{1,0:T(8,128)(2,1)S(1)}, bf16[72,1536]{1,0:T(8,128)(2,1)S(1)}, u32[]{:S(2)}, u32[]{:S(2)}) collective-permute-start(bf16[72,1536]{1,0:T(8,128)(2,1)S(1)} %get-tuple-element.64), channel_id=1, source_target_pairs={{0,8},{1,9},{16,24},{17,25},{32,40},{33,41},{48,56},{49,57},{2,10}... | collective-permute-start | bytes 663560 | tf_op jit(solution)/shard_map/ppermute | solution.py:47
  17.1 2.6 %collective-permute-start.5 = (bf16[72,1536]{1,0:T(8,128)(2,1)S(1)}, bf16[72,1536]{1,0:T(8,128)(2,1)S(1)}, u32[]{:S(2)}, u32[]{:S(2)}) collective-permute-start(bf16[72,1536]{1,0:T(8,128)(2,1)S(1)} %get-tuple-element.66), channel_id=1, source_target_pairs={{0,12},{1,13},{16,28},{17,29},{32,44},{33,45},{48,60},{49,61},{2,1... | collective-permute-start | bytes 663560 | tf_op jit(solution)/shard_map/ppermute | solution.py:47
  19.9 3.3 %collective-permute-done.3 = bf16[72,1536]{1,0:T(8,128)(2,1)S(1)} collective-permute-done((bf16[72,1536]{1,0:T(8,128)(2,1)S(1)}, bf16[72,1536]{1,0:T(8,128)(2,1)S(1)}, u32[]{:S(2)}, u32[]{:S(2)}) %collective-permute-start.3) | collective-permute-done | bytes 221216 | tf_op jit(solution)/shard_map/ppermute | solution.py:47
  23.1 2.9 %collective-permute-done.4 = bf16[72,1536]{1,0:T(8,128)(2,1)S(1)} collective-permute-done((bf16[72,1536]{1,0:T(8,128)(2,1)S(1)}, bf16[72,1536]{1,0:T(8,128)(2,1)S(1)}, u32[]{:S(2)}, u32[]{:S(2)}) %collective-permute-start.4) | collective-permute-done | bytes 221216 | tf_op jit(solution)/shard_map/ppermute | solution.py:47
  26.5 7.3 %collective-permute-start.6 = (bf16[72,1536]{1,0:T(8,128)(2,1)S(1)}, bf16[72,1536]{1,0:T(8,128)(2,1)S(1)}, u32[]{:S(2)}, u32[]{:S(2)}) collective-permute-start(bf16[72,1536]{1,0:T(8,128)(2,1)S(1)} %add_convert_fusion), channel_id=1, source_target_pairs={{0,2},{1,3},{16,18},{17,19},{32,34},{33,35},{48,50},{49,51},{2,0},... | collective-permute-start | bytes 663560 | tf_op jit(solution)/shard_map/ppermute | solution.py:47
  33.8 2.1 collective-permute-start.7
  39.4 3.8 %collective-permute-done.7 = bf16[72,1536]{1,0:T(8,128)(2,1)S(1)} collective-permute-done((bf16[72,1536]{1,0:T(8,128)(2,1)S(1)}, bf16[72,1536]{1,0:T(8,128)(2,1)S(1)}, u32[]{:S(2)}, u32[]{:S(2)}) %collective-permute-start.7) | collective-permute-done | bytes 221216 | tf_op jit(solution)/shard_map/ppermute | solution.py:47
  43.3 2.6 %collective-permute-done.8 = bf16[72,1536]{1,0:T(8,128)(2,1)S(1)} collective-permute-done((bf16[72,1536]{1,0:T(8,128)(2,1)S(1)}, bf16[72,1536]{1,0:T(8,128)(2,1)S(1)}, u32[]{:S(2)}, u32[]{:S(2)}) %collective-permute-start.8) | collective-permute-done | bytes 221216 | tf_op jit(solution)/shard_map/ppermute | solution.py:47
  48.4 2.1 collective-permute-start.13
  50.5 3.8 %collective-permute-start.14 = (s32[1]{0:T(128)}, s32[1]{0:T(128)}, u32[]{:S(2)}, u32[]{:S(2)}) collective-permute-start(s32[1]{0:T(128)} %param.14), channel_id=1, source_target_pairs={{0,48},{1,49},{16,0},{17,1},{32,16},{33,17},{48,32},{49,33},{2,50}... | collective-permute-start | bytes 20 | tf_op jit(solution)/shard_map/ppermute | solution.py:47
  58.9 6.0 %collective-permute-start.15 = (bf16[144,1536]{1,0:T(8,128)(2,1)S(1)}, bf16[144,1536]{1,0:T(8,128)(2,1)S(1)}, u32[]{:S(2)}, u32[]{:S(2)}) collective-permute-start(bf16[144,1536]{1,0:T(8,128)(2,1)S(1)} %bitcast.39), channel_id=1, source_target_pairs={{0,4},{16,20},{32,36},{48,52},{2,6},{18,22},{34,38},{50,54},{4,8},... | collective-permute-start | bytes 1327112 | tf_op jit(solution)/shard_map/ppermute | solution.py:47
  65.8 2.3 %collective-permute-start.22 = (bf16[144,1536]{1,0:T(8,128)(2,1)S(1)}, bf16[144,1536]{1,0:T(8,128)(2,1)S(1)}, u32[]{:S(2)}, u32[]{:S(2)}) collective-permute-start(bf16[144,1536]{1,0:T(8,128)(2,1)S(1)} %bitcast.42), channel_id=1, source_target_pairs={{0,50},{16,0},{32,16},{48,32},{2,48},{18,2},{34,18},{50,34},{4,54}... | collective-permute-start | bytes 1327112 | tf_op jit(solution)/shard_map/ppermute | solution.py:47
  68.1 5.9 %collective-permute-done.15 = bf16[144,1536]{1,0:T(8,128)(2,1)S(1)} collective-permute-done((bf16[144,1536]{1,0:T(8,128)(2,1)S(1)}, bf16[144,1536]{1,0:T(8,128)(2,1)S(1)}, u32[]{:S(2)}, u32[]{:S(2)}) %collective-permute-start.15) | collective-permute-done | bytes 442400 | tf_op jit(solution)/shard_map/ppermute | solution.py:47
  74.0 2.6 %collective-permute-start.16 = (bf16[72,1536]{1,0:T(8,128)(2,1)S(1)}, bf16[72,1536]{1,0:T(8,128)(2,1)S(1)}, u32[]{:S(2)}, u32[]{:S(2)}) collective-permute-start(bf16[72,1536]{1,0:T(8,128)(2,1)S(1)} %slice.20), channel_id=1, source_target_pairs={{0,4},{16,20},{32,36},{48,52},{2,6},{18,22},{34,38},{50,54},{4,8},... | collective-permute-start | bytes 663560 | tf_op jit(solution)/shard_map/ppermute | solution.py:47
  81.2 2.5 %collective-permute-done.16 = bf16[72,1536]{1,0:T(8,128)(2,1)S(1)} collective-permute-done((bf16[72,1536]{1,0:T(8,128)(2,1)S(1)}, bf16[72,1536]{1,0:T(8,128)(2,1)S(1)}, u32[]{:S(2)}, u32[]{:S(2)}) %collective-permute-start.16) | collective-permute-done | bytes 221216 | tf_op jit(solution)/shard_map/ppermute | solution.py:47
  83.6 2.9 %collective-permute-start.26 = (bf16[144,1536]{1,0:T(8,128)(2,1)}, bf16[144,1536]{1,0:T(8,128)(2,1)S(1)}, u32[]{:S(2)}, u32[]{:S(2)}) collective-permute-start(bf16[144,1536]{1,0:T(8,128)(2,1)} %collective-permute-done.21.refs_3_.refs_7_), channel_id=1, source_target_pairs={{0,16},{16,32},{32,48},{48,2},{2,18},{18,34},{34,50},{50,0},{4,20}... | collective-permute-start | bytes 1327112 | tf_op jit(solution)/shard_map/ppermute | solution.py:47
  91.2 4.6 %collective-permute-done.26.refs_9_.refs_13_ = bf16[144,1536]{1,0:T(8,128)(2,1)S(1)} collective-permute-done((bf16[144,1536]{1,0:T(8,128)(2,1)}, bf16[144,1536]{1,0:T(8,128)(2,1)S(1)}, u32[]{:S(2)}, u32[]{:S(2)}) %collective-permute-start.26) | collective-permute-done | bytes 442400 | tf_op jit(solution)/shard_map/ppermute | solution.py:47
  97.6 2.9 %collective-permute-done.19.refs_5_.refs_9_ = bf16[144,1536]{1,0:T(8,128)(2,1)} collective-permute-done((bf16[144,1536]{1,0:T(8,128)(2,1)}, bf16[144,1536]{1,0:T(8,128)(2,1)}, u32[]{:S(2)}, u32[]{:S(2)}) %collective-permute-start.19) | collective-permute-done | bytes 442400 | tf_op jit(solution)/shard_map/ppermute | solution.py:47
  107.4 3.7 %collective-permute-done.20.refs_11_.refs_15_ = bf16[144,1536]{1,0:T(8,128)(2,1)} collective-permute-done((bf16[144,1536]{1,0:T(8,128)(2,1)}, bf16[144,1536]{1,0:T(8,128)(2,1)}, u32[]{:S(2)}, u32[]{:S(2)}) %collective-permute-start.20) | collective-permute-done | bytes 442400 | tf_op jit(solution)/shard_map/ppermute | solution.py:47
  126.5 57.9 %collective-permute-done.42.rows_ref = bf16[64,576]{1,0:T(8,128)(2,1)S(1)} collective-permute-done((bf16[64,576]{1,0:T(8,128)(2,1)S(1)}, bf16[64,576]{1,0:T(8,128)(2,1)S(1)}, u32[]{:S(2)}, u32[]{:S(2)}) %collective-permute-start.42) | collective-permute-done | bytes 73760 | tf_op jit(solution)/shard_map/ppermute | solution.py:47
  184.4 17.9 %relay.7 = (bf16[64,576]{1,0:T(8,128)(2,1)S(1)}, bf16[64,576]{1,0:T(8,128)(2,1)S(1)}, bf16[64,576]{1,0:T(8,128)(2,1)S(1)}, bf16[64,576]{1,0:T(8,128)(2,1)S(1)}, bf16[64,576]{1,0:T(8,128)(2,1)}) custom-call(s32[8]{0:T(128)S(1)} %concatenate.11.info, bf16[64,576]{1,0:T(8,128)(2,1)S(1)} %collective-permute-done.42.rows_ref, ...), custom_call_target="tpu_custom_call" | custom-call | tf_op jit(solution)/shard_map/relay/pallas_call | solution.py:205
  203.2 2.1 collective-permute-start.44
  (130 shorter events, 57.7 us)
Async XLA Ops:
  13.2 10.0 %collective-permute-start.3 = (bf16[72,1536]{1,0:T(8,128)(2,1)S(1)}, bf16[72,1536]{1,0:T(8,128)(2,1)S(1)}, u32[]{:S(2)}, u32[]{:S(2)}) collective-permute-start(bf16[72,1536]{1,0:T(8,128)(2,1)S(1)} %get-tuple-element.64), channel_id=1, source_target_pairs={{0,8},{1,9},{16,24},{17,25},{32,40},{33,41},{48,56},{49,57},{2,10}... | collective-permute-start | bytes 663560 | tf_op jit(solution)/shard_map/ppermute | solution.py:47
  16.5 9.6 %collective-permute-start.4 = (bf16[72,1536]{1,0:T(8,128)(2,1)S(1)}, bf16[72,1536]{1,0:T(8,128)(2,1)S(1)}, u32[]{:S(2)}, u32[]{:S(2)}) collective-permute-start(bf16[72,1536]{1,0:T(8,128)(2,1)S(1)} %get-tuple-element.65), channel_id=1, source_target_pairs={{0,4},{1,5},{16,20},{17,21},{32,36},{33,37},{48,52},{49,53},{2,6},... | collective-permute-start | bytes 663560 | tf_op jit(solution)/shard_map/ppermute | solution.py:47
  17.1 9.2 %collective-permute-start.5 = (bf16[72,1536]{1,0:T(8,128)(2,1)S(1)}, bf16[72,1536]{1,0:T(8,128)(2,1)S(1)}, u32[]{:S(2)}, u32[]{:S(2)}) collective-permute-start(bf16[72,1536]{1,0:T(8,128)(2,1)S(1)} %get-tuple-element.66), channel_id=1, source_target_pairs={{0,12},{1,13},{16,28},{17,29},{32,44},{33,45},{48,60},{49,61},{2,1... | collective-permute-start | bytes 663560 | tf_op jit(solution)/shard_map/ppermute | solution.py:47
  26.5 12.8 %collective-permute-start.6 = (bf16[72,1536]{1,0:T(8,128)(2,1)S(1)}, bf16[72,1536]{1,0:T(8,128)(2,1)S(1)}, u32[]{:S(2)}, u32[]{:S(2)}) collective-permute-start(bf16[72,1536]{1,0:T(8,128)(2,1)S(1)} %add_convert_fusion), channel_id=1, source_target_pairs={{0,2},{1,3},{16,18},{17,19},{32,34},{33,35},{48,50},{49,51},{2,0},... | collective-permute-start | bytes 663560 | tf_op jit(solution)/shard_map/ppermute | solution.py:47
  33.8 9.5 %collective-permute-start.7 = (bf16[72,1536]{1,0:T(8,128)(2,1)S(1)}, bf16[72,1536]{1,0:T(8,128)(2,1)S(1)}, u32[]{:S(2)}, u32[]{:S(2)}) collective-permute-start(bf16[72,1536]{1,0:T(8,128)(2,1)S(1)} %get-tuple-element.78), channel_id=1, source_target_pairs={{0,8},{1,9},{16,24},{17,25},{32,40},{33,41},{48,56},{49,57},{2,10}... | collective-permute-start | bytes 663560 | tf_op jit(solution)/shard_map/ppermute | solution.py:47
  35.9 10.0 %collective-permute-start.8 = (bf16[72,1536]{1,0:T(8,128)(2,1)S(1)}, bf16[72,1536]{1,0:T(8,128)(2,1)S(1)}, u32[]{:S(2)}, u32[]{:S(2)}) collective-permute-start(bf16[72,1536]{1,0:T(8,128)(2,1)S(1)} %get-tuple-element.79), channel_id=1, source_target_pairs={{0,4},{1,5},{16,20},{17,21},{32,36},{33,37},{48,52},{49,53},{2,6},... | collective-permute-start | bytes 663560 | tf_op jit(solution)/shard_map/ppermute | solution.py:47
  37.3 8.8 %collective-permute-start.9 = (bf16[72,1536]{1,0:T(8,128)(2,1)S(1)}, bf16[72,1536]{1,0:T(8,128)(2,1)S(1)}, u32[]{:S(2)}, u32[]{:S(2)}) collective-permute-start(bf16[72,1536]{1,0:T(8,128)(2,1)S(1)} %get-tuple-element.80), channel_id=1, source_target_pairs={{0,12},{1,13},{16,28},{17,29},{32,44},{33,45},{48,60},{49,61},{2,1... | collective-permute-start | bytes 663560 | tf_op jit(solution)/shard_map/ppermute | solution.py:47
  46.3 12.5 %collective-permute-start.10 = (bf16[72,1536]{1,0:T(8,128)(2,1)S(1)}, bf16[72,1536]{1,0:T(8,128)(2,1)S(1)}, u32[]{:S(2)}, u32[]{:S(2)}) collective-permute-start(bf16[72,1536]{1,0:T(8,128)(2,1)S(1)} %get-tuple-element.121), channel_id=1, source_target_pairs={{0,2},{1,3},{16,18},{17,19},{32,34},{33,35},{48,50},{49,51},{2,0},... | collective-permute-start | bytes 663560 | tf_op jit(solution)/shard_map/ppermute | solution.py:47
  48.3 10.5 %collective-permute-start.11 = (f32[36,1536]{1,0:T(8,128)S(1)}, f32[36,1536]{1,0:T(8,128)S(1)}, u32[]{:S(2)}, u32[]{:S(2)}) collective-permute-start(f32[36,1536]{1,0:T(8,128)S(1)} %slice_select_fusion.1), channel_id=1, source_target_pairs={{0,1},{1,0},{16,17},{17,16},{32,33},{33,32},{48,49},{49,48},{2,3},... | collective-permute-start | bytes 663560 | tf_op jit(solution)/shard_map/ppermute | solution.py:47
  58.9 15.1 %collective-permute-start.15 = (bf16[144,1536]{1,0:T(8,128)(2,1)S(1)}, bf16[144,1536]{1,0:T(8,128)(2,1)S(1)}, u32[]{:S(2)}, u32[]{:S(2)}) collective-permute-start(bf16[144,1536]{1,0:T(8,128)(2,1)S(1)} %bitcast.39), channel_id=1, source_target_pairs={{0,4},{16,20},{32,36},{48,52},{2,6},{18,22},{34,38},{50,54},{4,8},... | collective-permute-start | bytes 1327112 | tf_op jit(solution)/shard_map/ppermute | solution.py:47
  64.9 11.7 %collective-permute-start.17 = (bf16[144,1536]{1,0:T(8,128)(2,1)S(1)}, bf16[144,1536]{1,0:T(8,128)(2,1)S(1)}, u32[]{:S(2)}, u32[]{:S(2)}) collective-permute-start(bf16[144,1536]{1,0:T(8,128)(2,1)S(1)} %bitcast.40), channel_id=1, source_target_pairs={{0,12},{16,28},{32,44},{48,60},{2,14},{18,30},{34,46},{50,62},{4,0... | collective-permute-start | bytes 1327112 | tf_op jit(solution)/shard_map/ppermute | solution.py:47
  64.9 15.1 %collective-permute-start.21 = (bf16[144,1536]{1,0:T(8,128)(2,1)S(1)}, bf16[144,1536]{1,0:T(8,128)(2,1)}, u32[]{:S(2)}, u32[]{:S(2)}) collective-permute-start(bf16[144,1536]{1,0:T(8,128)(2,1)S(1)} %bitcast.41), channel_id=1, source_target_pairs={{0,16},{16,32},{32,48},{48,2},{2,18},{18,34},{34,50},{50,0},{4,20}... | collective-permute-start | bytes 1327112 | tf_op jit(solution)/shard_map/ppermute | solution.py:47
  65.8 23.9 %collective-permute-start.22 = (bf16[144,1536]{1,0:T(8,128)(2,1)S(1)}, bf16[144,1536]{1,0:T(8,128)(2,1)S(1)}, u32[]{:S(2)}, u32[]{:S(2)}) collective-permute-start(bf16[144,1536]{1,0:T(8,128)(2,1)S(1)} %bitcast.42), channel_id=1, source_target_pairs={{0,50},{16,0},{32,16},{48,32},{2,48},{18,2},{34,18},{50,34},{4,54}... | collective-permute-start | bytes 1327112 | tf_op jit(solution)/shard_map/ppermute | solution.py:47
  74.0 9.7 %collective-permute-start.16 = (bf16[72,1536]{1,0:T(8,128)(2,1)S(1)}, bf16[72,1536]{1,0:T(8,128)(2,1)S(1)}, u32[]{:S(2)}, u32[]{:S(2)}) collective-permute-start(bf16[72,1536]{1,0:T(8,128)(2,1)S(1)} %slice.20), channel_id=1, source_target_pairs={{0,4},{16,20},{32,36},{48,52},{2,6},{18,22},{34,38},{50,54},{4,8},... | collective-permute-start | bytes 663560 | tf_op jit(solution)/shard_map/ppermute | solution.py:47
  76.7 26.0 %collective-permute-start.24 = (bf16[2,144,1536]{2,1,0:T(8,128)(2,1)S(1)}, bf16[2,144,1536]{2,1,0:T(8,128)(2,1)S(1)}, u32[]{:S(2)}, u32[]{:S(2)}) collective-permute-start(bf16[2,144,1536]{2,1,0:T(8,128)(2,1)S(1)} %pad_maximum_fusion.refs_1_.refs_5_), channel_id=1, source_target_pairs={{0,16},{16,32},{32,48},{48,2},{2,18},{18,34},{34,50},{50,0},{4,20}... | collective-permute-start | bytes 2654216 | tf_op jit(solution)/shard_map/ppermute | solution.py:47
  78.7 21.9 %collective-permute-start.23 = (bf16[2,144,1536]{2,1,0:T(8,128)(2,1)S(1)}, bf16[2,144,1536]{2,1,0:T(8,128)(2,1)S(1)}, u32[]{:S(2)}, u32[]{:S(2)}) collective-permute-start(bf16[2,144,1536]{2,1,0:T(8,128)(2,1)S(1)} %pad_maximum_fusion.refs_1_.refs_5_), channel_id=1, source_target_pairs={{0,50},{16,0},{32,16},{48,32},{2,48},{18,2},{34,18},{50,34},{4,54}... | collective-permute-start | bytes 2654216 | tf_op jit(solution)/shard_map/ppermute | solution.py:47
  83.6 12.1 %collective-permute-start.26 = (bf16[144,1536]{1,0:T(8,128)(2,1)}, bf16[144,1536]{1,0:T(8,128)(2,1)S(1)}, u32[]{:S(2)}, u32[]{:S(2)}) collective-permute-start(bf16[144,1536]{1,0:T(8,128)(2,1)} %collective-permute-done.21.refs_3_.refs_7_), channel_id=1, source_target_pairs={{0,16},{16,32},{32,48},{48,2},{2,18},{18,34},{34,50},{50,0},{4,20}... | collective-permute-start | bytes 1327112 | tf_op jit(solution)/shard_map/ppermute | solution.py:47
  89.7 10.8 %collective-permute-start.19 = (bf16[144,1536]{1,0:T(8,128)(2,1)}, bf16[144,1536]{1,0:T(8,128)(2,1)}, u32[]{:S(2)}, u32[]{:S(2)}) collective-permute-start(bf16[144,1536]{1,0:T(8,128)(2,1)} %constant_dynamic-update-slice_fusion.refs_2_.refs_6_), channel_id=1, source_target_pairs={{0,16},{16,32},{32,48},{48,2},{2,18},{18,34},{34,50},{50,0},{4,20}... | collective-permute-start | bytes 1327112 | tf_op jit(solution)/shard_map/ppermute | solution.py:47
  100.6 13.2 %collective-permute-start.27 = (bf16[2,144,1536]{2,1,0:T(8,128)(2,1)S(1)}, bf16[2,144,1536]{2,1,0:T(8,128)(2,1)}, u32[]{:S(2)}, u32[]{:S(2)}) collective-permute-start(bf16[2,144,1536]{2,1,0:T(8,128)(2,1)S(1)} %collective-permute-done.23.refs_7_.refs_11_), channel_id=1, source_target_pairs={{0,50},{16,0},{32,16},{48,32},{2,48},{18,2},{34,18},{50,34},{4,54}... | collective-permute-start | bytes 2654216 | tf_op jit(solution)/shard_map/ppermute | solution.py:47
  101.2 9.8 %collective-permute-start.20 = (bf16[144,1536]{1,0:T(8,128)(2,1)}, bf16[144,1536]{1,0:T(8,128)(2,1)}, u32[]{:S(2)}, u32[]{:S(2)}) collective-permute-start(bf16[144,1536]{1,0:T(8,128)(2,1)} %collective-permute-done.19.refs_5_.refs_9_), channel_id=1, source_target_pairs={{0,16},{16,32},{32,48},{48,2},{2,18},{18,34},{34,50},{50,0},{4,20}... | collective-permute-start | bytes 1327112 | tf_op jit(solution)/shard_map/ppermute | solution.py:47
  111.1 10.0 %collective-permute-start.35 = (bf16[2,144,1536]{2,1,0:T(8,128)(2,1)S(1)}, bf16[2,144,1536]{2,1,0:T(8,128)(2,1)}, u32[]{:S(2)}, u32[]{:S(2)}) collective-permute-start(bf16[2,144,1536]{2,1,0:T(8,128)(2,1)S(1)} %collective-permute-done.23.refs_7_.refs_11_), channel_id=1, source_target_pairs={{0,1},{1,0},{16,17},{17,16},{32,33},{33,32},{48,49},{49,48},{2,3},... | collective-permute-start | bytes 2654216 | tf_op jit(solution)/shard_map/ppermute | solution.py:47
  111.6 9.4 %collective-permute-start.29 = (bf16[2,144,1536]{2,1,0:T(8,128)(2,1)S(1)}, bf16[2,144,1536]{2,1,0:T(8,128)(2,1)}, u32[]{:S(2)}, u32[]{:S(2)}) collective-permute-start(bf16[2,144,1536]{2,1,0:T(8,128)(2,1)S(1)} %pad_maximum_fusion.refs_1_.refs_5_), channel_id=1, source_target_pairs={{0,1},{1,0},{16,17},{17,16},{32,33},{33,32},{48,49},{49,48},{2,3},... | collective-permute-start | bytes 2654216 | tf_op jit(solution)/shard_map/ppermute | solution.py:47
  111.7 9.3 %collective-permute-start.32 = (bf16[2,144,1536]{2,1,0:T(8,128)(2,1)S(1)}, bf16[2,144,1536]{2,1,0:T(8,128)(2,1)}, u32[]{:S(2)}, u32[]{:S(2)}) collective-permute-start(bf16[2,144,1536]{2,1,0:T(8,128)(2,1)S(1)} %collective-permute-done.24.refs_4_.refs_8_), channel_id=1, source_target_pairs={{0,1},{1,0},{16,17},{17,16},{32,33},{33,32},{48,49},{49,48},{2,3},... | collective-permute-start | bytes 2654216 | tf_op jit(solution)/shard_map/ppermute | solution.py:47
  125.2 59.2 %collective-permute-start.42 = (bf16[64,576]{1,0:T(8,128)(2,1)S(1)}, bf16[64,576]{1,0:T(8,128)(2,1)S(1)}, u32[]{:S(2)}, u32[]{:S(2)}) collective-permute-start(bf16[64,576]{1,0:T(8,128)(2,1)S(1)} %get-tuple-element.112), channel_id=1, source_target_pairs={{128,192},{129,193},{144,208},{145,209},{160,224},{161,225},{176,2... | collective-permute-start | bytes 221192 | tf_op jit(solution)/shard_map/ppermute | solution.py:47
  (40 other events, 452.2 us)
